TPU v7x, 32 devices: a whole 2x2x4 slice. The times are simulated.
32 devices in a mesh: dp: 8 (over z, x), expert: 4 (over y, core).
Axes of the slice: x: 2, y: 2, z: 4, core: 2. Of those that a mesh axis runs over, the one named last changes fastest.
Arguments:
- layer_input: bfloat16 [8, 2, 1024, 1536], P('dp', None, 'expert'), may hold values from -6 to 6
- cotangent: bfloat16 [8, 2, 1024, 1536], P('dp', None, 'expert'), may hold values from -6 to 6
- lengths: int32 [8, 2], P('dp'), may hold values from 512 to 1024, as said below
- routes: int32 [8, 2, 1024, 8], P('dp', None, 'expert'), may hold values from 0 to 39, all different within a row; in each aligned block of 256 rows (0 to 255, 256 to 511, ..., all dimensions but the last counted through in order) at most 64 rows name the same one
- capacity: int32 [40], replicated, may hold values from 48 to 64, as said below
- w_query: bfloat16 [1536, 1536], P(('dp', 'expert')), may hold values from -0.21875 to 0.21875
- key_weight: bfloat16 [1536, 512], P(('dp', 'expert')), may hold values from -0.21875 to 0.21875
- value_weight: bfloat16 [1536, 512], P(('dp', 'expert')), may hold values from -0.15625 to 0.15625
- w_output: bfloat16 [1536, 1536], P(('dp', 'expert')), may hold values from -0.625 to 0.625
- w_router: bfloat16 [1536, 40], P(('dp', 'expert')), may hold values from -0.078125 to 0.078125
- gain_attn: bfloat16 [1536], P(('dp', 'expert')), may hold values from 0.5 to 1.5
- gain_moe: bfloat16 [1536], P(('dp', 'expert')), may hold values from 0.5 to 1.5
- w_gate: bfloat16 [40, 1536, 512], P('expert', 'dp'), may hold values from -0.15625 to 0.15625
- w_up: bfloat16 [40, 1536, 512], P('expert', 'dp'), may hold values from -0.15625 to 0.15625
- w_down: bfloat16 [40, 512, 1536], P('expert', 'dp'), may hold values from -1 to 1
Outputs:
- layer_output: bfloat16 [8, 2, 1024, 1536], P('dp', None, 'expert')
- input_grad: float32 [8, 2, 1024, 1536], P('dp', None, 'expert')
- grad_query: float32 [1536, 1536], P(('dp', 'expert'))
- grad_key: float32 [1536, 512], P(('dp', 'expert'))
- grad_value: float32 [1536, 512], P(('dp', 'expert'))
- grad_output: float32 [1536, 1536], P(('dp', 'expert'))
- grad_router: float32 [1536, 40], P(('dp', 'expert'))
- grad_gain_attn: float32 [1536], P(('dp', 'expert'))
- grad_gain_moe: float32 [1536], P(('dp', 'expert'))
- grad_gate: float32 [40, 1536, 512], P('expert', 'dp')
- grad_up: float32 [40, 1536, 512], P('expert', 'dp')
- grad_down: float32 [40, 512, 1536], P('expert', 'dp')
Inputs may be any that keep to these rules, and one draw needn't show every extreme that they name: `lengths`: in every draw some sequence has all 1024 positions valid. `capacity`: some expert accepts exactly 64 slots. `routes`: each position names 8 different experts. In each aligned block of 256 positions (the positions of one device in one micro-batch) no expert is named more than 64 times, a bound that some block reaches.
All inputs are finite; a program needn't handle non-finite values.
Results may differ from a plain program's by a relative error of at most 0.019.
Values may be sent and summed in bfloat16 or wider, within the bound.
No kernel may reach another device: no remote copies, remote signals or barrier semaphores. Data moves between devices by JAX's collectives and lax.ppermute only.
A program may use at most 216 MiB of HBM per device.

v0:
```python
import jax
import jax.numpy as jnp
from jax import lax
from jax.sharding import PartitionSpec as P

QUERY_HEAD_COUNT = 24
KEY_VALUE_HEADS = 8
HEAD_DIMENSION = 64
EXPERTS = 40
TOPK = 8


epsilon = 1e-06
rope_base = 10000.0
masked_score = -1e30


def as_sent(array):

    def short(part):
        return part.astype(jnp.bfloat16) if part.dtype == jnp.float32 else part

    return jax.tree.map(short, array)


def matrix_product(left, right):
    return jnp.dot(left, right, preferred_element_type=jnp.float32)


def contract_rows(left, right):
    return lax.dot_general(
        left, right, (((0,), (0,)), ((), ())), preferred_element_type=jnp.float32
    )


def contract_cols(left, right):
    return lax.dot_general(
        left, right, (((1,), (1,)), ((), ())), preferred_element_type=jnp.float32
    )


def rope_tables(start_row, tally_count, head_size):
    places = (start_row + jnp.arange(tally_count, dtype=jnp.int32)).astype(jnp.float32)
    freqs = rope_base ** (-jnp.arange(0, head_size, 2, dtype=jnp.float32) / head_size)
    angles = places[:, None] * freqs[None, :]
    angles = jnp.concatenate([angles, angles], axis=1)
    return (jnp.cos(angles)[:, None, :], jnp.sin(angles)[:, None, :])


def rotate(value_matrix, cos_table, sin_table):
    half_size = value_matrix.shape[-1] // 2
    turned = jnp.concatenate(
        [-value_matrix[..., half_size:], value_matrix[..., :half_size]], axis=-1
    )
    return value_matrix * cos_table + turned * sin_table


def rotate_back(grads, cos_table, sin_table):
    half_size = grads.shape[-1] // 2
    scaled = grads * sin_table
    turned = jnp.concatenate([scaled[..., half_size:], -scaled[..., :half_size]], axis=-1)
    return grads * cos_table + turned


def attend_forward(split_query_heads, key_heads, value_heads, allowed, score_scale):

    def one_head(pieces):
        query_one, key_one, value_one = pieces
        scores = contract_cols(query_one, key_one) * score_scale
        scores = jnp.where(allowed, scores, masked_score)
        peak = jnp.max(scores, axis=1, keepdims=True)
        raised = jnp.exp(scores - peak)
        total = jnp.sum(raised, axis=1, keepdims=True)
        probs = (raised / total).astype(jnp.bfloat16)
        return (matrix_product(probs, value_one), (peak + jnp.log(total))[:, 0])

    return lax.map(one_head, (split_query_heads, key_heads, value_heads))


def attend_backward(
    split_query_heads, key_heads, value_heads, grad_heads, log_totals, allowed, score_scale
):

    def one_head(pieces):
        query_one, key_one, value_one, grad_one, log_total = pieces
        scores = contract_cols(query_one, key_one) * score_scale
        probs = jnp.where(allowed, jnp.exp(scores - log_total[:, None]), 0.0)
        grad_probs = contract_cols(grad_one, value_one)
        value_gradient = contract_rows(probs.astype(jnp.bfloat16), grad_one)
        grad_scores = probs * (grad_probs - jnp.sum(probs * grad_probs, axis=1, keepdims=True))
        grad_scores = grad_scores.astype(jnp.bfloat16)
        query_gradient = matrix_product(grad_scores, key_one) * score_scale
        grad_keys = contract_rows(grad_scores, query_one) * score_scale
        return (query_gradient, grad_keys, value_gradient)

    return lax.map(one_head, (split_query_heads, key_heads, value_heads, grad_heads, log_totals))


def shards(
    layer_input,
    cotangent,
    lengths,
    routes,
    capacity,
    w_query,
    key_weight,
    value_weight,
    w_output,
    w_router,
    gain_attn,
    gain_moe,
    w_gate,
    w_up,
    w_down,
):
    micro_count = layer_input.shape[1]
    total_row_count = layer_input.shape[2]
    model_width = layer_input.shape[3]
    owner_count = lax.axis_size("expert")
    owner_index = lax.axis_index("expert")
    slot_count = total_row_count // 4
    key_count = total_row_count * owner_count
    query_group_count = QUERY_HEAD_COUNT // KEY_VALUE_HEADS
    score_scale = HEAD_DIMENSION ** (-0.5)
    dump_slot = EXPERTS * slot_count
    start_row = owner_index * total_row_count
    cos_table, sin_table = rope_tables(start_row, total_row_count, HEAD_DIMENSION)
    query_places = start_row + jnp.arange(total_row_count, dtype=jnp.int32)
    key_places = jnp.arange(key_count, dtype=jnp.int32)
    query_tiled = jnp.tile(query_places, query_group_count)
    expert_ids = jnp.arange(EXPERTS, dtype=jnp.int32)
    dense_total = None
    expert_total = None
    output_list = []
    grad_list = []
    for index in range(micro_count):
        full_query = lax.all_gather(w_query, ("dp", "expert"), axis=0, tiled=True)
        complete_key = lax.all_gather(key_weight, ("dp", "expert"), axis=0, tiled=True)
        complete_value = lax.all_gather(value_weight, ("dp", "expert"), axis=0, tiled=True)
        full_output = lax.all_gather(w_output, ("dp", "expert"), axis=0, tiled=True)
        full_router = lax.all_gather(w_router, ("dp", "expert"), axis=0, tiled=True)
        full_gain_attn = lax.all_gather(gain_attn, ("dp", "expert"), axis=0, tiled=True)
        full_gain_moe = lax.all_gather(gain_moe, ("dp", "expert"), axis=0, tiled=True)
        full_gate = lax.all_gather(w_gate, "dp", axis=1, tiled=True)
        full_up = lax.all_gather(w_up, "dp", axis=1, tiled=True)
        full_down = lax.all_gather(w_down, "dp", axis=1, tiled=True)
        inputs = layer_input[0, index].astype(jnp.float32)
        length = lengths[0, index]
        picks = routes[0, index]
        valid = query_places < length
        scale_one = lax.rsqrt(jnp.mean(inputs * inputs, axis=1, keepdims=True) + epsilon)
        first_normalized = (inputs * scale_one * full_gain_attn).astype(jnp.bfloat16)
        query_raw = matrix_product(first_normalized, full_query).reshape(
            total_row_count, QUERY_HEAD_COUNT, HEAD_DIMENSION
        )
        unrotated_key = matrix_product(first_normalized, complete_key).reshape(
            total_row_count, KEY_VALUE_HEADS, HEAD_DIMENSION
        )
        value_rows = (
            matrix_product(first_normalized, complete_value)
            .astype(jnp.bfloat16)
            .reshape(total_row_count, KEY_VALUE_HEADS, HEAD_DIMENSION)
        )
        rotated_query = rotate(query_raw, cos_table, sin_table).astype(jnp.bfloat16)
        key_rot = rotate(unrotated_key, cos_table, sin_table).astype(jnp.bfloat16)
        key_local = key_rot.transpose(1, 0, 2)
        value_local = value_rows.transpose(1, 0, 2)
        key_heads = lax.all_gather(key_local, "expert", axis=1, tiled=True)
        value_heads = lax.all_gather(value_local, "expert", axis=1, tiled=True)
        split_query_heads = (
            rotated_query.reshape(
                total_row_count, KEY_VALUE_HEADS, query_group_count, HEAD_DIMENSION
            )
            .transpose(1, 2, 0, 3)
            .reshape(KEY_VALUE_HEADS, query_group_count * total_row_count, HEAD_DIMENSION)
        )
        allowed = (key_places[None, :] <= query_tiled[:, None]) & (key_places[None, :] < length)
        blended_output, log_totals = attend_forward(
            split_query_heads, key_heads, value_heads, allowed, score_scale
        )
        attended = (
            blended_output.reshape(
                KEY_VALUE_HEADS, query_group_count, total_row_count, HEAD_DIMENSION
            )
            .transpose(2, 0, 1, 3)
            .reshape(total_row_count, QUERY_HEAD_COUNT * HEAD_DIMENSION)
            .astype(jnp.bfloat16)
        )
        middle = inputs + matrix_product(attended, full_output)
        scale_two = lax.rsqrt(jnp.mean(middle * middle, axis=1, keepdims=True) + epsilon)
        normed_two = (middle * scale_two * full_gain_moe).astype(jnp.bfloat16)
        logits = matrix_product(normed_two, full_router)
        chosen = jnp.take_along_axis(logits, picks, axis=1)
        gate_weights = jax.nn.softmax(chosen, axis=1)
        flat_picks = picks.reshape(total_row_count * TOPK)
        pair_valid = jnp.repeat(valid, TOPK)
        matches = flat_picks[:, None] == expert_ids[None, :]
        onehot = (matches & pair_valid[:, None]).astype(jnp.int32)
        running = jnp.cumsum(onehot, axis=0)
        slot_ranks = jnp.sum(running * onehot, axis=1) - 1
        limits = jnp.sum(matches.astype(jnp.int32) * capacity[None, :], axis=1)
        kept = pair_valid & (slot_ranks < limits)
        slots = jnp.where(kept, flat_picks * slot_count + slot_ranks, dump_slot)
        pair_rows = jnp.repeat(normed_two, TOPK, axis=0)
        send_rows = (
            jnp.zeros((dump_slot + 1, model_width), jnp.bfloat16)
            .at[slots]
            .set(pair_rows)[:dump_slot]
        )
        send_rows = send_rows.reshape(owner_count, EXPERTS // owner_count, slot_count, model_width)
        received = lax.all_to_all(send_rows, "expert", split_axis=0, concat_axis=0, tiled=True)
        gate_pre = jnp.einsum(
            "secd,edf->secf", received, full_gate, preferred_element_type=jnp.float32
        )
        up_pre = jnp.einsum("secd,edf->secf", received, full_up, preferred_element_type=jnp.float32)
        hidden = (jax.nn.silu(gate_pre) * up_pre).astype(jnp.bfloat16)
        expert_out = jnp.einsum(
            "secf,efd->secd", hidden, full_down, preferred_element_type=jnp.float32
        ).astype(jnp.bfloat16)
        returned = lax.all_to_all(expert_out, "expert", split_axis=0, concat_axis=0, tiled=True)
        out_table = jnp.concatenate(
            [returned.reshape(dump_slot, model_width), jnp.zeros((1, model_width), jnp.bfloat16)],
            axis=0,
        )
        picked = out_table[slots].reshape(total_row_count, TOPK, model_width)
        mixture = jnp.einsum("tk,tkd->td", gate_weights, picked.astype(jnp.float32))
        output_rows = (middle + mixture).astype(jnp.bfloat16)
        grad_out = cotangent[0, index].astype(jnp.float32) * valid[:, None].astype(jnp.float32)
        gate_grads = jnp.einsum("td,tkd->tk", grad_out, picked.astype(jnp.float32))
        grad_pairs = (
            (gate_weights[:, :, None] * grad_out[:, None, :])
            .astype(jnp.bfloat16)
            .reshape(total_row_count * TOPK, model_width)
        )
        grad_send = (
            jnp.zeros((dump_slot + 1, model_width), jnp.bfloat16)
            .at[slots]
            .set(grad_pairs)[:dump_slot]
        )
        grad_send = grad_send.reshape(owner_count, EXPERTS // owner_count, slot_count, model_width)
        grad_received = lax.all_to_all(grad_send, "expert", split_axis=0, concat_axis=0, tiled=True)
        grad_hidden = jnp.einsum(
            "secd,efd->secf", grad_received, full_down, preferred_element_type=jnp.float32
        )
        grad_down = jnp.einsum(
            "secf,secd->efd", hidden, grad_received, preferred_element_type=jnp.float32
        )
        sigmoid_gate = jax.nn.sigmoid(gate_pre)
        silu_gate = gate_pre * sigmoid_gate
        grad_gate_pre = (
            grad_hidden * up_pre * sigmoid_gate * (1.0 + gate_pre * (1.0 - sigmoid_gate))
        ).astype(jnp.bfloat16)
        grad_up_pre = (grad_hidden * silu_gate).astype(jnp.bfloat16)
        grad_gate = jnp.einsum(
            "secd,secf->edf", received, grad_gate_pre, preferred_element_type=jnp.float32
        )
        grad_up = jnp.einsum(
            "secd,secf->edf", received, grad_up_pre, preferred_element_type=jnp.float32
        )
        grad_rows = jnp.einsum(
            "secf,edf->secd", grad_gate_pre, full_gate, preferred_element_type=jnp.float32
        )
        grad_rows = (
            grad_rows
            + jnp.einsum("secf,edf->secd", grad_up_pre, full_up, preferred_element_type=jnp.float32)
        ).astype(jnp.bfloat16)
        grad_back = lax.all_to_all(grad_rows, "expert", split_axis=0, concat_axis=0, tiled=True)
        grad_table = jnp.concatenate(
            [grad_back.reshape(dump_slot, model_width), jnp.zeros((1, model_width), jnp.bfloat16)],
            axis=0,
        )
        grad_normed_two = jnp.sum(
            grad_table[slots].reshape(total_row_count, TOPK, model_width).astype(jnp.float32),
            axis=1,
        )
        grad_chosen = gate_weights * (
            gate_grads - jnp.sum(gate_weights * gate_grads, axis=1, keepdims=True)
        )
        route_hits = (picks[:, :, None] == expert_ids[None, None, :]).astype(jnp.float32)
        grad_logits = jnp.sum(grad_chosen[:, :, None] * route_hits, axis=1).astype(jnp.bfloat16)
        grad_normed_two = grad_normed_two + contract_cols(grad_logits, full_router)
        grad_router = contract_rows(normed_two, grad_logits)
        grad_scaled_two = grad_normed_two * full_gain_moe
        grad_gain_moe = jnp.sum(grad_normed_two * middle * scale_two, axis=0)
        grad_middle = (
            grad_out
            + scale_two * grad_scaled_two
            - middle * scale_two**3 * jnp.mean(grad_scaled_two * middle, axis=1, keepdims=True)
        )
        grad_branch = grad_middle.astype(jnp.bfloat16)
        grad_output = contract_rows(attended, grad_branch)
        attended_gradient = contract_cols(grad_branch, full_output).astype(jnp.bfloat16)
        grad_heads = (
            attended_gradient.reshape(
                total_row_count, KEY_VALUE_HEADS, query_group_count, HEAD_DIMENSION
            )
            .transpose(1, 2, 0, 3)
            .reshape(KEY_VALUE_HEADS, query_group_count * total_row_count, HEAD_DIMENSION)
        )
        query_head_gradient, key_partial, value_partial = attend_backward(
            split_query_heads, key_heads, value_heads, grad_heads, log_totals, allowed, score_scale
        )
        grad_keys = lax.psum_scatter(
            key_partial.astype(jnp.bfloat16), "expert", scatter_dimension=1, tiled=True
        ).astype(jnp.float32)
        value_gradient = lax.psum_scatter(
            value_partial.astype(jnp.bfloat16), "expert", scatter_dimension=1, tiled=True
        ).astype(jnp.float32)
        query_gradient = query_head_gradient.reshape(
            KEY_VALUE_HEADS, query_group_count, total_row_count, HEAD_DIMENSION
        ).transpose(2, 0, 1, 3)
        query_gradient = rotate_back(
            query_gradient.reshape(total_row_count, QUERY_HEAD_COUNT, HEAD_DIMENSION),
            cos_table,
            sin_table,
        )
        grad_query_rows = query_gradient.reshape(
            total_row_count, QUERY_HEAD_COUNT * HEAD_DIMENSION
        ).astype(jnp.bfloat16)
        grad_key_rows = (
            rotate_back(grad_keys.transpose(1, 0, 2), cos_table, sin_table)
            .reshape(total_row_count, KEY_VALUE_HEADS * HEAD_DIMENSION)
            .astype(jnp.bfloat16)
        )
        grad_value_rows = (
            value_gradient.transpose(1, 0, 2)
            .reshape(total_row_count, KEY_VALUE_HEADS * HEAD_DIMENSION)
            .astype(jnp.bfloat16)
        )
        grad_normed_one = (
            contract_cols(grad_query_rows, full_query)
            + contract_cols(grad_key_rows, complete_key)
            + contract_cols(grad_value_rows, complete_value)
        )
        grad_query = contract_rows(first_normalized, grad_query_rows)
        grad_key = contract_rows(first_normalized, grad_key_rows)
        grad_value = contract_rows(first_normalized, grad_value_rows)
        grad_scaled_one = grad_normed_one * full_gain_attn
        grad_gain_attn = jnp.sum(grad_normed_one * inputs * scale_one, axis=0)
        grad_inputs = (
            grad_middle
            + scale_one * grad_scaled_one
            - inputs * scale_one**3 * jnp.mean(grad_scaled_one * inputs, axis=1, keepdims=True)
        )
        dense_grads = (
            grad_query,
            grad_key,
            grad_value,
            grad_output,
            grad_router,
            grad_gain_attn,
            grad_gain_moe,
        )
        output_rows, grad_inputs, dense_grads, expert_grads = (
            output_rows,
            grad_inputs,
            dense_grads,
            (grad_gate, grad_up, grad_down),
        )
        if dense_total is None:
            dense_total = dense_grads
            expert_total = expert_grads
        else:
            dense_total = tuple((total + piece for total, piece in zip(dense_total, dense_grads)))
            expert_total = tuple(
                (total + piece for total, piece in zip(expert_total, expert_grads))
            )
        output_list.append(output_rows)
        grad_list.append(grad_inputs)
    dense_total = lax.psum_scatter(dense_total, ("dp", "expert"), scatter_dimension=0, tiled=True)
    expert_total = jax.tree.map(
        lambda part: part.astype(jnp.float32),
        lax.psum_scatter(as_sent(expert_total), "dp", scatter_dimension=1, tiled=True),
    )
    layer_output = jnp.stack(output_list, axis=0)[None]
    input_grad = jnp.stack(grad_list, axis=0)[None]
    return (
        layer_output,
        input_grad,
        dense_total[0],
        dense_total[1],
        dense_total[2],
        dense_total[3],
        dense_total[4],
        dense_total[5],
        dense_total[6],
        expert_total[0],
        expert_total[1],
        expert_total[2],
    )


def solution(mesh):
    return jax.shard_map(
        shards,
        mesh=mesh,
        in_specs=(
            P("dp", None, "expert", None),
            P("dp", None, "expert", None),
            P("dp", None),
            P("dp", None, "expert", None),
            P(),
            P(("dp", "expert"), None),
            P(("dp", "expert"), None),
            P(("dp", "expert"), None),
            P(("dp", "expert"), None),
            P(("dp", "expert"), None),
            P(("dp", "expert")),
            P(("dp", "expert")),
            P("expert", "dp", None),
            P("expert", "dp", None),
            P("expert", "dp", None),
        ),
        out_specs=(
            P("dp", None, "expert", None),
            P("dp", None, "expert", None),
            P(("dp", "expert"), None),
            P(("dp", "expert"), None),
            P(("dp", "expert"), None),
            P(("dp", "expert"), None),
            P(("dp", "expert"), None),
            P(("dp", "expert")),
            P(("dp", "expert")),
            P("expert", "dp", None),
            P("expert", "dp", None),
            P("expert", "dp", None),
        ),
        check_vma=False,
    )
```

profile of v0, /device:TPU:0, one launch (start us, length us, event | category | flops | bytes accessed | tf_op | source)
XLA Modules:
  0.0 3631.4 jit_solution(8102096790168585625)
XLA Ops:
  10.4 42.1 %all-reduce.9 = (bf16[1536]{0:T(1024)(128)(2,1)S(1)}, bf16[1536]{0:T(1024)(128)(2,1)S(1)}) all-reduce(bf16[1536]{0:T(1024)(128)(2,1)S(1)} %dynamic-update-slice, bf16[1536]{0:T(1024)(128)(2,1)S(1)} %dynamic-update-slice.1), channel_id=1, replica_groups=mesh['dp'=8,'expert'=4] {'dp','expert'}, use_global_device_ids=true, to_apply=%add.4 | all-reduce | flops 3072 | bytes 12288
  72.1 53.4 %all-gather.15.cloned.1.call-done = bf16[1536,512]{1,0:T(8,128)(2,1)} async-done(((bf16[48,512]{1,0:T(8,128)(2,1)}), bf16[1536,512]{1,0:T(8,128)(2,1)}) %all-gather.15.cloned.1.call-update) | async-done | bytes 1572880 | tf_op jit(solution)/shard_map/all_gather | solution.py:138
  174.2 54.6 %all-gather.13.cloned.1.call-done = bf16[1536,1536]{1,0:T(8,128)(2,1)} async-done(((bf16[48,1536]{1,0:T(8,128)(2,1)}), bf16[1536,1536]{1,0:T(8,128)(2,1)}) %all-gather.13.cloned.1.call-update) | async-done | bytes 4718608 | tf_op jit(solution)/shard_map/all_gather | solution.py:137
  245.8 40.1 %while.56 = (s32[]{:T(128)}, bf16[8,768,64]{1,2,0:T(8,128)(2,1)S(1)}, f32[8,768]{1,0:T(8,128)S(1)}, bf16[8,768,64]{2,1,0:T(8,128)(2,1)}, bf16[8,1024,64]{2,1,0:T...) while((s32[]{:T(128)}, ...), condition=%wide.region_4.5_spmd.clone, body=%wide.region_1.4_spmd.clone.sunk | while | flops 209190144 | bytes 10399857 | solution.py:77
  299.2 15.1 scatter_custom_fusion
  321.1 94.9 %all_to_all.40 = bf16[4,10,64,1536]{3,2,1,0:T(8,128)(2,1)} all-to-all(bf16[4,10,64,1536]{3,2,1,0:T(8,128)(2,1)} %bitcast.775), channel_id=1, replica_groups=mesh['dp'=8,'expert'=4] {'expert'}, dimensions={0} | all-to-all | bytes 15728640 | tf_op jit(solution)/shard_map/all_to_all | solution.py:211
  415.9 93.8 %all-gather.25.cloned.1.call-done = bf16[10,1536,512]{2,1,0:T(8,128)(2,1)} async-done(((bf16[10,192,512]{2,1,0:T(8,128)(2,1)}), bf16[10,1536,512]{2,1,0:T(8,128)(2,1)}) %all-gather.25.cloned.1.call-update) | async-done | bytes 15728656 | tf_op jit(solution)/shard_map/all_gather | solution.py:144
  524.2 200.8 %all-gather.27.cloned.1.call-done = bf16[10,1536,512]{2,1,0:T(8,128)(2,1)} async-done(((bf16[10,192,512]{2,1,0:T(8,128)(2,1)}), bf16[10,1536,512]{2,1,0:T(8,128)(2,1)}) %all-gather.27.cloned.1.call-update) | async-done | bytes 15728656 | tf_op jit(solution)/shard_map/all_gather | solution.py:145
  725.0 17.8 fusion.181
  742.8 197.4 %all-gather.29.cloned.1.call-done = bf16[10,512,1536]{2,1,0:T(8,128)(2,1)} async-done(((bf16[10,64,1536]{2,1,0:T(8,128)(2,1)}), bf16[10,512,1536]{2,1,0:T(8,128)(2,1)}) %all-gather.29.cloned.1.call-update) | async-done | bytes 15728656 | tf_op jit(solution)/shard_map/all_gather | solution.py:146
  967.0 118.1 %all-gather = bf16[32,48,40]{1,2,0:T(8,128)(2,1)S(1)} all-gather(bf16[1,48,40]{1,2,0:T(8,128)(2,1)S(1)} %bitcast.834), channel_id=1, replica_groups=mesh['dp'=8,'expert'=4] {'dp','expert'}, dimensions={0}, use_global_device_ids=true | all-gather | bytes 126720 | tf_op jit(solution)/shard_map/all_gather | solution.py:141
  1091.0 17.0 gather_fusion.4
  1115.2 17.5 gather_fusion
  1140.0 15.6 scatter_custom_fusion.2
  1173.1 18.7 all-gather.33.cloned.1.call-done
  1194.6 22.0 all-gather.31.cloned.1.call-done
  1220.9 46.0 %all-to-all-done.4 = bf16[4,10,64,1536]{3,2,1,0:T(8,128)(2,1)} async-done(((bf16[4,10,64,1536]{3,2,1,0:T(8,128)(2,1)}), bf16[4,10,64,1536]{3,2,1,0:T(8,128)(2,1)}, u32[]{:S(2)}, u32[]{:S(2)}) %all-to-all-start.4) | async-done | bytes 7864352 | tf_op jit(solution)/shard_map/all_to_all | solution.py:241
  1266.9 15.8 fusion.174
  1294.6 15.8 fusion.129
  1323.7 40.0 %while.57 = (s32[]{:T(128)}, bf16[8,768,64]{1,2,0:T(8,128)(2,1)S(1)}, f32[8,768]{1,0:T(8,128)S(1)}, bf16[8,768,64]{2,1,0:T(8,128)(2,1)}, bf16[8,1024,64]{2,1,0:T...) while((s32[]{:T(128)}, ...), condition=%wide.region_17.19_spmd.clone, body=%wide.region_14.18_spmd.clone.sunk | while | flops 209190144 | bytes 10399857 | solution.py:77
  1369.4 41.8 %all-to-all-done.5 = bf16[4,10,64,1536]{3,2,1,0:T(8,128)(2,1)} async-done(((bf16[4,10,64,1536]{3,2,1,0:T(8,128)(2,1)}), bf16[4,10,64,1536]{3,2,1,0:T(8,128)(2,1)}, u32[]{:S(2)}, u32[]{:S(2)}) %all-to-all-start.5) | async-done | bytes 7864352 | tf_op jit(solution)/shard_map/all_to_all | solution.py:267
  1418.1 17.7 gather_fusion.2
  1464.2 91.5 %all_to_all.41 = bf16[4,10,64,1536]{3,2,1,0:T(8,128)(2,1)} all-to-all(bf16[4,10,64,1536]{3,2,1,0:T(8,128)(2,1)S(1)} %bitcast.773), channel_id=1, replica_groups=mesh['dp'=8,'expert'=4] {'expert'}, dimensions={0} | all-to-all | bytes 15728640 | tf_op jit(solution)/shard_map/all_to_all | solution.py:211
  1569.8 16.7 fusion.176
  1607.7 16.8 gather_fusion.5
  1624.9 69.8 %all-to-all-done.3 = bf16[4,10,64,1536]{3,2,1,0:T(8,128)(2,1)} async-done(((bf16[4,10,64,1536]{3,2,1,0:T(8,128)(2,1)}), bf16[4,10,64,1536]{3,2,1,0:T(8,128)(2,1)}, u32[]{:S(2)}, u32[]{:S(2)}) %all-to-all-start.3) | async-done | bytes 7864352 | tf_op jit(solution)/shard_map/all_to_all | solution.py:220
  1701.5 17.6 gather_fusion.1
  1725.7 15.5 scatter_custom_fusion.3
  1744.5 91.2 %all_to_all.42 = bf16[4,10,64,1536]{3,2,1,0:T(8,128)(2,1)} all-to-all(bf16[4,10,64,1536]{3,2,1,0:T(8,128)(2,1)S(1)} %bitcast.772), channel_id=1, replica_groups=mesh['dp'=8,'expert'=4] {'expert'}, dimensions={0} | all-to-all | bytes 15728640 | tf_op jit(solution)/shard_map/all_to_all | solution.py:241
  1835.7 14.9 fusion.170
  1895.4 77.0 %all-to-all-done.7 = bf16[4,10,64,1536]{3,2,1,0:T(8,128)(2,1)} async-done(((bf16[4,10,64,1536]{3,2,1,0:T(8,128)(2,1)}), bf16[4,10,64,1536]{3,2,1,0:T(8,128)(2,1)}, u32[]{:S(2)}, u32[]{:S(2)}) %all-to-all-start.7) | async-done | bytes 7864352 | tf_op jit(solution)/shard_map/all_to_all | solution.py:267
  1979.3 17.8 gather_fusion.3
  2019.2 82.6 %while.58 = (s32[]{:T(128)}, f32[8,768,64]{1,2,0:T(8,128)S(1)}, bf16[8,1024,64]{1,2,0:T(8,128)(2,1)}, bf16[8,1024,64]{1,2,0:T(8,128)(2,1)}, bf16[8,768,64]{2,1,0...) while((s32[]{:T(128)}, f32[8,768,64]{1,2,0:T(8,128)S(1)}, ...), condition=%wide.region_33.35_spmd.clone, body=%wide.region_31.34_spmd.clone.sunk | while | flops 512081152 | bytes 25911424 | solution.py:96
  2106.3 82.0 %while.59 = (s32[]{:T(128)}, f32[8,768,64]{1,2,0:T(8,128)S(1)}, bf16[8,1024,64]{1,2,0:T(8,128)(2,1)}, bf16[8,1024,64]{1,2,0:T(8,128)(2,1)}, bf16[8,768,64]{2,1,0...) while((s32[]{:T(128)}, f32[8,768,64]{1,2,0:T(8,128)S(1)}, ...), condition=%wide.region_44.46_spmd.clone, body=%wide.region_42.45_spmd.clone.sunk | while | flops 512081152 | bytes 25911424 | solution.py:96
  2190.3 19.4 fusion.137
  2211.2 21.5 fusion.100
  2234.5 15.0 fusion.196
  2249.5 21.0 fusion.102
  2272.3 14.7 fusion.193
  2287.0 21.2 fusion.101
  2379.5 46.3 %all-reduce.8 = (f32[1536]{0:T(1024)S(1)}, f32[1536]{0:T(1024)S(1)}) all-reduce(f32[1536]{0:T(1024)S(1)} %add.408, f32[1536]{0:T(1024)S(1)} %add.409), channel_id=11, replica_groups=mesh['dp'=8,'expert'=4] {'dp','expert'}, use_global_device_ids=true, to_apply=%region_55.57.clone | all-reduce | flops 3072 | bytes 24576
  2432.4 188.3 %reduce-scatter.35.cloned.1.call-done = bf16[10,64,1536]{2,1,0:T(8,128)(2,1)} async-done(((bf16[10,512,1536]{2,1,0:T(8,128)(2,1)}), bf16[10,64,1536]{2,1,0:T(8,128)(2,1)}) %reduce-scatter.35.cloned.1.call-update) | async-done | bytes 1966096 | tf_op jit(solution)/shard_map/reduce_scatter | solution.py:373
  2624.7 249.7 %reduce-scatter.31.cloned.1.call-done = bf16[10,192,512]{2,1,0:T(8,128)(2,1)} async-done(((bf16[10,1536,512]{2,1,0:T(8,128)(2,1)}), bf16[10,192,512]{2,1,0:T(8,128)(2,1)}) %reduce-scatter.31.cloned.1.call-update) | async-done | bytes 1966096 | tf_op jit(solution)/shard_map/reduce_scatter | solution.py:373
  2878.4 249.9 %reduce-scatter.33.cloned.1.call-done = bf16[10,192,512]{2,1,0:T(8,128)(2,1)} async-done(((bf16[10,1536,512]{2,1,0:T(8,128)(2,1)}), bf16[10,192,512]{2,1,0:T(8,128)(2,1)}) %reduce-scatter.33.cloned.1.call-update) | async-done | bytes 1966096 | tf_op jit(solution)/shard_map/reduce_scatter | solution.py:373
  3132.3 102.5 %reduce-scatter.27.cloned.1.call-done = f32[48,512]{1,0:T(8,128)} async-done(((f32[1536,512]{1,0:T(8,128)}), f32[48,512]{1,0:T(8,128)}) %reduce-scatter.27.cloned.1.call-update) | async-done | bytes 98320 | tf_op jit(solution)/shard_map/reduce_scatter | solution.py:370
  3234.8 106.5 %reduce-scatter.25.cloned.1.call-done = f32[48,512]{1,0:T(8,128)} async-done(((f32[1536,512]{1,0:T(8,128)}), f32[48,512]{1,0:T(8,128)}) %reduce-scatter.25.cloned.1.call-update) | async-done | bytes 98320 | tf_op jit(solution)/shard_map/reduce_scatter | solution.py:370
  3341.3 140.9 %reduce-scatter.29.cloned.1.call-done = f32[48,1536]{1,0:T(8,128)} async-done(((f32[1536,1536]{1,0:T(8,128)}), f32[48,1536]{1,0:T(8,128)}) %reduce-scatter.29.cloned.1.call-update) | async-done | bytes 294928 | tf_op jit(solution)/shard_map/reduce_scatter | solution.py:370
  3482.3 142.1 %reduce-scatter.23.cloned.1.call-done = f32[48,1536]{1,0:T(8,128)} async-done(((f32[1536,1536]{1,0:T(8,128)}), f32[48,1536]{1,0:T(8,128)}) %reduce-scatter.23.cloned.1.call-update) | async-done | bytes 294928 | tf_op jit(solution)/shard_map/reduce_scatter | solution.py:370
  (722 shorter events, 729.6 us)
Async XLA Ops:
  7.2 61.5 %all-gather.19.cloned.1.call-start = ((), (), s32[]{:S(2)}) async-start(), calls=%async_computation.23 | async-start | bytes 1622016 | tf_op jit(solution)/shard_map/all_gather | solution.py:139
  7.9 117.6 %all-gather.15.cloned.1.call-start = ((), (), s32[]{:S(2)}) async-start(), calls=%async_computation.21 | async-start | bytes 1622016 | tf_op jit(solution)/shard_map/all_gather | solution.py:138
  8.7 160.0 %all-gather.21.cloned.1.call-start = ((), (), s32[]{:S(2)}) async-start(), calls=%async_computation.24 | async-start | bytes 1310720 | tf_op jit(solution)/shard_map/all_gather | solution.py:169
  52.5 187.1 %copy-start.67 = (f32[1536]{0:T(1024)}, f32[1536]{0:T(1024)S(1)}, u32[]{:S(2)}) copy-start(f32[1536]{0:T(1024)S(1)} %convert_element_type.376) | copy-start | bytes 18436
  54.9 180.5 %copy-start.82 = (f32[256]{0:T(256)}, f32[256]{0:T(256)S(1)}, u32[]{:S(2)}) copy-start(f32[256]{0:T(256)S(1)} %get-tuple-element.681) | copy-start | bytes 3076
  54.9 184.7 %copy-start.90 = (f32[256]{0:T(256)}, f32[256]{0:T(256)S(1)}, u32[]{:S(2)}) copy-start(f32[256]{0:T(256)S(1)} %get-tuple-element.663) | copy-start | bytes 3076
  71.0 57.1 %copy-start = (bf16[1,2,256,1536]{3,2,1,0:T(8,128)(2,1)S(1)}, bf16[1,2,256,1536]{3,2,1,0:T(8,128)(2,1)}, u32[]{:S(2)}) copy-start(bf16[1,2,256,1536]{3,2,1,0:T(8,128)(2,1)} %param.25) | copy-start | bytes 4718596
  71.8 99.6 %all-gather.17.cloned.1.call-start = ((), (), s32[]{:S(2)}) async-start(), calls=%async_computation.22 | async-start | bytes 1310720 | tf_op jit(solution)/shard_map/all_gather | solution.py:168
  72.1 169.2 %copy-start.49 = (f32[256,64]{0,1:T(8,128)}, f32[256,64]{0,1:T(8,128)S(1)}, u32[]{:S(2)}) copy-start(f32[256,64]{0,1:T(8,128)S(1)} %get-tuple-element.653) | copy-start | bytes 196612
  72.1 169.2 %copy-start.58 = (f32[256,64]{0,1:T(8,128)}, f32[256,64]{0,1:T(8,128)S(1)}, u32[]{:S(2)}) copy-start(f32[256,64]{0,1:T(8,128)S(1)} %get-tuple-element.654) | copy-start | bytes 196612
  132.1 96.6 %all-gather.13.cloned.1.call-start = ((), (), s32[]{:S(2)}) async-start(), calls=%async_computation.20 | async-start | bytes 4866048 | tf_op jit(solution)/shard_map/all_gather | solution.py:137
  132.7 161.2 %all-gather.23.cloned.1.call-start = ((), (), s32[]{:S(2)}) async-start(), calls=%async_computation.25 | async-start | bytes 4866048 | tf_op jit(solution)/shard_map/all_gather | solution.py:140
  133.3 376.5 %all-gather.25.cloned.1.call-start = ((), (), s32[]{:S(2)}) async-start(), calls=%async_computation.26 | async-start | bytes 17694720 | tf_op jit(solution)/shard_map/all_gather | solution.py:144
  134.1 590.9 %all-gather.27.cloned.1.call-start = ((), (), s32[]{:S(2)}) async-start(), calls=%async_computation.27 | async-start | bytes 17694720 | tf_op jit(solution)/shard_map/all_gather | solution.py:145
  134.8 805.4 %all-gather.29.cloned.1.call-start = ((), (), s32[]{:S(2)}) async-start(), calls=%async_computation.28 | async-start | bytes 17694720 | tf_op jit(solution)/shard_map/all_gather | solution.py:146
  137.5 951.2 %copy-start.99 = (f32[256]{0:T(256)}, f32[256]{0:T(256)S(1)}, u32[]{:S(2)}) copy-start(f32[256]{0:T(256)S(1)} %get-tuple-element.589) | copy-start | bytes 3076
  137.5 951.2 %copy-start.101 = (f32[256]{0:T(256)}, f32[256]{0:T(256)S(1)}, u32[]{:S(2)}) copy-start(f32[256]{0:T(256)S(1)} %get-tuple-element.687) | copy-start | bytes 3076
  138.9 27.1 copy-start.25
  139.8 158.7 %copy-start.75 = (f32[1536]{0:T(1024)}, f32[1536]{0:T(1024)S(1)}, u32[]{:S(2)}) copy-start(f32[1536]{0:T(1024)S(1)} %convert_element_type.388) | copy-start | bytes 18436
  961.1 147.3 %all-to-all-start.1 = ((bf16[4,10,64,1536]{3,2,1,0:T(8,128)(2,1)}), bf16[4,10,64,1536]{3,2,1,0:T(8,128)(2,1)}, u32[]{:S(2)}, u32[]{:S(2)}) async-start(bf16[4,10,64,1536]{3,2,1,0:T(8,128)(2,1)} %copy.190), calls=%async_computation.1 | async-start | bytes 15728640 | tf_op jit(solution)/shard_map/all_to_all | solution.py:220
  966.8 120.4 %copy-start.15 = (bf16[1,2,256,1536]{3,2,1,0:T(8,128)(2,1)S(1)}, bf16[1,2,256,1536]{3,2,1,0:T(8,128)(2,1)}, u32[]{:S(2)}) copy-start(bf16[1,2,256,1536]{3,2,1,0:T(8,128)(2,1)} %param.26) | copy-start | bytes 4718596
  1162.4 104.5 %all-to-all-start.4 = ((bf16[4,10,64,1536]{3,2,1,0:T(8,128)(2,1)}), bf16[4,10,64,1536]{3,2,1,0:T(8,128)(2,1)}, u32[]{:S(2)}, u32[]{:S(2)}) async-start(bf16[4,10,64,1536]{3,2,1,0:T(8,128)(2,1)} %bitcast.774), calls=%async_computation.4 | async-start | bytes 15728640 | tf_op jit(solution)/shard_map/all_to_all | solution.py:241
  1168.2 23.7 all-gather.33.cloned.1.call-start
  1171.4 45.2 %all-gather.31.cloned.1.call-start = ((), (), s32[]{:S(2)}) async-start(), calls=%async_computation.29 | async-start | bytes 1310720 | tf_op jit(solution)/shard_map/all_gather | solution.py:168
  1173.1 46.2 %copy-start.43 = (bf16[256,24,64]{0,2,1:T(8,128)(2,1)S(1)}, bf16[256,24,64]{0,2,1:T(8,128)(2,1)}, u32[]{:S(2)}) copy-start(bf16[256,24,64]{0,2,1:T(8,128)(2,1)} %get-tuple-element.642) | copy-start | bytes 2359300
  1317.6 93.7 %all-to-all-start.5 = ((bf16[4,10,64,1536]{3,2,1,0:T(8,128)(2,1)}), bf16[4,10,64,1536]{3,2,1,0:T(8,128)(2,1)}, u32[]{:S(2)}, u32[]{:S(2)}) async-start(bf16[4,10,64,1536]{3,2,1,0:T(8,128)(2,1)} %copy.204), calls=%async_computation.5 | async-start | bytes 15728640 | tf_op jit(solution)/shard_map/all_to_all | solution.py:267
  1368.6 74.3 %copy-start.5 = (f32[256,1536]{1,0:T(8,128)}, f32[256,1536]{1,0:T(8,128)S(1)}, u32[]{:S(2)}) copy-start(f32[256,1536]{1,0:T(8,128)S(1)} %get-tuple-element.675) | copy-start | bytes 4718596
  1369.2 73.7 %copy-start.96 = (f32[256]{0:T(256)}, f32[256]{0:T(256)S(1)}, u32[]{:S(2)}) copy-start(f32[256]{0:T(256)S(1)} %get-tuple-element.667) | copy-start | bytes 3076
  1369.4 73.5 %copy-start.78 = (bf16[256,40]{0,1:T(8,128)(2,1)}, bf16[256,40]{0,1:T(8,128)(2,1)S(1)}, u32[]{:S(2)}) copy-start(bf16[256,40]{0,1:T(8,128)(2,1)S(1)} %select_reduce_fusion.1) | copy-start | bytes 61444
  1601.0 93.6 %all-to-all-start.3 = ((bf16[4,10,64,1536]{3,2,1,0:T(8,128)(2,1)}), bf16[4,10,64,1536]{3,2,1,0:T(8,128)(2,1)}, u32[]{:S(2)}, u32[]{:S(2)}) async-start(bf16[4,10,64,1536]{3,2,1,0:T(8,128)(2,1)} %copy.202), calls=%async_computation.3 | async-start | bytes 15728640 | tf_op jit(solution)/shard_map/all_to_all | solution.py:220
  1879.2 93.2 %all-to-all-start.7 = ((bf16[4,10,64,1536]{3,2,1,0:T(8,128)(2,1)}), bf16[4,10,64,1536]{3,2,1,0:T(8,128)(2,1)}, u32[]{:S(2)}, u32[]{:S(2)}) async-start(bf16[4,10,64,1536]{3,2,1,0:T(8,128)(2,1)} %copy.215), calls=%async_computation.9 | async-start | bytes 15728640 | tf_op jit(solution)/shard_map/all_to_all | solution.py:267
  1884.9 423.4 %reduce-scatter.17.cloned.1.call-start = ((), (), s32[]{:S(2)}) async-start(), calls=%async_computation.32 | async-start | bytes 1310720 | tf_op jit(solution)/shard_map/reduce_scatter | solution.py:306
  1979.3 25.0 copy-start.77
  1979.3 25.0 copy-start.97
  2101.8 211.1 %reduce-scatter.21.cloned.1.call-start = ((), (), s32[]{:S(2)}) async-start(), calls=%async_computation.34 | async-start | bytes 1310720 | tf_op jit(solution)/shard_map/reduce_scatter | solution.py:306
  2188.4 129.0 %reduce-scatter.15.cloned.1.call-start = ((), (), s32[]{:S(2)}) async-start(), calls=%async_computation.31 | async-start | bytes 1310720 | tf_op jit(solution)/shard_map/reduce_scatter | solution.py:303
  2189.0 128.4 %reduce-scatter.19.cloned.1.call-start = ((), (), s32[]{:S(2)}) async-start(), calls=%async_computation.33 | async-start | bytes 1310720 | tf_op jit(solution)/shard_map/reduce_scatter | solution.py:303
  2189.6 175.3 %reduce-scatter.37.cloned.1.call-start = ((), (), s32[]{:S(2)}) async-start(), calls=%async_computation.42 | async-start | bytes 811008
  2211.2 409.5 %reduce-scatter.35.cloned.1.call-start = ((), (), s32[]{:S(2)}) async-start(), calls=%async_computation.41 | async-start | bytes 17694720 | tf_op jit(solution)/shard_map/reduce_scatter | solution.py:373
  2232.7 641.7 %reduce-scatter.31.cloned.1.call-start = ((), (), s32[]{:S(2)}) async-start(), calls=%async_computation.39 | async-start | bytes 17694720 | tf_op jit(solution)/shard_map/reduce_scatter | solution.py:373
  2270.5 857.7 %reduce-scatter.33.cloned.1.call-start = ((), (), s32[]{:S(2)}) async-start(), calls=%async_computation.40 | async-start | bytes 17694720 | tf_op jit(solution)/shard_map/reduce_scatter | solution.py:373
  2308.2 926.6 %reduce-scatter.27.cloned.1.call-start = ((), (), s32[]{:S(2)}) async-start(), calls=%async_computation.37 | async-start | bytes 3244032 | tf_op jit(solution)/shard_map/reduce_scatter | solution.py:370
  2317.3 1024.0 %reduce-scatter.25.cloned.1.call-start = ((), (), s32[]{:S(2)}) async-start(), calls=%async_computation.36 | async-start | bytes 3244032 | tf_op jit(solution)/shard_map/reduce_scatter | solution.py:370
  2322.8 1159.4 %reduce-scatter.29.cloned.1.call-start = ((), (), s32[]{:S(2)}) async-start(), calls=%async_computation.38 | async-start | bytes 9732096 | tf_op jit(solution)/shard_map/reduce_scatter | solution.py:370
  2332.1 1292.2 %reduce-scatter.23.cloned.1.call-start = ((), (), s32[]{:S(2)}) async-start(), calls=%async_computation.35 | async-start | bytes 9732096 | tf_op jit(solution)/shard_map/reduce_scatter | solution.py:370
  2377.4 49.6 %copy-start.12 = (f32[256,1536]{1,0:T(8,128)S(1)}, f32[256,1536]{1,0:T(8,128)}, u32[]{:S(2)}) copy-start(f32[256,1536]{1,0:T(8,128)} %copy-done.10) | copy-start | bytes 4718596
  2377.4 49.6 %copy-start.107 = (f32[256]{0:T(256)S(1)}, f32[256]{0:T(256)}, u32[]{:S(2)}) copy-start(f32[256]{0:T(256)} %get-tuple-element.662) | copy-start | bytes 3076
  2377.4 49.6 %copy-start.108 = (f32[256]{0:T(256)S(1)}, f32[256]{0:T(256)}, u32[]{:S(2)}) copy-start(f32[256]{0:T(256)} %get-tuple-element.682) | copy-start | bytes 3076
  (104 other events, 575.6 us)
Sparse Core Ops, SparseCore 0:
  10.9 57.7 all-gather.18
  71.6 53.9 all-gather.14
  127.7 15.7 all-gather.20
  145.4 16.8 all-gather.16
  165.1 63.5 all-gather.12
  231.5 62.4 all-gather.22
  296.1 213.5 all-gather.24
  512.0 212.9 all-gather.26
  727.2 212.9 all-gather.28
  1171.5 20.2 all-gather.32
  1194.0 22.5 all-gather.30
  2101.9 21.0 reduce-scatter.16
  2188.5 21.0 reduce-scatter.20
  2212.0 24.9 reduce-scatter.14
  2239.5 24.8 reduce-scatter.18
  2269.4 95.4 reduce-scatter.36
  2368.3 252.3 reduce-scatter.34
  2624.2 250.2 reduce-scatter.30
  2878.0 250.2 reduce-scatter.32
  3134.1 100.6 reduce-scatter.26
  3240.8 100.4 reduce-scatter.24
  3347.8 134.4 reduce-scatter.28
  3489.8 134.5 reduce-scatter.22
where the time goes:
time: 3640 us; the launch traced here: 3630 us
  waiting for transfers between devices  2090 us (57%)
  matrix products  578 us (16%)
  blocking collectives  484 us (13%)
  local copies, waits for them, and re-layouts  293 us (8%)
  other arithmetic  136 us (4%)
    reduce_scatter x3, waiting for transfers between devices, shards(): lax.psum_scatter(as_sent(expert_total), 'dp', scatter_dimension=1, tiled=...  688 us
    reduce_scatter x4, waiting for transfers between devices, shards(): lax.psum_scatter(dense_total, ('dp', 'expert'), scatter_dimension=0, tile...  492 us
    all_gather x1, waiting for transfers between devices, shards(): full_up = lax.all_gather(w_up, 'dp', axis=1, tiled=True)  201 us
    all_gather x1, waiting for transfers between devices, shards(): full_down = lax.all_gather(w_down, 'dp', axis=1, tiled=True)  197 us
    all_to_all x2, blocking collectives, shards(): lax.all_to_all(send_rows, 'expert', split_axis=0, concat_axis=0, tiled=True)  186 us
    dot_general x58, matrix products, contract_cols(): lax.dot_general(left, right, (((1,), (1,)), ((), ())), preferred_element_...  120 us
    all_to_all x2, waiting for transfers between devices, shards(): lax.all_to_all(grad_rows, 'expert', split_axis=0, concat_axis=0, tiled=True)  119 us
    all_gather x1, blocking collectives, shards(): full_router = lax.all_gather(w_router, ('dp', 'expert'), axis=0, tiled=True)  118 us
  transfers between devices with their start and end apart: 28, of which 21 were waited for; matrix products, arithmetic and copies ran while one was open for 15% of the time, Pallas kernels for 0%

commit v1 on v0

v1 whole, which is shorter than its diff:
```python
import functools

import jax
import jax.numpy as jnp
from jax import lax
from jax.experimental import pallas as pl
from jax.experimental.pallas import tpu as pltpu
from jax.sharding import PartitionSpec as P

QUERY_HEAD_COUNT = 24
KEY_VALUE_HEADS = 8
HEAD_DIMENSION = 64
EXPERTS = 40
TOPK = 8

epsilon = 1e-06
rope_base = 10000.0
masked_score = -1e30

F32 = jnp.float32
BF16 = jnp.bfloat16
AXES = ("dp", "expert")
HALF_HEAD = HEAD_DIMENSION // 2
GROUP = QUERY_HEAD_COUNT // KEY_VALUE_HEADS
PAIRS = KEY_VALUE_HEADS // 2
PAIR_LANES = 2 * HEAD_DIMENSION
QUERY_LANES = GROUP * PAIR_LANES
LANES = 128
BLOCKS_PER_STEP = 4


def dot(left, right):
    return jnp.dot(left, right, preferred_element_type=F32)


def dot_rows(left, right):
    return lax.dot_general(left, right, (((0,), (0,)), ((), ())), preferred_element_type=F32)


def dot_cols(left, right):
    return lax.dot_general(left, right, (((1,), (1,)), ((), ())), preferred_element_type=F32)


def add_rounded(left, right):
    return (left.astype(F32) + right.astype(F32)).astype(left.dtype)


def params(limit_mib, steps=1):
    return pltpu.CompilerParams(
        dimension_semantics=("arbitrary",) * steps, vmem_limit_bytes=limit_mib << 20
    )


def lasting(micros):
    return pl.CostEstimate(flops=int(micros * 1.1e9), bytes_accessed=0, transcendentals=0)


def whole_spec():
    return pl.BlockSpec(memory_space=pltpu.VMEM)


def swap(array, place):
    axis, bit = place
    dp_count, owner_count = lax.axis_size("dp"), lax.axis_size("expert")
    flip = (1 << bit) * (owner_count if axis == "dp" else 1)
    return lax.ppermute(array, AXES, [(i, i ^ flip) for i in range(dp_count * owner_count)])


def gather_pieces(array, places):
    pieces = [array]
    for place in places:
        pieces = pieces + [swap(piece, place) for piece in pieces]
    return pieces


def after(value, *others):
    return lax.optimization_barrier((value, *others))


def gather_rows(array, places):
    pieces = jnp.stack(gather_pieces(array, places[:-1]))
    return pieces, swap(pieces, places[-1])


def sum_home(low, high, places):
    for place in reversed(places):
        total = high.shape[0]
        received = swap(high, place)
        if total == 1:
            return add_rounded(low, received)
        low, high = (
            add_rounded(low[: total // 2], received[: total // 2]),
            add_rounded(low[total // 2 :], received[total // 2 :]),
        )
    return low


class Trip:
    def __init__(self, stages, places, split):
        self.stages, self.places, self.split = stages[:-2], places, split
        self.rest = stages[-2]
        self.stage = len(places) - 1
        self.waiting = [swap(stages[-1], places[-1])]
        self.first = True
        self.mine = self.other = None

    def gather(self, received, stages):
        start = 0
        for stage in stages:
            size = self.stages[stage].shape[0]
            self.stages[stage] = add_rounded(
                self.stages[stage], received[start : start + size]
            )
            start += size

    def step(self, received):
        if self.first:
            self.first = False
            self.gather(received, [self.stage])
            self.waiting = [
                swap(self.rest, self.places[-1]),
                swap(self.stages[self.stage], self.places[self.stage - 1]),
            ]
            self.rest = None
        elif self.stage == len(self.places) - 1:
            self.gather(received, range(self.stage))
            self.stage -= 1
        elif self.stage > 0:
            self.gather(received, range(self.stage + 1))
            self.waiting.append(swap(self.stages[self.stage], self.places[self.stage - 1]))
            self.stage -= 1
        else:
            mine, received = self.stages[0][0].astype(F32), received[0].astype(F32)
            self.mine = mine if self.split == 2 else mine + received
            self.other = received


def arrive(value, *trips):
    value, *received = after(value, *[trip.waiting[0] for trip in trips])
    for trip, array in zip(trips, received):
        trip.waiting = trip.waiting[1:]
        trip.step(array)
    return value


def masks_of(places):
    found = []
    for piece in range(1 << len(places)):
        mask = {"dp": 0, "expert": 0}
        for stage, (axis, bit) in enumerate(places):
            if piece >> stage & 1:
                mask[axis] |= 1 << bit
        found.append(mask)
    return found


def half_swap(rows):
    lane = lax.broadcasted_iota(jnp.int32, rows.shape, 1)
    return jnp.where(
        lane % HEAD_DIMENSION < HALF_HEAD,
        pltpu.roll(rows, rows.shape[1] - HALF_HEAD, 1),
        pltpu.roll(rows, HALF_HEAD, 1),
    )


def project_kernel(x_ref, gain_ref, w_ref, cos_ref, sin_ref, h_ref, q_ref, kv_ref):
    x = x_ref[0].astype(F32)
    scale = lax.rsqrt(jnp.mean(x * x, axis=1, keepdims=True) + epsilon)
    h_ref[0] = (x * scale * gain_ref[...]).astype(BF16)
    cos, sin = cos_ref[...], sin_ref[...]
    width = q_ref.shape[2]
    key_width = kv_ref.shape[2] // 2

    def turn_into(out_ref, start, rows):
        for tile in range(0, rows.shape[1], LANES):
            part = rows[:, tile : tile + LANES]
            out_ref[0, :, start + tile : start + tile + LANES] = (
                part * cos + half_swap(part) * sin
            ).astype(BF16)

    for start in range(0, width, key_width):
        turn_into(q_ref, start, dot(h_ref[0], w_ref[:, start : start + key_width]))
    turn_into(kv_ref, 0, dot(h_ref[0], w_ref[:, width : width + key_width]))
    value = dot(h_ref[0], w_ref[:, width + key_width : width + 2 * key_width])
    kv_ref[0, :, key_width:] = value.astype(BF16)


def project(x, gain, dense, cos, sin):
    count, rows, width = x.shape
    key_width = KEY_VALUE_HEADS * HEAD_DIMENSION
    row_spec = pl.BlockSpec((1, rows, width), lambda i: (i, 0, 0))
    return pl.pallas_call(
        project_kernel,
        grid=(count,),
        in_specs=[
            row_spec,
            pl.BlockSpec((1, width), lambda i: (0, 0)),
            pl.BlockSpec(dense.shape, lambda i: (0, 0)),
            pl.BlockSpec((rows, LANES), lambda i: (0, 0)),
            pl.BlockSpec((rows, LANES), lambda i: (0, 0)),
        ],
        out_specs=[
            row_spec,
            row_spec,
            pl.BlockSpec((1, rows, 2 * key_width), lambda i: (i, 0, 0)),
        ],
        out_shape=[
            jax.ShapeDtypeStruct(x.shape, BF16),
            jax.ShapeDtypeStruct(x.shape, BF16),
            jax.ShapeDtypeStruct((count, rows, 2 * key_width), BF16),
        ],
        cost_estimate=lasting(8),
        compiler_params=params(48),
    )(x, gain, dense, cos, sin)


def middle_kernel(x_ref, o_ref, wo_ref, wr_ref, gain_ref, code_ref, y_ref, h_ref, g_ref):
    middle = x_ref[...].astype(F32) + dot(o_ref[...], wo_ref[...])
    y_ref[...] = middle
    scale = lax.rsqrt(jnp.mean(middle * middle, axis=1, keepdims=True) + epsilon)
    normed = (middle * scale * gain_ref[...]).astype(BF16)
    h_ref[...] = normed
    logits = dot(normed, wr_ref[...])
    chosen = code_ref[...] > -1.5
    peak = jnp.max(jnp.where(chosen, logits, masked_score), axis=1, keepdims=True)
    raised = jnp.where(chosen, jnp.exp(jnp.where(chosen, logits, peak) - peak), 0.0)
    g_ref[...] = raised / jnp.sum(raised, axis=1, keepdims=True)


def middle_rows(x, attended, dense, gain, code):
    rows, width = x.shape
    full = pl.BlockSpec((rows, width), lambda i: (0, 0))
    return pl.pallas_call(
        middle_kernel,
        grid=(1,),
        in_specs=[
            full,
            full,
            pl.BlockSpec((width, width), lambda i: (0, 0)),
            pl.BlockSpec((width, LANES), lambda i: (0, width // LANES)),
            pl.BlockSpec((1, width), lambda i: (0, 0)),
            pl.BlockSpec((rows, LANES), lambda i: (0, 0)),
        ],
        out_specs=[full, full, pl.BlockSpec((rows, LANES), lambda i: (0, 0))],
        out_shape=[
            jax.ShapeDtypeStruct((rows, width), F32),
            jax.ShapeDtypeStruct((rows, width), BF16),
            jax.ShapeDtypeStruct((rows, LANES), F32),
        ],
        cost_estimate=lasting(4.5),
        compiler_params=params(48),
    )(x, attended, dense, dense, gain, code)


def middle_back_kernel(
    acc_ref, y_ref, dy_ref, g_ref, dg_ref, gain_ref, wr_ref, wo_ref,
    dz_ref, dy1_ref, dr_ref, do_ref, dgain_ref,
):
    gates, gate_grads = g_ref[...], dg_ref[...].astype(F32)
    mean = jnp.sum(gates * gate_grads, axis=1, keepdims=True)
    dz = (gates * (gate_grads - mean)).astype(BF16)
    dz_ref[...] = dz
    dh = acc_ref[...].astype(F32) + dot_cols(dz, wr_ref[...])
    middle = y_ref[...]
    scale = lax.rsqrt(jnp.mean(middle * middle, axis=1, keepdims=True) + epsilon)
    dgain_ref[...] = jnp.sum(dh * middle * scale, axis=0, keepdims=True)
    scaled = dh * gain_ref[...]
    along = jnp.mean(scaled * middle, axis=1, keepdims=True)
    dy1 = dy_ref[...].astype(F32) + scale * scaled - middle * (scale * scale * scale * along)
    dy1_ref[...] = dy1
    rounded = dy1.astype(BF16)
    dr_ref[...] = rounded
    do_ref[...] = dot_cols(rounded, wo_ref[...]).astype(BF16)


def middle_back(acc, middle, dy, gates, gain, dense):
    rows, width = middle.shape
    full = pl.BlockSpec((rows, width), lambda i: (0, 0))
    lane = pl.BlockSpec((rows, LANES), lambda i: (0, 0))
    line = pl.BlockSpec((1, width), lambda i: (0, 0))
    return pl.pallas_call(
        middle_back_kernel,
        grid=(1,),
        in_specs=[
            full, full, full, lane,
            pl.BlockSpec((rows, LANES), lambda i: (0, width // LANES)),
            line,
            pl.BlockSpec((width, LANES), lambda i: (0, width // LANES)),
            pl.BlockSpec((width, width), lambda i: (0, 0)),
        ],
        out_specs=[lane, full, full, full, line],
        out_shape=[
            jax.ShapeDtypeStruct((rows, LANES), BF16),
            jax.ShapeDtypeStruct((rows, width), F32),
            jax.ShapeDtypeStruct((rows, width), BF16),
            jax.ShapeDtypeStruct((rows, width), BF16),
            jax.ShapeDtypeStruct((1, width), F32),
        ],
        cost_estimate=lasting(6.6),
        compiler_params=params(56),
    )(acc, middle, dy, gates, acc, gain, dense, dense)


def project_back_kernel(
    dq_ref, pairs_ref, x_ref, dy1_ref, gain_ref, w_ref, cos_ref, sin_ref,
    dx_ref, dkv_ref, dgain_ref,
):
    cos, sin = cos_ref[...], sin_ref[...]
    width = x_ref.shape[1]
    key_width = dkv_ref.shape[1] // 2
    for pair in range(PAIRS):
        lanes = slice(pair * LANES, (pair + 1) * LANES)
        start = 2 * pair * LANES
        part = pairs_ref[:, start : start + LANES].astype(F32)
        dkv_ref[:, lanes] = (part * cos - half_swap(part) * sin).astype(BF16)
        lanes = slice(key_width + pair * LANES, key_width + (pair + 1) * LANES)
        dkv_ref[:, lanes] = pairs_ref[:, start + LANES : start + 2 * LANES]
    dh = dot_cols(dq_ref[...], w_ref[:, :width])
    dh = dh + dot_cols(dkv_ref[...], w_ref[:, width : width + 2 * key_width])
    x = x_ref[...].astype(F32)
    scale = lax.rsqrt(jnp.mean(x * x, axis=1, keepdims=True) + epsilon)
    dgain_ref[...] = jnp.sum(dh * x * scale, axis=0, keepdims=True)
    scaled = dh * gain_ref[...]
    along = jnp.mean(scaled * x, axis=1, keepdims=True)
    dx_ref[...] = dy1_ref[...] + scale * scaled - x * (scale * scale * scale * along)


def project_back(dq, pairs, x, dy1, gain, dense, cos, sin):
    rows, width = x.shape
    key_width = pairs.shape[1] // 2
    full = pl.BlockSpec((rows, width), lambda i: (0, 0))
    lane = pl.BlockSpec((rows, LANES), lambda i: (0, 0))
    line = pl.BlockSpec((1, width), lambda i: (0, 0))
    both = pl.BlockSpec((rows, 2 * key_width), lambda i: (0, 0))
    return pl.pallas_call(
        project_back_kernel,
        grid=(1,),
        in_specs=[
            full, both, full, full, line, pl.BlockSpec(dense.shape, lambda i: (0, 0)), lane, lane,
        ],
        out_specs=[full, both, line],
        out_shape=[
            jax.ShapeDtypeStruct((rows, width), F32),
            jax.ShapeDtypeStruct((rows, 2 * key_width), BF16),
            jax.ShapeDtypeStruct((1, width), F32),
        ],
        cost_estimate=lasting(8.2),
        compiler_params=params(56),
    )(dq, pairs, x, dy1, gain, dense, cos, sin)


def weight_grad_kernel(count, *refs):
    left_refs, right_refs, out_ref = refs[:count], refs[count : 2 * count], refs[-1]
    rows, columns = out_ref.shape
    if len(refs) > 2 * count + 1:
        gain = jnp.broadcast_to(refs[2 * count][...], (8, rows)).T
    lane = lax.broadcasted_iota(jnp.int32, (rows, LANES), 1)
    start = 0
    for left_ref, right_ref in zip(left_refs, right_refs):
        left = left_ref[...].T
        width = right_ref.shape[1]
        step = min(width, 4 * LANES)
        for tile in range(0, width, step):
            part = dot(left, right_ref[:, tile : tile + step])
            if start + tile + step == columns and len(refs) > 2 * count + 1:
                edge = part[:, step - LANES :]
                edge = jnp.where(lane == EXPERTS, gain[:, 0:1], edge)
                out_ref[:, columns - LANES :] = edge.astype(BF16)
                part = part[:, : step - LANES]
            if part.shape[1]:
                out_ref[:, start + tile : start + tile + part.shape[1]] = part.astype(BF16)
        start += width
    if start < columns:
        out_ref[:, start:] = jnp.where(lane == EXPERTS, gain[:, 0:1], 0.0).astype(BF16)


def weight_grads(lefts, rights, gain, columns):
    rows = lefts[0].shape[1]
    operands = [*lefts, *rights] + ([] if gain is None else [gain])
    return pl.pallas_call(
        functools.partial(weight_grad_kernel, len(lefts)),
        in_specs=[whole_spec() for _ in operands],
        out_specs=whole_spec(),
        out_shape=jax.ShapeDtypeStruct((rows, columns), BF16),
        cost_estimate=lasting(9),
        compiler_params=pltpu.CompilerParams(vmem_limit_bytes=56 << 20),
    )(*operands)


def fill_bias(places_ref, bias_ref, rows):
    query = places_ref[0] + lax.broadcasted_iota(jnp.int32, (rows, rows), 1)
    inside = lax.broadcasted_iota(jnp.int32, (rows, rows), 0)
    for block in range(bias_ref.shape[0] // rows):
        key = places_ref[2 + block] + inside
        allowed = (key <= query) & (key < places_ref[1])
        bias_ref[block * rows : (block + 1) * rows, :] = jnp.where(allowed, 0.0, masked_score)


def attend_kernel(places_ref, q_ref, k_ref, v_ref, o_ref, lse_ref, bias_ref):
    rows = q_ref.shape[0]

    @pl.when(pl.program_id(0) == 0)
    def _():
        fill_bias(places_ref, bias_ref, rows)

    outs = []
    for side in range(2):
        lanes = slice(side * HEAD_DIMENSION, (side + 1) * HEAD_DIMENSION)
        key = k_ref[:, lanes]
        value_t = v_ref[:, lanes].T
        for member in range(GROUP):
            head = side * GROUP + member
            query = q_ref[:, head * HEAD_DIMENSION : (head + 1) * HEAD_DIMENSION]
            scores = dot_cols(key, query * HEAD_DIMENSION**-0.5) + bias_ref[...]
            peak = jnp.max(scores, axis=0, keepdims=True)
            raised = jnp.exp(scores - peak)
            total = jnp.sum(raised, axis=0, keepdims=True)
            outs.append(dot(value_t, raised.astype(BF16)) / total)
            lse_ref[0, head : head + 1, :] = peak + jnp.log(total)
    o_ref[...] = jnp.concatenate(outs, axis=0).T.astype(BF16)


def attend(places, q, kv):
    rows, width = q.shape
    keys = kv.shape[0]
    return pl.pallas_call(
        attend_kernel,
        grid_spec=pltpu.PrefetchScalarGridSpec(
            num_scalar_prefetch=1,
            grid=(PAIRS,),
            in_specs=[
                pl.BlockSpec((rows, QUERY_LANES), lambda i, s: (0, i)),
                pl.BlockSpec((keys, PAIR_LANES), lambda i, s: (0, i)),
                pl.BlockSpec((keys, PAIR_LANES), lambda i, s: (0, PAIRS + i)),
            ],
            out_specs=[
                pl.BlockSpec((rows, QUERY_LANES), lambda i, s: (0, i)),
                pl.BlockSpec((1, 8, rows), lambda i, s: (i, 0, 0)),
            ],
            scratch_shapes=[pltpu.VMEM((keys, rows), F32)],
        ),
        out_shape=[
            jax.ShapeDtypeStruct((rows, width), BF16),
            jax.ShapeDtypeStruct((PAIRS, 8, rows), F32),
        ],
        cost_estimate=lasting(19),
        compiler_params=params(48),
    )(places, q, kv, kv)


def attend_back_kernel(
    places_ref, q_ref, k_ref, v_ref, do_ref, o_ref, lse_ref, cos_ref, sin_ref,
    dq_ref, dkv_ref, bias_ref,
):
    rows = q_ref.shape[0]

    @pl.when(pl.program_id(0) == 0)
    def _():
        fill_bias(places_ref, bias_ref, rows)

    score_scale = HEAD_DIMENSION**-0.5
    cos, sin = cos_ref[...], sin_ref[...]
    ones = jnp.ones((8, HEAD_DIMENSION), F32)
    query_grads = []
    for side in range(2):
        lanes = slice(side * HEAD_DIMENSION, (side + 1) * HEAD_DIMENSION)
        key, value = k_ref[:, lanes], v_ref[:, lanes]
        key_t = key.T
        key_grad = None
        value_grad = None
        for member in range(GROUP):
            head = side * GROUP + member
            columns = slice(head * HEAD_DIMENSION, (head + 1) * HEAD_DIMENSION)
            query = q_ref[:, columns] * score_scale
            grad = do_ref[:, columns]
            overlap = grad.astype(F32) * o_ref[:, columns].astype(F32)
            along = lax.dot_general(
                ones, overlap, (((1,), (1,)), ((), ())),
                precision=lax.Precision.HIGHEST, preferred_element_type=F32,
            )[0:1]
            scores = dot_cols(key, query) + bias_ref[...]
            probs = jnp.exp(scores - lse_ref[0, head : head + 1, :])
            score_grad = (probs * (dot_cols(value, grad) - along)).astype(BF16)
            value_part = dot(probs.astype(BF16), grad)
            key_part = dot(score_grad, query)
            value_grad = value_part if value_grad is None else value_grad + value_part
            key_grad = key_part if key_grad is None else key_grad + key_part
            turned = dot(key_t, score_grad) * score_scale
            upper, lower = turned[:HALF_HEAD], turned[HALF_HEAD:]
            query_grads += [upper * cos + lower * sin, lower * cos - upper * sin]
        dkv_ref[:, lanes] = key_grad.astype(BF16)
        shifted = slice(LANES + side * HEAD_DIMENSION, LANES + (side + 1) * HEAD_DIMENSION)
        dkv_ref[:, shifted] = value_grad.astype(BF16)
    dq_ref[...] = jnp.concatenate(query_grads, axis=0).T.astype(BF16)


def attend_back(places, q, kv, grad, attended, lse, cos_t, sin_t):
    rows, width = q.shape
    keys = kv.shape[0]
    key_width = kv.shape[1] // 2
    wide = pl.BlockSpec((rows, QUERY_LANES), lambda i, s: (0, i))
    tall = pl.BlockSpec((keys, PAIR_LANES), lambda i, s: (0, i))
    table = pl.BlockSpec((HALF_HEAD, rows), lambda i, s: (0, 0))
    return pl.pallas_call(
        attend_back_kernel,
        grid_spec=pltpu.PrefetchScalarGridSpec(
            num_scalar_prefetch=1,
            grid=(PAIRS,),
            in_specs=[
                wide,
                tall,
                pl.BlockSpec((keys, PAIR_LANES), lambda i, s: (0, PAIRS + i)),
                wide,
                wide,
                pl.BlockSpec((1, 8, rows), lambda i, s: (i, 0, 0)),
                table,
                table,
            ],
            out_specs=[wide, pl.BlockSpec((keys, 2 * PAIR_LANES), lambda i, s: (0, i))],
            scratch_shapes=[pltpu.VMEM((keys, rows), F32)],
        ),
        out_shape=[
            jax.ShapeDtypeStruct((rows, width), BF16),
            jax.ShapeDtypeStruct((keys, 2 * key_width), BF16),
        ],
        cost_estimate=lasting(23.5),
        compiler_params=params(56),
    )(places, q, kv, kv, grad, attended, lse, cos_t, sin_t)


def expert_kernel(masks, stage_sizes, expert, aliased, me_ref, *refs):
    count = len(masks)
    pieces, refs = refs[:count], refs[count:]
    h_ref, dy_ref, rank_ref, gate_ref = refs[:4]
    refs = refs[4 + (2 if aliased else 0) :]
    eg_ref, db_ref = refs[:2]
    out_refs, refs = refs[2 : 2 + len(stage_sizes)], refs[2 + len(stage_sizes) :]
    w_in, w_down, g_in, g_down, rows_all, de_all, hidden_all, dau_all, in_sem, out_sem = refs
    step = pl.program_id(0)
    blocks, tokens, width = h_ref.shape
    slots = eg_ref.shape[2]
    chunk = blocks * slots
    inner = w_down.shape[0]
    deep = width // count
    shallow = inner // count
    wide = width // inner
    me = me_ref[0]

    def windows(piece_ref, shard, into, down):
        top = pl.ds(pl.multiple_of(shard * deep, 16), deep)
        low = pl.ds(pl.multiple_of(shard * shallow, 16), shallow)
        pairs = [
            (piece_ref.at[pl.ds(0, deep)], into.at[top, pl.ds(0, inner)]),
            (piece_ref.at[pl.ds(deep, deep)], into.at[top, pl.ds(inner, inner)]),
        ]
        for part in range(wide):
            pairs.append(
                (
                    piece_ref.at[pl.ds(2 * deep + part * shallow, shallow)],
                    down.at[low, pl.ds(part * inner, inner)],
                )
            )
        return pairs

    def loads():
        made = []
        for piece, mask in enumerate(masks):
            for source, target in windows(pieces[piece].at[expert], me ^ mask, w_in, w_down):
                made.append(pltpu.make_async_copy(source, target, in_sem.at[len(made)]))
        return made

    def stores():
        made = []
        for piece, mask in enumerate(masks):
            start = 0
            for out_ref, size in zip(out_refs, stage_sizes):
                if start <= piece < start + size:
                    target = out_ref.at[piece - start]
                start += size
            for there, here in windows(target, me ^ mask, g_in, g_down):
                made.append(pltpu.make_async_copy(here, there, out_sem.at[len(made)]))
        return made

    @pl.when(step == 0)
    def _():
        for copy in loads():
            copy.start()

    slot = lax.broadcasted_iota(jnp.int32, (slots, tokens), 0)
    grads = []
    weights = []
    for block in range(blocks):
        start = pl.multiple_of((step * blocks + block) * tokens, LANES)
        hit = slot == rank_ref[expert : expert + 1, pl.ds(start, tokens)]
        select = jnp.where(hit, 1.0, 0.0).astype(BF16)
        place = pl.ds(pl.multiple_of(step * chunk + block * slots, 16), slots)
        rows_all[place, :] = dot(select, h_ref[block]).astype(BF16)
        grads.append(dot(select, dy_ref[block]))
        gate = gate_ref[expert : expert + 1, pl.ds(start, tokens)]
        weights.append(jnp.sum(jnp.where(hit, gate, 0.0), axis=1, keepdims=True))

    @pl.when(step == 0)
    def _():
        for copy in loads():
            copy.wait()

    here = pl.ds(pl.multiple_of(step * chunk, 16), chunk)
    grad_rows = jnp.concatenate(grads, axis=0)
    weight = jnp.concatenate(weights, axis=0)
    pre = dot(rows_all[here, :], w_in[...])
    gate_pre, up_pre = pre[:, :inner], pre[:, inner:]
    sigmoid = 1.0 / (1.0 + jnp.exp(-gate_pre))
    silu = gate_pre * sigmoid
    hidden = (silu * up_pre).astype(BF16)
    hidden_all[here, :] = hidden
    out = dot(hidden, w_down[...]).astype(BF16).astype(F32)
    row_grad = jnp.sum(grad_rows * out, axis=1, keepdims=True)
    out = (weight * out).astype(BF16)
    lane = lax.broadcasted_iota(jnp.int32, (slots, LANES), 1)
    for block in range(blocks):
        part = slice(block * slots, (block + 1) * slots)
        eg_ref[block, 0] = out[part]
        db_ref[block, 0, :, width:] = jnp.where(lane == me_ref[1] + expert, row_grad[part], 0.0).astype(
            BF16
        )
    de = (weight * grad_rows).astype(BF16)
    de_all[here, :] = de
    grad_hidden = dot_cols(de, w_down[...])
    grad_up = (grad_hidden * silu).astype(BF16)
    grad_gate = (
        grad_hidden * up_pre * sigmoid * (1.0 + gate_pre * (1.0 - sigmoid))
    ).astype(BF16)
    dau_all[here, :inner] = grad_gate
    dau_all[here, inner:] = grad_up
    back = dot_cols(dau_all[here, :], w_in[...]).astype(BF16)
    for block in range(blocks):
        db_ref[block, 0, :, :width] = back[block * slots : (block + 1) * slots]

    @pl.when(step == pl.num_programs(0) - 1)
    def _():
        for part in range(wide):
            lanes = slice(part * inner, (part + 1) * inner)
            g_in[lanes, :] = dot_rows(rows_all[:, lanes], dau_all[...]).astype(BF16)
        g_down[...] = dot_rows(hidden_all[...], de_all[...]).astype(BF16)
        made = stores()
        for copy in made:
            copy.start()
        for copy in made:
            copy.wait()


def run_expert(
    expert, me, pieces, masks, h_all, dy_all, ranks, gates, slots, local, earlier
):
    block_count, tokens, width = h_all.shape
    piece_rows, inner = pieces[0].shape[1:]
    count = len(pieces)
    stage_sizes = [1]
    while 2 * sum(stage_sizes) < count:
        stage_sizes.append(sum(stage_sizes))
    stage_sizes += [count // 4, count // 4]
    steps = block_count // BLOCKS_PER_STEP
    rows = block_count * slots
    block_spec = pl.BlockSpec((BLOCKS_PER_STEP, tokens, width), lambda i, s: (i, 0, 0))
    any_spec = pl.BlockSpec(memory_space=pl.ANY)
    table = pl.BlockSpec(ranks.shape, lambda i, s: (0, 0))
    widths = (width, width + LANES)
    copies = count * (2 + width // inner)
    aliases = {}
    extra = []
    if earlier is not None:
        extra = list(earlier)
        aliases = {1 + count + 4: 0, 1 + count + 5: 1}
    return pl.pallas_call(
        functools.partial(expert_kernel, masks, stage_sizes, expert, earlier is not None),
        grid_spec=pltpu.PrefetchScalarGridSpec(
            num_scalar_prefetch=1,
            grid=(steps,),
            in_specs=[any_spec] * count
            + [block_spec, block_spec, table, table]
            + [any_spec] * len(extra),
            out_specs=[
                pl.BlockSpec((BLOCKS_PER_STEP, 1, slots, w), lambda i, s: (i, expert, 0, 0))
                for w in widths
            ]
            + [any_spec] * len(stage_sizes),
            scratch_shapes=[
                pltpu.VMEM((width, 2 * inner), BF16),
                pltpu.VMEM((inner, width), BF16),
                pltpu.VMEM((width, 2 * inner), BF16),
                pltpu.VMEM((inner, width), BF16),
                pltpu.VMEM((rows, width), BF16),
                pltpu.VMEM((rows, width), BF16),
                pltpu.VMEM((rows, inner), BF16),
                pltpu.VMEM((rows, 2 * inner), BF16),
                pltpu.SemaphoreType.DMA((copies,)),
                pltpu.SemaphoreType.DMA((copies,)),
            ],
        ),
        out_shape=[jax.ShapeDtypeStruct((block_count, local, slots, w), BF16) for w in widths]
        + [jax.ShapeDtypeStruct((size, piece_rows, inner), BF16) for size in stage_sizes],
        input_output_aliases=aliases,
        cost_estimate=lasting(31),
        compiler_params=params(60),
    )(me, *pieces, h_all, dy_all, ranks, gates, *extra)


def combine_kernel(src_ref, place_ref, out_ref):
    _, local, slots, width = src_ref.shape
    tokens = out_ref.shape[1]
    lane = lax.broadcasted_iota(jnp.int32, (tokens, local * slots), 1)
    hit = lane == place_ref[0, :, 0:1]
    for expert in range(1, local):
        hit = hit | (lane == place_ref[0, :, expert : expert + 1])
    source = src_ref[0].reshape(local * slots, width)
    out_ref[0] = dot(jnp.where(hit, 1.0, 0.0).astype(BF16), source).astype(BF16)


def combine(source, places, first, size):
    _, local, slots, width = source.shape
    tokens = places.shape[1]
    return pl.pallas_call(
        combine_kernel,
        grid=(size,),
        in_specs=[
            pl.BlockSpec((1, local, slots, width), lambda i: (first + i, 0, 0, 0)),
            pl.BlockSpec((1, tokens, places.shape[2]), lambda i: (first + i, 0, 0)),
        ],
        out_specs=pl.BlockSpec((1, tokens, width), lambda i: (i, 0, 0)),
        out_shape=jax.ShapeDtypeStruct((size, tokens, width), BF16),
        cost_estimate=lasting(4.4),
        compiler_params=params(32),
    )(source, places)


def pack_experts(gate, up, down):
    count, shallow, width = down.shape
    inner = gate.shape[2]
    turned = down.reshape(count, shallow, width // inner, inner).transpose(0, 2, 1, 3)
    return jnp.concatenate(
        [gate, up, turned.reshape(count, shallow * width // inner, inner)], axis=1
    )


def slot_codes(picks, valid, capacity):
    rows = picks.shape[0]
    ids = jnp.arange(EXPERTS, dtype=jnp.int32)
    named = jnp.any(picks[:, :, None] == ids[None, None, :], axis=1)
    counted = (named & valid[:, None]).astype(BF16)
    before = (
        lax.broadcasted_iota(jnp.int32, (rows, rows), 1)
        < lax.broadcasted_iota(jnp.int32, (rows, rows), 0)
    ).astype(BF16)
    ranks = dot(before, counted)
    kept = (counted > 0) & (ranks < capacity[None, :].astype(F32))
    return jnp.where(kept, ranks, jnp.where(named, -1.0, -2.0))


def shards(
    layer_input,
    cotangent,
    lengths,
    routes,
    capacity,
    w_query,
    key_weight,
    value_weight,
    w_output,
    w_router,
    gain_attn,
    gain_moe,
    w_gate,
    w_up,
    w_down,
):
    micro_count, tokens, width = layer_input.shape[1:]
    dp_count, owner_count = lax.axis_size("dp"), lax.axis_size("expert")
    dp_index, owner_index = lax.axis_index("dp"), lax.axis_index("expert")
    slots = tokens // 4
    owned = w_gate.shape[0]
    key_width = key_weight.shape[1]
    dp_bits = dp_count.bit_length() - 1
    owner_bits = owner_count.bit_length() - 1
    split = 2 if owned % 2 == 0 and dp_bits > 1 else 1
    local = owned // split
    pair_bit = 1 if dp_bits > 1 else 0
    dp_places = [("dp", pair_bit)] + [
        ("dp", bit) for bit in reversed(range(dp_bits)) if bit != pair_bit
    ]
    row_places = [("expert", bit) for bit in range(1, owner_bits)]
    key_places = row_places + [("expert", 0)]
    if split == 2:
        token_places = [
            row_places + [("dp", pair_bit), ("expert", 0)],
            [("dp", pair_bit)] + row_places + [("expert", 0)],
        ]
    else:
        token_places = [key_places, key_places]
    half = (dp_index >> pair_bit) & 1 if split == 2 else 0
    first_expert = owner_index * owned + half * local

    rows_owned = w_query.shape[0]

    def dense_gather(parts):
        taken = sum(part.shape[1] for part in parts)
        pad = jnp.zeros((rows_owned, -taken % LANES), BF16)
        packed = jnp.concatenate(parts + [pad], axis=1)
        return lax.all_gather(packed, AXES, axis=0, tiled=True)

    dense_one = dense_gather([w_query, key_weight, value_weight, gain_attn[:, None]])

    def packed_half(which):
        return pack_experts(
            *[
                lax.dynamic_slice_in_dim(weight, which * local, local, 0)
                for weight in (w_gate, w_up, w_down)
            ]
        )

    mine_packed = packed_half(half)
    other_packed = packed_half(1 - half) if split == 2 else mine_packed
    weight_masks = [mask["dp"] for mask in masks_of(dp_places)]
    start_row = owner_index * tokens
    places = start_row + jnp.arange(tokens, dtype=jnp.int32)
    freqs = rope_base ** (-jnp.arange(0, HEAD_DIMENSION, 2, dtype=F32) / HEAD_DIMENSION)
    angles = places.astype(F32)[:, None] * freqs[None, :]
    cos_half, sin_half = jnp.cos(angles), jnp.sin(angles)
    cos = jnp.tile(cos_half, (1, LANES // HALF_HEAD))
    sin = jnp.tile(jnp.concatenate([-sin_half, sin_half], axis=1), (1, LANES // HEAD_DIMENSION))
    cos_t, sin_t = cos_half.T, sin_half.T
    key_starts = jnp.stack(
        [(owner_index ^ mask["expert"]) * tokens for mask in masks_of(key_places)]
    )
    codes, attend_places, dys, dy_rows = [], [], [], []
    for index in range(micro_count):
        length = lengths[0, index]
        valid = places < length
        code = slot_codes(routes[0, index], valid, capacity)
        code = jnp.concatenate([code, jnp.full((tokens, LANES - EXPERTS), -2.0, F32)], axis=1)
        codes.append(code)
        attend_places.append(
            jnp.concatenate([jnp.stack([start_row, length]), key_starts]).astype(jnp.int32)
        )
        dy = jnp.where(valid[:, None], cotangent[0, index], 0)
        dys.append(dy)
        dy_rows.append(jnp.concatenate([dy, code.astype(BF16)], axis=1))

    rows_here = jnp.stack(dy_rows)[None]
    direct = [
        swap(other_packed if stage == 0 else mine_packed, place)
        for stage, place in enumerate(dp_places)
    ]
    dy_received = swap(rows_here, token_places[0][0])
    dense_one, dy_received, *direct = after(dense_one, dy_received, *direct)
    rows_here = jnp.concatenate([rows_here, dy_received], axis=0)

    weight_pieces = [mine_packed, direct[0]]
    for stage, place in enumerate(dp_places[1:], 1):
        received = [direct[stage]]
        for piece in weight_pieces[1:]:
            if len(received) > 1:
                piece, received[-1] = after(piece, received[-1])
            received.append(swap(piece, place))
        weight_pieces = weight_pieces + received
    levels = [index.bit_count() for index in range(len(weight_pieces))]

    def weights_here(value, indices):
        value, *pieces = after(value, *[weight_pieces[index] for index in indices])
        for index, piece in zip(indices, pieces):
            weight_pieces[index] = piece
        return value

    output_rows, dense_one = after(w_output, dense_one)
    dense_two = dense_gather([output_rows, w_router, gain_moe[:, None]])
    for place in token_places[0][1:-1]:
        rows_here = jnp.concatenate([rows_here, swap(rows_here, place)], axis=0)

    gain_one = dense_one[:, width + 2 * key_width].astype(F32)[None]
    gain_two = dense_two[:, width + EXPERTS].astype(F32)[None]
    x = layer_input[0]
    normed, queries, keys_values = project(x, gain_one, dense_one, cos, sin)
    key_rows, attended, log_totals, middles, normed_two, gates = [], [], [], [], [], []
    row_halves = []
    for index in range(micro_count):
        halves = gather_rows(keys_values[index], key_places)
        key_rows.append(jnp.concatenate(halves, axis=0).reshape(-1, 2 * key_width))
    for index in range(micro_count):
        if index == 1:
            attend_places[index], rows_here = after(attend_places[index], rows_here)
            rows_there = swap(rows_here, token_places[0][-1])
        rows, lse = attend(attend_places[index], queries[index], key_rows[index])
        attended.append(rows)
        log_totals.append(lse)
        if index == 1:
            gain_two = weights_here(
                gain_two,
                [
                    i for i, level in enumerate(levels)
                    if level == 2 and i > len(levels) // 2
                ][:1],
            )
        middle, normed_rows, gate = middle_rows(x[index], rows, dense_two, gain_two, codes[index])
        middles.append(middle)
        normed_two.append(normed_rows)
        gates.append(gate)
        row_halves += gather_rows(normed_rows, token_places[index])
    row_all = jnp.concatenate(row_halves, axis=0)
    block_count = row_all.shape[0]
    per_micro = block_count // micro_count

    dy_blocks = []
    for index in range(micro_count):
        order = [token_places[0].index(place) for place in token_places[index]]
        for piece in range(per_micro):
            source = sum((piece >> stage & 1) << order[stage] for stage in range(len(order)))
            side = rows_here if source < per_micro // 2 else rows_there
            dy_blocks.append(side[source % (per_micro // 2), index])
    dy_all = jnp.stack(dy_blocks)
    code_all = dy_all[:, :, width : width + EXPERTS].astype(F32).transpose(2, 0, 1)
    code_all = jnp.roll(code_all.reshape(EXPERTS, block_count * tokens), -first_expert, axis=0)
    rank_table = code_all[:8].astype(jnp.int32)

    router_t = jnp.roll(dense_two[:, width : width + EXPERTS].T, -first_expert, axis=0)
    router_t = weights_here(router_t, [i for i, level in enumerate(levels) if level == 2])
    logits = dot_cols(router_t, row_all.reshape(block_count * tokens, width))
    chosen = code_all > -1.5
    peak = jnp.max(jnp.where(chosen, logits, masked_score), axis=0, keepdims=True)
    raised = jnp.where(chosen, jnp.exp(jnp.where(chosen, logits, peak) - peak), 0.0)
    gate_table = (raised / jnp.sum(raised, axis=0, keepdims=True))[:8]
    me = jnp.stack([dp_index, first_expert]).astype(jnp.int32)
    held = None
    trips = []
    for expert in range(local):
        if 2 <= expert <= 4:
            me = arrive(me, *[trips[0], trips[0], trips[1]][expert - 2 : expert - 1])
            if expert == 4:
                me = arrive(me, trips[0])
        outs = run_expert(
            expert, me, weight_pieces, weight_masks, row_all, dy_all, rank_table,
            gate_table, slots, local, held,
        )
        held = outs[:2]
        trips.append(Trip(list(outs[2:]), dp_places, split))
    eg_all, db_all = held

    slot_place = rank_table[:local]
    slot_place = jnp.where(
        slot_place >= 0, slot_place + slots * jnp.arange(local, dtype=jnp.int32)[:, None], -1
    )
    slot_place = jnp.concatenate(
        [slot_place, jnp.full((8 - local, block_count * tokens), -1, jnp.int32)], axis=0
    )
    slot_place = slot_place.reshape(8, block_count, tokens).transpose(1, 2, 0)

    def first_trade(source, places):
        found = []
        for index in range(micro_count):
            first, size = index * per_micro, per_micro // 2
            high = combine(source, places, first + size, size)
            received = swap(high, token_places[index][-1])
            low = combine(source, places, first, size)
            half_size = size // 2
            found.append(
                [
                    add_rounded(low[:half_size], received[:half_size]),
                    add_rounded(low[half_size:], received[half_size:]),
                ]
            )
        return found

    slot_place = arrive(slot_place, trips[1])
    sums = first_trade(db_all, slot_place)
    sums[1][1] = arrive(sums[1][1], trips[2], trips[1], trips[0])
    received = [
        swap(sums[index][1], token_places[index][-2]) for index in range(micro_count)
    ]
    mix_place, *lows = after(slot_place, *[pair[0] for pair in sums])
    mixed = first_trade(eg_all, mix_place)
    flat, shape = jax.tree.flatten((received, mixed))
    received, mixed = jax.tree.unflatten(shape, lax.optimization_barrier(tuple(flat)))
    row_grads = []
    lows[0] = arrive(lows[0], trips[2])
    for index in range(micro_count):
        total = add_rounded(lows[index], received[index])
        row_grads.append(sum_home(total[:1], total[1:], token_places[index][:1])[0])
    back_gain = arrive(gain_two, trips[3], trips[2], trips[1])

    router_grads, middle_grads, branch_grads, head_grads, gain_two_grads = [], [], [], [], []
    for index in range(micro_count):
        dz, dy1, branch, head_grad, gain_grad = middle_back(
            row_grads[index], middles[index], dys[index], gates[index], back_gain, dense_two
        )
        router_grads.append(dz)
        middle_grads.append(dy1)
        branch_grads.append(branch)
        head_grads.append(head_grad)
        gain_two_grads.append(gain_grad)

    def tall(parts):
        return jnp.concatenate(parts, axis=0)

    def to_owner(grads):
        return lax.psum_scatter(grads, AXES, scatter_dimension=0, tiled=True).astype(F32)

    gain_two_grads[0] = arrive(gain_two_grads[0], trips[3])
    early = weight_grads(
        [tall(attended), tall(normed_two)],
        [tall(branch_grads), tall(router_grads)],
        sum(gain_two_grads),
        width + LANES,
    )
    output_grads = to_owner(early)
    head_grads[0], early = after(head_grads[0], early)

    query_grads, pair_grads = [], []
    for index in range(micro_count):
        if index == micro_count - 1:
            attend_places[index], query_grads[0] = after(attend_places[index], query_grads[0])
            attend_places[index] = arrive(attend_places[index], trips[4], trips[3], trips[2])
        dq, pairs = attend_back(
            attend_places[index], queries[index], key_rows[index], head_grads[index],
            attended[index], log_totals[index], cos_t, sin_t,
        )
        pairs = pairs.reshape(owner_count, tokens, pairs.shape[1])
        middle_point = owner_count // 2
        pair_grads.append(sum_home(pairs[:middle_point], pairs[middle_point:], key_places)[0])
        query_grads.append(dq)
    normed_all = normed.reshape(micro_count * tokens, width)

    query_grads[-1], *highs = after(query_grads[-1], *[pair[1] for pair in mixed])
    last_gain = arrive(gain_one, trips[4])
    mix_received = [
        swap(highs[index], token_places[index][-2]) for index in range(micro_count)
    ]
    key_grads, input_grads, gain_one_grads = [], [], []
    for index in range(micro_count):
        dx, dkv, gain_grad = project_back(
            query_grads[index], pair_grads[index], x[index], middle_grads[index], last_gain,
            dense_one, cos, sin,
        )
        input_grads.append(dx)
        key_grads.append(dkv)
        gain_one_grads.append(gain_grad)
    gain_one_grad = arrive(sum(gain_one_grads), trips[4], trips[3])
    gain_one_grad, output_grads, *mix_received = after(gain_one_grad, output_grads, *mix_received)
    late = weight_grads(
        [normed_all, normed_all],
        [tall(query_grads), tall(key_grads)],
        gain_one_grad,
        width + 2 * key_width + LANES,
    )
    late_grads = to_owner(late)
    mix_received[0], late = after(mix_received[0], late)
    mixtures = []
    for index in range(micro_count):
        total = add_rounded(mixed[index][0], mix_received[index])
        mixtures.append(sum_home(total[:1], total[1:], token_places[index][:1])[0])
    layer_output = jnp.stack(
        [
            (middles[index] + mixtures[index].astype(F32)).astype(BF16)
            for index in range(micro_count)
        ]
    )[None]
    for trip in trips:
        while trip.mine is None:
            trip.step(trip.waiting.pop(0))

    mine = jnp.stack([trip.mine for trip in trips])
    if split == 2:
        other = jnp.stack([trip.other for trip in trips])
        lower = half == 0
        mine = jnp.concatenate(
            [jnp.where(lower, mine, other), jnp.where(lower, other, mine)], axis=0
        )
    deep = w_gate.shape[1]
    inner = w_gate.shape[2]
    grad_gate = mine[:, :deep]
    grad_up = mine[:, deep : 2 * deep]
    grad_down = (
        mine[:, 2 * deep :]
        .reshape(owned, width // inner, w_down.shape[1], inner)
        .transpose(0, 2, 1, 3)
        .reshape(w_down.shape)
    )
    return (
        layer_output,
        jnp.stack(input_grads)[None],
        late_grads[:, :width],
        late_grads[:, width : width + key_width],
        late_grads[:, width + key_width : width + 2 * key_width],
        output_grads[:, :width],
        output_grads[:, width : width + EXPERTS],
        late_grads[:, width + 2 * key_width + EXPERTS],
        output_grads[:, width + EXPERTS],
        grad_gate,
        grad_up,
        grad_down,
    )


def solution(mesh):
    return jax.shard_map(
        shards,
        mesh=mesh,
        in_specs=(
            P("dp", None, "expert", None),
            P("dp", None, "expert", None),
            P("dp", None),
            P("dp", None, "expert", None),
            P(),
            P(("dp", "expert"), None),
            P(("dp", "expert"), None),
            P(("dp", "expert"), None),
            P(("dp", "expert"), None),
            P(("dp", "expert"), None),
            P(("dp", "expert")),
            P(("dp", "expert")),
            P("expert", "dp", None),
            P("expert", "dp", None),
            P("expert", "dp", None),
        ),
        out_specs=(
            P("dp", None, "expert", None),
            P("dp", None, "expert", None),
            P(("dp", "expert"), None),
            P(("dp", "expert"), None),
            P(("dp", "expert"), None),
            P(("dp", "expert"), None),
            P(("dp", "expert"), None),
            P(("dp", "expert")),
            P(("dp", "expert")),
            P("expert", "dp", None),
            P("expert", "dp", None),
            P("expert", "dp", None),
        ),
        check_vma=False,
    )
```

time: 3640 us -> 1330 us (0.37)
  waiting for transfers between devices: 2090 us -> 657 us
  matrix products: 578 us -> 9.04 us
  blocking collectives: 484 us -> 0 us
  Pallas kernels: 0 us -> 338 us
  local copies, waits for them, and re-layouts: 293 us -> 127 us
    reduce_scatter x11 -> x2, waiting for transfers between devices: 1180 us -> 91.9 us  [to_owner(): lax.psum_scatter(grads, AXES, scatter_dimension=0, tiled=True).astype(F32)]
    all_gather x11 -> x2, waiting for transfers between devices: 660 us -> 37.8 us  [dense_gather(): return lax.all_gather(packed, AXES, axis=0, tiled=True)]
    dot_general x164 -> x3, matrix products: 578 us -> 9.04 us  [the longest x1 8.51 us: dot_cols(): lax.dot_general(left, right, (((1,), (1,)), ((), ())), preferred_element_...]
    ppermute x0 -> x58, waiting for transfers between devices: none -> 528 us  [swap(): lax.ppermute(array, AXES, [(i, i ^ flip) for i in range(dp_count * owner_...]
    pallas_call x0 -> x26, Pallas kernels: none -> 338 us  [the longest x5 158 us: run_expert(): pl.pallas_call(functools.partial(expert_kernel, masks, stage_sizes, exper...]
    all_to_all x3 -> x0, blocking collectives: 278 us -> none  [the longest x2 186 us: shards(): lax.all_to_all(send_rows, 'expert', split_axis=0, concat_axis=0, tiled=True)]
    all_to_all x5 -> x0, waiting for transfers between devices: 235 us -> none  [the longest x2 119 us: shards(): lax.all_to_all(grad_rows, 'expert', split_axis=0, concat_axis=0, tiled=True)]
    all_gather x1 -> x0, blocking collectives: 118 us -> none  [shards(): full_router = lax.all_gather(w_router, ('dp', 'expert'), axis=0, tiled=True)]
  transfers between devices with their start and end apart: 28 -> 62, of which waited for: 21 -> 24; matrix products, arithmetic and copies ran while one was open for 15% -> 17% of each run, Pallas kernels for 0% -> 20%
where the time goes in v1:
time: 1330 us; the launch traced here: 1320 us
  waiting for transfers between devices  657 us (49%)
  Pallas kernels  338 us (25%)
  local copies, waits for them, and re-layouts  127 us (10%)
  other arithmetic  116 us (9%)
  starting transfers between devices  57.1 us (4%)
  between operations  15.5 us (1%)
    ppermute x58, waiting for transfers between devices, swap(): lax.ppermute(array, AXES, [(i, i ^ flip) for i in range(dp_count * owner_...  528 us
    pallas_call x5, Pallas kernels, run_expert(): pl.pallas_call(functools.partial(expert_kernel, masks, stage_sizes, exper...  158 us
    reduce_scatter x2, waiting for transfers between devices, to_owner(): lax.psum_scatter(grads, AXES, scatter_dimension=0, tiled=True).astype(F32)  91.9 us
    unnamed x229, local copies, waits for them, and re-layouts  75.3 us
    ppermute x58, starting transfers between devices, swap(): lax.ppermute(array, AXES, [(i, i ^ flip) for i in range(dp_count * owner_...  56.6 us
    pallas_call x2, Pallas kernels, attend_back(): pl.pallas_call(attend_back_kernel, grid_spec=pltpu.PrefetchScalarGridSpec...  46.9 us
    convert_element_type x20, other arithmetic, add_rounded(): return (left.astype(F32) + right.astype(F32)).astype(left.dtype)  45.4 us
    pallas_call x2, Pallas kernels, attend(): pl.pallas_call(attend_kernel, grid_spec=pltpu.PrefetchScalarGridSpec(num_...  37.9 us
  transfers between devices with their start and end apart: 62, of which 24 were waited for; matrix products, arithmetic and copies ran while one was open for 17% of the time, Pallas kernels for 20%

profile of v1, /device:TPU:0, one launch (start us, length us, event | category | flops | bytes accessed | tf_op | source)
XLA Modules:
  0.0 1319.9 jit_solution(15189454921635425816)
XLA Ops:
  37.1 36.6 %collective-permute-done = bf16[1,2,256,1664]{3,2,1,0:T(8,128)(2,1)} collective-permute-done((bf16[1,2,256,1664]{3,2,1,0:T(8,128)(2,1)S(1)}, bf16[1,2,256,1664]{3,2,1,0:T(8,128)(2,1)}, u32[]{:S(2)}, u32[]{:S(2)}) %collective-permute-start) | collective-permute-done | bytes 1703968 | tf_op jit(solution)/shard_map/ppermute | solution.py:66
  73.8 95.2 %collective-permute-done.1.refs_1_ = bf16[5,576,512]{2,1,0:T(8,128)(2,1)} collective-permute-done((bf16[5,576,512]{2,1,0:T(8,128)(2,1)}, bf16[5,576,512]{2,1,0:T(8,128)(2,1)}, u32[]{:S(2)}, u32[]{:S(2)}) %collective-permute-start.1) | collective-permute-done | bytes 2949152 | tf_op jit(solution)/shard_map/ppermute | solution.py:66
  169.0 37.8 %all-gather.3.cloned.1.call-done.w_ref = bf16[1536,2688]{1,0:T(8,128)(2,1)} async-done(((bf16[48,2688]{1,0:T(8,128)(2,1)}), bf16[1536,2688]{1,0:T(8,128)(2,1)}) %all-gather.3.cloned.1.call-update) | async-done | bytes 8257552 | tf_op jit(solution)/shard_map/all_gather | solution.py:808
  215.9 8.1 shard_map.238
  230.0 10.0 collective-permute-done.4
  245.8 13.0 collective-permute-done.15
  260.4 92.2 %collective-permute-done.14 = bf16[2,2,256,1664]{3,2,1,0:T(8,128)(2,1)} collective-permute-done((bf16[2,2,256,1664]{3,2,1,0:T(8,128)(2,1)}, bf16[2,2,256,1664]{3,2,1,0:T(8,128)(2,1)}, u32[]{:S(2)}, u32[]{:S(2)}) %collective-permute-start.14) | collective-permute-done | bytes 3407904 | tf_op jit(solution)/shard_map/ppermute | solution.py:66
  352.6 5.8 pad_maximum_fusion
  358.5 18.7 %shard_map.239 = (bf16[256,1536]{1,0:T(8,128)(2,1)S(1)}, f32[4,8,256]{2,1,0:T(8,128)S(1)}) custom-call(s32[6]{0:T(128)S(1)} %concatenate.89.places_ref, bf16[256,1536]{1,0:T(8,128)(2,1)S(1)} %get-tuple-element.350.q_ref, bf16[1024,1024]{1,0:T(8,128)(2,1)S(1)} %bitcast.189, bf16[1024,1024]{1,0:T(8,128)(2,1)S(1)} %bitcast.190), custom_call_target="tpu_custom_call" | custom-call | flops 20899999744 | tf_op jit(solution)/shard_map/pallas_call | solution.py:426
  388.0 19.2 %shard_map.241 = (bf16[256,1536]{1,0:T(8,128)(2,1)S(1)}, f32[4,8,256]{2,1,0:T(8,128)S(1)}) custom-call(s32[6]{0:T(128)S(1)} %concatenate.101.places_ref, bf16[256,1536]{1,0:T(8,128)(2,1)S(1)} %get-tuple-element.351.q_ref, bf16[1024,1024]{1,0:T(8,128)(2,1)S(1)} %bitcast.185, bf16[1024,1024]{1,0:T(8,128)(2,1)S(1)} %bitcast.186), custom_call_target="tpu_custom_call" | custom-call | flops 20899999744 | tf_op jit(solution)/shard_map/pallas_call | solution.py:426
  407.8 36.5 %collective-permute-done.8.refs_6_ = bf16[5,576,512]{2,1,0:T(8,128)(2,1)} collective-permute-done((bf16[5,576,512]{2,1,0:T(8,128)(2,1)}, bf16[5,576,512]{2,1,0:T(8,128)(2,1)}, u32[]{:S(2)}, u32[]{:S(2)}) %collective-permute-start.8) | collective-permute-done | bytes 2949152 | tf_op jit(solution)/shard_map/ppermute | solution.py:66
  447.4 4.4 shard_map.240
  484.4 21.5 %collective-permute-done.12 = bf16[256,1536]{1,0:T(8,128)(2,1)S(1)} collective-permute-done((bf16[256,1536]{1,0:T(8,128)(2,1)S(1)}, bf16[256,1536]{1,0:T(8,128)(2,1)S(1)}, u32[]{:S(2)}, u32[]{:S(2)}) %collective-permute-start.12) | collective-permute-done | bytes 786464 | tf_op jit(solution)/shard_map/ppermute | solution.py:66
  521.7 10.5 collective-permute-done.19
  547.9 8.5 select_reduce_fusion
  557.9 31.3 %shard_map.243 = (bf16[16,5,64,1536]{3,2,1,0:T(8,128)(2,1)}, bf16[16,5,64,1664]{3,2,1,0:T(8,128)(2,1)}, bf16[1,576,512]{2,1,0:T(8,128)(2,1)}, bf16[1,576,512]{2,...) custom-call(s32[2]{0:T(128)} %pad_add_fusion.me_ref, ...), custom_call_target="tpu_custom_call" | custom-call | flops 34100000768 | tf_op jit(solution)/shard_map/pallas_call | solution.py:674
  591.3 31.7 %shard_map.244 = (bf16[16,5,64,1536]{3,2,1,0:T(8,128)(2,1)}, bf16[16,5,64,1664]{3,2,1,0:T(8,128)(2,1)}, bf16[1,576,512]{2,1,0:T(8,128)(2,1)}, bf16[1,576,512]{2,...) custom-call(s32[2]{0:T(128)} %pad_add_fusion.me_ref, ...), custom_call_target="tpu_custom_call", output_to_operand_aliasing={{0}: (13, {}), {1}: (14, {})} | custom-call | flops 34100000768 | tf_op jit(solution)/shard_map/pallas_call | solution.py:674
  629.0 14.7 %collective-permute-done.23 = bf16[2,576,512]{2,1,0:T(8,128)(2,1)} collective-permute-done((bf16[2,576,512]{2,1,0:T(8,128)(2,1)}, bf16[2,576,512]{2,1,0:T(8,128)(2,1)}, u32[]{:S(2)}, u32[]{:S(2)}) %collective-permute-start.23) | collective-permute-done | bytes 1179680 | tf_op jit(solution)/shard_map/ppermute | solution.py:66
  647.5 31.6 %shard_map.245 = (bf16[16,5,64,1536]{3,2,1,0:T(8,128)(2,1)}, bf16[16,5,64,1664]{3,2,1,0:T(8,128)(2,1)}, bf16[1,576,512]{2,1,0:T(8,128)(2,1)}, bf16[1,576,512]{2,...) custom-call(s32[2]{0:T(128)} %pad_add_fusion.me_ref, ...), custom_call_target="tpu_custom_call", output_to_operand_aliasing={{0}: (13, {}), {1}: (14, {})} | custom-call | flops 34100000768 | tf_op jit(solution)/shard_map/pallas_call | solution.py:674
  679.2 31.8 %shard_map.246 = (bf16[16,5,64,1536]{3,2,1,0:T(8,128)(2,1)}, bf16[16,5,64,1664]{3,2,1,0:T(8,128)(2,1)}, bf16[1,576,512]{2,1,0:T(8,128)(2,1)}, bf16[1,576,512]{2,...) custom-call(s32[2]{0:T(128)} %pad_add_fusion.me_ref, ...), custom_call_target="tpu_custom_call", output_to_operand_aliasing={{0}: (13, {}), {1}: (14, {})} | custom-call | flops 34100000768 | tf_op jit(solution)/shard_map/pallas_call | solution.py:674
  711.0 31.5 %shard_map.247 = (bf16[16,5,64,1536]{3,2,1,0:T(8,128)(2,1)}, bf16[16,5,64,1664]{3,2,1,0:T(8,128)(2,1)}, bf16[1,576,512]{2,1,0:T(8,128)(2,1)}, bf16[1,576,512]{2,...) custom-call(s32[2]{0:T(128)} %pad_add_fusion.me_ref, ...), custom_call_target="tpu_custom_call", output_to_operand_aliasing={{0}: (13, {}), {1}: (14, {})} | custom-call | flops 34100000768 | tf_op jit(solution)/shard_map/pallas_call | solution.py:674
  742.6 5.8 copy-done
  748.4 4.5 shard_map.249
  771.1 4.5 add_convert_fusion.3
  779.6 5.5 copy-done.1
  796.2 19.4 %collective-permute-done.31 = bf16[2,576,512]{2,1,0:T(8,128)(2,1)} collective-permute-done((bf16[2,576,512]{2,1,0:T(8,128)(2,1)}, bf16[2,576,512]{2,1,0:T(8,128)(2,1)}, u32[]{:S(2)}, u32[]{:S(2)}) %collective-permute-start.31) | collective-permute-done | bytes 1179680 | tf_op jit(solution)/shard_map/ppermute | solution.py:66
  817.8 10.3 collective-permute-done.32
  843.2 18.0 %collective-permute-done.38 = bf16[2,576,512]{2,1,0:T(8,128)(2,1)S(1)} collective-permute-done((bf16[2,576,512]{2,1,0:T(8,128)(2,1)S(1)}, bf16[2,576,512]{2,1,0:T(8,128)(2,1)S(1)}, u32[]{:S(2)}, u32[]{:S(2)}) %collective-permute-start.38) | collective-permute-done | bytes 1179680 | tf_op jit(solution)/shard_map/ppermute | solution.py:66
  863.0 9.2 collective-permute-done.40
  877.4 8.7 collective-permute-done.39
  897.6 50.2 %collective-permute-done.28 = bf16[2,256,1664]{2,1,0:T(8,128)(2,1)} collective-permute-done((bf16[2,256,1664]{2,1,0:T(8,128)(2,1)}, bf16[2,256,1664]{2,1,0:T(8,128)(2,1)}, u32[]{:S(2)}, u32[]{:S(2)}) %collective-permute-start.28) | collective-permute-done | bytes 1703968 | tf_op jit(solution)/shard_map/ppermute | solution.py:66
  955.5 15.2 %collective-permute-done.37 = bf16[1,256,1664]{2,1,0:T(8,128)(2,1)S(1)} collective-permute-done((bf16[1,256,1664]{2,1,0:T(8,128)(2,1)S(1)}, bf16[1,256,1664]{2,1,0:T(8,128)(2,1)S(1)}, u32[]{:S(2)}, u32[]{:S(2)}) %collective-permute-start.37) | collective-permute-done | bytes 852000 | tf_op jit(solution)/shard_map/ppermute | solution.py:66
  971.8 6.6 shard_map.256
  978.4 12.3 collective-permute-done.41
  991.9 6.6 shard_map.257
  1002.2 7.7 shard_map.258
  1010.0 23.3 %shard_map.259 = (bf16[256,1536]{1,0:T(8,128)(2,1)}, bf16[1024,1024]{1,0:T(8,128)(2,1)}) custom-call(s32[6]{0:T(128)} %copy-done.24, bf16[256,1536]{1,0:T(8,128)(2,1)} %copy-done.16, bf16[1024,1024]{1,0:T(8,128)(2,1)} %bitcast.191, bf16[1024,1024]{1,0:T(8,128)(2,1)} %bitcast.192, bf16[256,1536]{1,0:T(8,128)(2,1)} %get-tuple-element.231.do_ref, ...), custom_call_target="tpu_custom_call" | custom-call | flops 25849999360 | tf_op jit(solution)/shard_map/pallas_call | solution.py:504
  1035.6 23.6 %shard_map.261 = (bf16[256,1536]{1,0:T(8,128)(2,1)}, bf16[1024,1024]{1,0:T(8,128)(2,1)}) custom-call(s32[6]{0:T(128)} %copy-done.23, bf16[256,1536]{1,0:T(8,128)(2,1)} %copy-done.15, bf16[1024,1024]{1,0:T(8,128)(2,1)} %bitcast.187, bf16[1024,1024]{1,0:T(8,128)(2,1)} %bitcast.188, bf16[256,1536]{1,0:T(8,128)(2,1)} %get-tuple-element.248.do_ref, ...), custom_call_target="tpu_custom_call" | custom-call | flops 25849999360 | tf_op jit(solution)/shard_map/pallas_call | solution.py:504
  1074.1 10.6 collective-permute-done.44
  1088.2 8.1 shard_map.260
  1096.4 31.7 %collective-permute-done.50 = bf16[1,256,1024]{2,1,0:T(8,128)(2,1)} collective-permute-done((bf16[1,256,1024]{2,1,0:T(8,128)(2,1)}, bf16[1,256,1024]{2,1,0:T(8,128)(2,1)}, u32[]{:S(2)}, u32[]{:S(2)}) %collective-permute-start.50) | collective-permute-done | bytes 524320 | tf_op jit(solution)/shard_map/ppermute | solution.py:66
  1130.3 8.5 shard_map.262
  1143.3 24.1 %reduce-scatter.3.cloned.1.call-done = bf16[48,1664]{1,0:T(8,128)(2,1)} async-done(((bf16[1536,1664]{1,0:T(8,128)(2,1)}), bf16[48,1664]{1,0:T(8,128)(2,1)}) %reduce-scatter.3.cloned.1.call-update) | async-done | bytes 159760 | tf_op jit(solution)/shard_map/reduce_scatter | solution.py:1003
  1168.3 10.4 shard_map.263
  1196.2 7.7 collective-permute-done.57
  1221.1 5.0 copy.99
  1226.1 7.8 reshape.185
  1240.4 67.8 %reduce-scatter.5.cloned.1.call-done = bf16[48,2688]{1,0:T(8,128)(2,1)} async-done(((bf16[1536,2688]{1,0:T(8,128)(2,1)}), bf16[48,2688]{1,0:T(8,128)(2,1)}) %reduce-scatter.5.cloned.1.call-update) | async-done | bytes 258064 | tf_op jit(solution)/shard_map/reduce_scatter | solution.py:1003
  (466 shorter events, 300.4 us)
Async XLA Ops:
  7.2 199.7 %all-gather.3.cloned.1.call-start = ((), (), s32[]{:S(2)}) async-start(), calls=%async_computation.2 | async-start | bytes 8515584 | tf_op jit(solution)/shard_map/all_gather | solution.py:808
  9.7 436.3 %all-gather.5.cloned.1.call-start = ((), (), s32[]{:S(2)}) async-start(), calls=%async_computation.3 | async-start | bytes 5271552 | tf_op jit(solution)/shard_map/all_gather | solution.py:808
  18.5 150.5 %collective-permute-start.2 = (bf16[5,576,512]{2,1,0:T(8,128)(2,1)}, bf16[5,576,512]{2,1,0:T(8,128)(2,1)}, u32[]{:S(2)}, u32[]{:S(2)}) collective-permute-start(bf16[5,576,512]{2,1,0:T(8,128)(2,1)} %pad_maximum_fusion.6.refs_0_), channel_id=1, source_target_pairs={{0,16},{1,17},{2,18},{3,19},{4,20},{5,21},{6,22},{7,23},{8,24},{9,... | collective-permute-start | bytes 8847368 | tf_op jit(solution)/shard_map/ppermute | solution.py:66
  22.5 146.5 %collective-permute-start.3 = (bf16[5,576,512]{2,1,0:T(8,128)(2,1)}, bf16[5,576,512]{2,1,0:T(8,128)(2,1)}, u32[]{:S(2)}, u32[]{:S(2)}) collective-permute-start(bf16[5,576,512]{2,1,0:T(8,128)(2,1)} %pad_maximum_fusion.6.refs_0_), channel_id=1, source_target_pairs={{0,4},{1,5},{2,6},{3,7},{4,0},{5,1},{6,2},{7,3},{8,12},{9,13},{10,... | collective-permute-start | bytes 8847368 | tf_op jit(solution)/shard_map/ppermute | solution.py:66
  27.8 141.2 %collective-permute-start.1 = (bf16[5,576,512]{2,1,0:T(8,128)(2,1)}, bf16[5,576,512]{2,1,0:T(8,128)(2,1)}, u32[]{:S(2)}, u32[]{:S(2)}) collective-permute-start(bf16[5,576,512]{2,1,0:T(8,128)(2,1)} %pad_maximum_fusion.5), channel_id=1, source_target_pairs={{0,8},{1,9},{2,10},{3,11},{4,12},{5,13},{6,14},{7,15},{8,0},{9,1},... | collective-permute-start | bytes 8847368 | tf_op jit(solution)/shard_map/ppermute | solution.py:66
  35.5 38.3 %collective-permute-start = (bf16[1,2,256,1664]{3,2,1,0:T(8,128)(2,1)S(1)}, bf16[1,2,256,1664]{3,2,1,0:T(8,128)(2,1)}, u32[]{:S(2)}, u32[]{:S(2)}) collective-permute-start(bf16[1,2,256,1664]{3,2,1,0:T(8,128)(2,1)S(1)} %maximum_bitcast_fusion.1), channel_id=1, source_target_pairs={{0,2},{1,3},{2,0},{3,1},{4,6},{5,7},{6,4},{7,5},{8,10},{9,11},{10,... | collective-permute-start | bytes 5111816 | tf_op jit(solution)/shard_map/ppermute | solution.py:66
  210.4 142.2 %collective-permute-start.14 = (bf16[2,2,256,1664]{3,2,1,0:T(8,128)(2,1)}, bf16[2,2,256,1664]{3,2,1,0:T(8,128)(2,1)}, u32[]{:S(2)}, u32[]{:S(2)}) collective-permute-start(bf16[2,2,256,1664]{3,2,1,0:T(8,128)(2,1)} %pad_maximum_fusion.2), channel_id=1, source_target_pairs={{0,8},{1,9},{2,10},{3,11},{4,12},{5,13},{6,14},{7,15},{8,0},{9,1},... | collective-permute-start | bytes 10223624 | tf_op jit(solution)/shard_map/ppermute | solution.py:66
  214.0 953.3 %reduce-scatter.3.cloned.1.call-start = ((), (), s32[]{:S(2)}) async-start(), calls=%async_computation.4 | async-start | bytes 5271552 | tf_op jit(solution)/shard_map/reduce_scatter | solution.py:1003
  242.7 134.7 %collective-permute-start.7 = (bf16[5,576,512]{2,1,0:T(8,128)(2,1)}, bf16[5,576,512]{2,1,0:T(8,128)(2,1)S(1)}, u32[]{:S(2)}, u32[]{:S(2)}) collective-permute-start(bf16[5,576,512]{2,1,0:T(8,128)(2,1)} %collective-permute-done.1.refs_1_), channel_id=1, source_target_pairs={{0,4},{1,5},{2,6},{3,7},{4,0},{5,1},{6,2},{7,3},{8,12},{9,13},{10,... | collective-permute-start | bytes 8847368 | tf_op jit(solution)/shard_map/ppermute | solution.py:66
  244.1 163.7 %collective-permute-start.6 = (bf16[5,576,512]{2,1,0:T(8,128)(2,1)}, bf16[5,576,512]{2,1,0:T(8,128)(2,1)}, u32[]{:S(2)}, u32[]{:S(2)}) collective-permute-start(bf16[5,576,512]{2,1,0:T(8,128)(2,1)} %collective-permute-done.1.refs_1_), channel_id=1, source_target_pairs={{0,16},{1,17},{2,18},{3,19},{4,20},{5,21},{6,22},{7,23},{8,24},{9,... | collective-permute-start | bytes 8847368 | tf_op jit(solution)/shard_map/ppermute | solution.py:66
  258.9 118.2 %collective-permute-start.16 = (bf16[2,256,1024]{2,1,0:T(8,128)(2,1)S(1)}, bf16[2,256,1024]{2,1,0:T(8,128)(2,1)S(1)}, u32[]{:S(2)}, u32[]{:S(2)}) collective-permute-start(bf16[2,256,1024]{2,1,0:T(8,128)(2,1)S(1)} %pad_maximum_fusion.14), channel_id=1, source_target_pairs={{0,1},{1,0},{2,3},{3,2},{4,5},{5,4},{6,7},{7,6},{8,9},{9,8},{10,11... | collective-permute-start | bytes 3145736 | tf_op jit(solution)/shard_map/ppermute | solution.py:66
  358.4 104.6 %collective-permute-start.21 = (bf16[4,2,256,1664]{3,2,1,0:T(8,128)(2,1)}, bf16[4,2,256,1664]{3,2,1,0:T(8,128)(2,1)}, u32[]{:S(2)}, u32[]{:S(2)}) collective-permute-start(bf16[4,2,256,1664]{3,2,1,0:T(8,128)(2,1)} %pad_maximum_fusion), channel_id=1, source_target_pairs={{0,1},{1,0},{2,3},{3,2},{4,5},{5,4},{6,7},{7,6},{8,9},{9,8},{10,11... | collective-permute-start | bytes 20447240 | tf_op jit(solution)/shard_map/ppermute | solution.py:66
  377.4 66.9 %collective-permute-start.8 = (bf16[5,576,512]{2,1,0:T(8,128)(2,1)}, bf16[5,576,512]{2,1,0:T(8,128)(2,1)}, u32[]{:S(2)}, u32[]{:S(2)}) collective-permute-start(bf16[5,576,512]{2,1,0:T(8,128)(2,1)} %collective-permute-done.2.refs_2_), channel_id=1, source_target_pairs={{0,4},{1,5},{2,6},{3,7},{4,0},{5,1},{6,2},{7,3},{8,12},{9,13},{10,... | collective-permute-start | bytes 8847368 | tf_op jit(solution)/shard_map/ppermute | solution.py:66
  444.3 113.6 %collective-permute-start.9 = (bf16[5,576,512]{2,1,0:T(8,128)(2,1)}, bf16[5,576,512]{2,1,0:T(8,128)(2,1)}, u32[]{:S(2)}, u32[]{:S(2)}) collective-permute-start(bf16[5,576,512]{2,1,0:T(8,128)(2,1)} %collective-permute-done.6.refs_3_), channel_id=1, source_target_pairs={{0,4},{1,5},{2,6},{3,7},{4,0},{5,1},{6,2},{7,3},{8,12},{9,13},{10,... | collective-permute-start | bytes 8847368 | tf_op jit(solution)/shard_map/ppermute | solution.py:66
  453.0 26.8 %collective-permute-start.10 = (bf16[256,1536]{1,0:T(8,128)(2,1)S(1)}, bf16[256,1536]{1,0:T(8,128)(2,1)S(1)}, u32[]{:S(2)}, u32[]{:S(2)}) collective-permute-start(bf16[256,1536]{1,0:T(8,128)(2,1)S(1)} %get-tuple-element.168), channel_id=1, source_target_pairs={{0,2},{1,3},{2,0},{3,1},{4,6},{5,7},{6,4},{7,5},{8,10},{9,11},{10,... | collective-permute-start | bytes 2359304 | tf_op jit(solution)/shard_map/ppermute | solution.py:66
  453.4 31.0 %collective-permute-start.11 = (bf16[256,1536]{1,0:T(8,128)(2,1)S(1)}, bf16[256,1536]{1,0:T(8,128)(2,1)S(1)}, u32[]{:S(2)}, u32[]{:S(2)}) collective-permute-start(bf16[256,1536]{1,0:T(8,128)(2,1)S(1)} %get-tuple-element.168), channel_id=1, source_target_pairs={{0,8},{1,9},{2,10},{3,11},{4,12},{5,13},{6,14},{7,15},{8,0},{9,1},... | collective-permute-start | bytes 2359304 | tf_op jit(solution)/shard_map/ppermute | solution.py:66
  460.0 52.2 %collective-permute-start.17 = (bf16[256,1536]{1,0:T(8,128)(2,1)S(1)}, bf16[256,1536]{1,0:T(8,128)(2,1)S(1)}, u32[]{:S(2)}, u32[]{:S(2)}) collective-permute-start(bf16[256,1536]{1,0:T(8,128)(2,1)S(1)} %get-tuple-element.173), channel_id=1, source_target_pairs={{0,8},{1,9},{2,10},{3,11},{4,12},{5,13},{6,14},{7,15},{8,0},{9,1},... | collective-permute-start | bytes 2359304 | tf_op jit(solution)/shard_map/ppermute | solution.py:66
  463.1 58.7 %collective-permute-start.18 = (bf16[256,1536]{1,0:T(8,128)(2,1)S(1)}, bf16[256,1536]{1,0:T(8,128)(2,1)}, u32[]{:S(2)}, u32[]{:S(2)}) collective-permute-start(bf16[256,1536]{1,0:T(8,128)(2,1)S(1)} %get-tuple-element.173), channel_id=1, source_target_pairs={{0,2},{1,3},{2,0},{3,1},{4,6},{5,7},{6,4},{7,5},{8,10},{9,11},{10,... | collective-permute-start | bytes 2359304 | tf_op jit(solution)/shard_map/ppermute | solution.py:66
  479.8 26.1 %collective-permute-start.12 = (bf16[256,1536]{1,0:T(8,128)(2,1)S(1)}, bf16[256,1536]{1,0:T(8,128)(2,1)S(1)}, u32[]{:S(2)}, u32[]{:S(2)}) collective-permute-start(bf16[256,1536]{1,0:T(8,128)(2,1)S(1)} %collective-permute-done.10), channel_id=1, source_target_pairs={{0,8},{1,9},{2,10},{3,11},{4,12},{5,13},{6,14},{7,15},{8,0},{9,1},... | collective-permute-start | bytes 2359304 | tf_op jit(solution)/shard_map/ppermute | solution.py:66
  507.8 28.3 %collective-permute-start.13 = (bf16[4,256,1536]{2,1,0:T(8,128)(2,1)}, bf16[4,256,1536]{2,1,0:T(8,128)(2,1)}, u32[]{:S(2)}, u32[]{:S(2)}) collective-permute-start(bf16[4,256,1536]{2,1,0:T(8,128)(2,1)} %pad_maximum_fusion.3), channel_id=1, source_target_pairs={{0,1},{1,0},{2,3},{3,2},{4,5},{5,4},{6,7},{7,6},{8,9},{9,8},{10,11... | collective-permute-start | bytes 9437192 | tf_op jit(solution)/shard_map/ppermute | solution.py:66
  589.2 39.7 %collective-permute-start.22 = (bf16[2,576,512]{2,1,0:T(8,128)(2,1)}, bf16[2,576,512]{2,1,0:T(8,128)(2,1)}, u32[]{:S(2)}, u32[]{:S(2)}) collective-permute-start(bf16[2,576,512]{2,1,0:T(8,128)(2,1)} %get-tuple-element.176), channel_id=1, source_target_pairs={{0,4},{1,5},{2,6},{3,7},{4,0},{5,1},{6,2},{7,3},{8,12},{9,13},{10,... | collective-permute-start | bytes 3538952 | tf_op jit(solution)/shard_map/ppermute | solution.py:66
  590.8 52.8 %collective-permute-start.23 = (bf16[2,576,512]{2,1,0:T(8,128)(2,1)}, bf16[2,576,512]{2,1,0:T(8,128)(2,1)}, u32[]{:S(2)}, u32[]{:S(2)}) collective-permute-start(bf16[2,576,512]{2,1,0:T(8,128)(2,1)} %get-tuple-element.178), channel_id=1, source_target_pairs={{0,4},{1,5},{2,6},{3,7},{4,0},{5,1},{6,2},{7,3},{8,12},{9,13},{10,... | collective-permute-start | bytes 3538952 | tf_op jit(solution)/shard_map/ppermute | solution.py:66
  623.1 87.9 %collective-permute-start.24 = (bf16[2,576,512]{2,1,0:T(8,128)(2,1)}, bf16[2,576,512]{2,1,0:T(8,128)(2,1)}, u32[]{:S(2)}, u32[]{:S(2)}) collective-permute-start(bf16[2,576,512]{2,1,0:T(8,128)(2,1)} %get-tuple-element.182), channel_id=1, source_target_pairs={{0,4},{1,5},{2,6},{3,7},{4,0},{5,1},{6,2},{7,3},{8,12},{9,13},{10,... | collective-permute-start | bytes 3538952 | tf_op jit(solution)/shard_map/ppermute | solution.py:66
  626.7 84.3 %collective-permute-start.26 = (bf16[2,576,512]{2,1,0:T(8,128)(2,1)}, bf16[2,576,512]{2,1,0:T(8,128)(2,1)}, u32[]{:S(2)}, u32[]{:S(2)}) collective-permute-start(bf16[2,576,512]{2,1,0:T(8,128)(2,1)} %get-tuple-element.194), channel_id=1, source_target_pairs={{0,4},{1,5},{2,6},{3,7},{4,0},{5,1},{6,2},{7,3},{8,12},{9,13},{10,... | collective-permute-start | bytes 3538952 | tf_op jit(solution)/shard_map/ppermute | solution.py:66
  646.3 64.7 %collective-permute-start.25 = (bf16[2,576,512]{2,1,0:T(8,128)(2,1)}, bf16[2,576,512]{2,1,0:T(8,128)(2,1)}, u32[]{:S(2)}, u32[]{:S(2)}) collective-permute-start(bf16[2,576,512]{2,1,0:T(8,128)(2,1)} %add_convert_fusion.16), channel_id=1, source_target_pairs={{0,16},{1,17},{2,18},{3,19},{4,20},{5,21},{6,22},{7,23},{8,24},{9,... | collective-permute-start | bytes 3538952 | tf_op jit(solution)/shard_map/ppermute | solution.py:66
  757.2 33.2 %collective-permute-start.30 = (bf16[2,576,512]{2,1,0:T(8,128)(2,1)}, bf16[2,576,512]{2,1,0:T(8,128)(2,1)}, u32[]{:S(2)}, u32[]{:S(2)}) collective-permute-start(bf16[2,576,512]{2,1,0:T(8,128)(2,1)} %get-tuple-element.196), channel_id=1, source_target_pairs={{0,4},{1,5},{2,6},{3,7},{4,0},{5,1},{6,2},{7,3},{8,12},{9,13},{10,... | collective-permute-start | bytes 3538952 | tf_op jit(solution)/shard_map/ppermute | solution.py:66
  761.4 54.3 %collective-permute-start.31 = (bf16[2,576,512]{2,1,0:T(8,128)(2,1)}, bf16[2,576,512]{2,1,0:T(8,128)(2,1)}, u32[]{:S(2)}, u32[]{:S(2)}) collective-permute-start(bf16[2,576,512]{2,1,0:T(8,128)(2,1)} %add_convert_fusion.15), channel_id=1, source_target_pairs={{0,16},{1,17},{2,18},{3,19},{4,20},{5,21},{6,22},{7,23},{8,24},{9,... | collective-permute-start | bytes 3538952 | tf_op jit(solution)/shard_map/ppermute | solution.py:66
  763.1 69.8 %collective-permute-start.36 = (bf16[2,576,512]{2,1,0:T(8,128)(2,1)}, bf16[2,576,512]{2,1,0:T(8,128)(2,1)}, u32[]{:S(2)}, u32[]{:S(2)}) collective-permute-start(bf16[2,576,512]{2,1,0:T(8,128)(2,1)} %get-tuple-element.207), channel_id=1, source_target_pairs={{0,4},{1,5},{2,6},{3,7},{4,0},{5,1},{6,2},{7,3},{8,12},{9,13},{10,... | collective-permute-start | bytes 3538952 | tf_op jit(solution)/shard_map/ppermute | solution.py:66
  788.5 100.6 %collective-permute-start.34 = (bf16[4,256,1536]{2,1,0:T(8,128)(2,1)S(1)}, bf16[4,256,1536]{2,1,0:T(8,128)(2,1)}, u32[]{:S(2)}, u32[]{:S(2)}) collective-permute-start(bf16[4,256,1536]{2,1,0:T(8,128)(2,1)S(1)} %shard_map.253), channel_id=1, source_target_pairs={{0,1},{1,0},{2,3},{3,2},{4,5},{5,4},{6,7},{7,6},{8,9},{9,8},{10,11... | collective-permute-start | bytes 9437192 | tf_op jit(solution)/shard_map/ppermute | solution.py:66
  790.0 38.1 %collective-permute-start.32 = (bf16[1,576,512]{2,1,0:T(8,128)(2,1)S(1)}, bf16[1,576,512]{2,1,0:T(8,128)(2,1)S(1)}, u32[]{:S(2)}, u32[]{:S(2)}) collective-permute-start(bf16[1,576,512]{2,1,0:T(8,128)(2,1)S(1)} %add_convert_fusion.39), channel_id=1, source_target_pairs={{0,8},{1,9},{2,10},{3,11},{4,12},{5,13},{6,14},{7,15},{8,0},{9,1},... | collective-permute-start | bytes 1769480 | tf_op jit(solution)/shard_map/ppermute | solution.py:66
  790.4 46.4 %collective-permute-start.45 = (bf16[2,576,512]{2,1,0:T(8,128)(2,1)}, bf16[2,576,512]{2,1,0:T(8,128)(2,1)S(1)}, u32[]{:S(2)}, u32[]{:S(2)}) collective-permute-start(bf16[2,576,512]{2,1,0:T(8,128)(2,1)} %get-tuple-element.237), channel_id=1, source_target_pairs={{0,4},{1,5},{2,6},{3,7},{4,0},{5,1},{6,2},{7,3},{8,12},{9,13},{10,... | collective-permute-start | bytes 3538952 | tf_op jit(solution)/shard_map/ppermute | solution.py:66
  815.7 77.8 %collective-permute-start.35 = (bf16[4,256,1536]{2,1,0:T(8,128)(2,1)}, bf16[4,256,1536]{2,1,0:T(8,128)(2,1)}, u32[]{:S(2)}, u32[]{:S(2)}) collective-permute-start(bf16[4,256,1536]{2,1,0:T(8,128)(2,1)} %shard_map.255), channel_id=1, source_target_pairs={{0,1},{1,0},{2,3},{3,2},{4,5},{5,4},{6,7},{7,6},{8,9},{9,8},{10,11... | collective-permute-start | bytes 9437192 | tf_op jit(solution)/shard_map/ppermute | solution.py:66
  828.1 33.1 %collective-permute-start.38 = (bf16[2,576,512]{2,1,0:T(8,128)(2,1)S(1)}, bf16[2,576,512]{2,1,0:T(8,128)(2,1)S(1)}, u32[]{:S(2)}, u32[]{:S(2)}) collective-permute-start(bf16[2,576,512]{2,1,0:T(8,128)(2,1)S(1)} %copy-done.97), channel_id=1, source_target_pairs={{0,4},{1,5},{2,6},{3,7},{4,0},{5,1},{6,2},{7,3},{8,12},{9,13},{10,... | collective-permute-start | bytes 3538952 | tf_op jit(solution)/shard_map/ppermute | solution.py:66
  832.9 53.2 %collective-permute-start.39 = (bf16[2,576,512]{2,1,0:T(8,128)(2,1)}, bf16[2,576,512]{2,1,0:T(8,128)(2,1)}, u32[]{:S(2)}, u32[]{:S(2)}) collective-permute-start(bf16[2,576,512]{2,1,0:T(8,128)(2,1)} %add_convert_fusion.14), channel_id=1, source_target_pairs={{0,16},{1,17},{2,18},{3,19},{4,20},{5,21},{6,22},{7,23},{8,24},{9,... | collective-permute-start | bytes 3538952 | tf_op jit(solution)/shard_map/ppermute | solution.py:66
  836.8 35.3 %collective-permute-start.40 = (bf16[1,576,512]{2,1,0:T(8,128)(2,1)S(1)}, bf16[1,576,512]{2,1,0:T(8,128)(2,1)S(1)}, u32[]{:S(2)}, u32[]{:S(2)}) collective-permute-start(bf16[1,576,512]{2,1,0:T(8,128)(2,1)S(1)} %add_convert_fusion.37), channel_id=1, source_target_pairs={{0,8},{1,9},{2,10},{3,11},{4,12},{5,13},{6,14},{7,15},{8,0},{9,1},... | collective-permute-start | bytes 1769480 | tf_op jit(solution)/shard_map/ppermute | solution.py:66
  861.2 86.6 %collective-permute-start.28 = (bf16[2,256,1664]{2,1,0:T(8,128)(2,1)}, bf16[2,256,1664]{2,1,0:T(8,128)(2,1)}, u32[]{:S(2)}, u32[]{:S(2)}) collective-permute-start(bf16[2,256,1664]{2,1,0:T(8,128)(2,1)} %get-tuple-element.335), channel_id=1, source_target_pairs={{0,8},{1,9},{2,10},{3,11},{4,12},{5,13},{6,14},{7,15},{8,0},{9,1},... | collective-permute-start | bytes 5111816 | tf_op jit(solution)/shard_map/ppermute | solution.py:66
  872.1 75.7 %collective-permute-start.33 = (bf16[2,256,1664]{2,1,0:T(8,128)(2,1)}, bf16[2,256,1664]{2,1,0:T(8,128)(2,1)}, u32[]{:S(2)}, u32[]{:S(2)}) collective-permute-start(bf16[2,256,1664]{2,1,0:T(8,128)(2,1)} %get-tuple-element.202), channel_id=1, source_target_pairs={{0,2},{1,3},{2,0},{3,1},{4,6},{5,7},{6,4},{7,5},{8,10},{9,11},{10,... | collective-permute-start | bytes 5111816 | tf_op jit(solution)/shard_map/ppermute | solution.py:66
  886.1 92.3 %collective-permute-start.42 = (bf16[2,576,512]{2,1,0:T(8,128)(2,1)}, bf16[2,576,512]{2,1,0:T(8,128)(2,1)}, u32[]{:S(2)}, u32[]{:S(2)}) collective-permute-start(bf16[2,576,512]{2,1,0:T(8,128)(2,1)} %get-tuple-element.228), channel_id=1, source_target_pairs={{0,4},{1,5},{2,6},{3,7},{4,0},{5,1},{6,2},{7,3},{8,12},{9,13},{10,... | collective-permute-start | bytes 3538952 | tf_op jit(solution)/shard_map/ppermute | solution.py:66
  889.0 146.6 %collective-permute-start.46 = (bf16[2,576,512]{2,1,0:T(8,128)(2,1)}, bf16[2,576,512]{2,1,0:T(8,128)(2,1)}, u32[]{:S(2)}, u32[]{:S(2)}) collective-permute-start(bf16[2,576,512]{2,1,0:T(8,128)(2,1)} %get-tuple-element.241), channel_id=1, source_target_pairs={{0,4},{1,5},{2,6},{3,7},{4,0},{5,1},{6,2},{7,3},{8,12},{9,13},{10,... | collective-permute-start | bytes 3538952 | tf_op jit(solution)/shard_map/ppermute | solution.py:66
  893.5 142.1 %collective-permute-start.47 = (bf16[2,576,512]{2,1,0:T(8,128)(2,1)}, bf16[2,576,512]{2,1,0:T(8,128)(2,1)}, u32[]{:S(2)}, u32[]{:S(2)}) collective-permute-start(bf16[2,576,512]{2,1,0:T(8,128)(2,1)} %add_convert_fusion.13), channel_id=1, source_target_pairs={{0,16},{1,17},{2,18},{3,19},{4,20},{5,21},{6,22},{7,23},{8,24},{9,... | collective-permute-start | bytes 3538952 | tf_op jit(solution)/shard_map/ppermute | solution.py:66
  953.6 82.0 %collective-permute-start.48 = (bf16[1,576,512]{2,1,0:T(8,128)(2,1)}, bf16[1,576,512]{2,1,0:T(8,128)(2,1)}, u32[]{:S(2)}, u32[]{:S(2)}) collective-permute-start(bf16[1,576,512]{2,1,0:T(8,128)(2,1)} %add_convert_fusion.35), channel_id=1, source_target_pairs={{0,8},{1,9},{2,10},{3,11},{4,12},{5,13},{6,14},{7,15},{8,0},{9,1},... | collective-permute-start | bytes 1769480 | tf_op jit(solution)/shard_map/ppermute | solution.py:66
  1009.9 298.3 %reduce-scatter.5.cloned.1.call-start = ((), (), s32[]{:S(2)}) async-start(), calls=%async_computation.5 | async-start | bytes 8515584 | tf_op jit(solution)/shard_map/reduce_scatter | solution.py:1003
  1035.6 32.9 %collective-permute-start.43 = (bf16[2,256,1024]{2,1,0:T(8,128)(2,1)}, bf16[2,256,1024]{2,1,0:T(8,128)(2,1)}, u32[]{:S(2)}, u32[]{:S(2)}) collective-permute-start(bf16[2,256,1024]{2,1,0:T(8,128)(2,1)} %bitcast.70), channel_id=1, source_target_pairs={{0,1},{1,0},{2,3},{3,2},{4,5},{5,4},{6,7},{7,6},{8,9},{9,8},{10,11... | collective-permute-start | bytes 3145736 | tf_op jit(solution)/shard_map/ppermute | solution.py:66
  1062.9 77.2 %collective-permute-start.51 = (bf16[2,576,512]{2,1,0:T(8,128)(2,1)S(1)}, bf16[2,576,512]{2,1,0:T(8,128)(2,1)S(1)}, u32[]{:S(2)}, u32[]{:S(2)}) collective-permute-start(bf16[2,576,512]{2,1,0:T(8,128)(2,1)S(1)} %add_convert_fusion.12), channel_id=1, source_target_pairs={{0,16},{1,17},{2,18},{3,19},{4,20},{5,21},{6,22},{7,23},{8,24},{9,... | collective-permute-start | bytes 3538952 | tf_op jit(solution)/shard_map/ppermute | solution.py:66
  1066.5 73.6 %collective-permute-start.52 = (bf16[1,576,512]{2,1,0:T(8,128)(2,1)}, bf16[1,576,512]{2,1,0:T(8,128)(2,1)}, u32[]{:S(2)}, u32[]{:S(2)}) collective-permute-start(bf16[1,576,512]{2,1,0:T(8,128)(2,1)} %add_convert_fusion.33), channel_id=1, source_target_pairs={{0,8},{1,9},{2,10},{3,11},{4,12},{5,13},{6,14},{7,15},{8,0},{9,1},... | collective-permute-start | bytes 1769480 | tf_op jit(solution)/shard_map/ppermute | solution.py:66
  1068.3 99.9 %collective-permute-start.53 = (bf16[2,256,1536]{2,1,0:T(8,128)(2,1)}, bf16[2,256,1536]{2,1,0:T(8,128)(2,1)}, u32[]{:S(2)}, u32[]{:S(2)}) collective-permute-start(bf16[2,256,1536]{2,1,0:T(8,128)(2,1)} %get-tuple-element.263), channel_id=1, source_target_pairs={{0,8},{1,9},{2,10},{3,11},{4,12},{5,13},{6,14},{7,15},{8,0},{9,1},... | collective-permute-start | bytes 4718600 | tf_op jit(solution)/shard_map/ppermute | solution.py:66
  1072.5 95.8 %collective-permute-start.54 = (bf16[2,256,1536]{2,1,0:T(8,128)(2,1)}, bf16[2,256,1536]{2,1,0:T(8,128)(2,1)}, u32[]{:S(2)}, u32[]{:S(2)}) collective-permute-start(bf16[2,256,1536]{2,1,0:T(8,128)(2,1)} %get-tuple-element.264), channel_id=1, source_target_pairs={{0,2},{1,3},{2,0},{3,1},{4,6},{5,7},{6,4},{7,5},{8,10},{9,11},{10,... | collective-permute-start | bytes 4718600 | tf_op jit(solution)/shard_map/ppermute | solution.py:66
  1084.7 43.4 %collective-permute-start.50 = (bf16[1,256,1024]{2,1,0:T(8,128)(2,1)}, bf16[1,256,1024]{2,1,0:T(8,128)(2,1)}, u32[]{:S(2)}, u32[]{:S(2)}) collective-permute-start(bf16[1,256,1024]{2,1,0:T(8,128)(2,1)} %fusion.4), channel_id=1, source_target_pairs={{0,2},{1,3},{2,0},{3,1},{4,6},{5,7},{6,4},{7,5},{8,10},{9,11},{10,... | collective-permute-start | bytes 1572872 | tf_op jit(solution)/shard_map/ppermute | solution.py:66
  (113 other events, 3865.6 us)
Sparse Core Ops, SparseCore 0:
  11.5 195.2 all-gather.2
  214.1 169.7 all-gather.4
  1010.1 157.2 reduce-scatter.2
  1178.9 129.3 reduce-scatter.4

commit v2 on v1

--- a/solution.py
+++ b/solution.py
@@ -52,7 +52,7 @@
 
 
 def lasting(micros):
-    return pl.CostEstimate(flops=int(micros * 1.1e9), bytes_accessed=0, transcendentals=0)
+    return pl.CostEstimate(flops=int(micros * 3e7), bytes_accessed=0, transcendentals=0)
 
 
 def whole_spec():
@@ -95,52 +95,44 @@
     return low
 
 
-class Trip:
-    def __init__(self, stages, places, split):
-        self.stages, self.places, self.split = stages[:-2], places, split
-        self.rest = stages[-2]
-        self.stage = len(places) - 1
-        self.waiting = [swap(stages[-1], places[-1])]
-        self.first = True
-        self.mine = self.other = None
-
-    def gather(self, received, stages):
-        start = 0
-        for stage in stages:
-            size = self.stages[stage].shape[0]
-            self.stages[stage] = add_rounded(
-                self.stages[stage], received[start : start + size]
-            )
-            start += size
-
-    def step(self, received):
-        if self.first:
-            self.first = False
-            self.gather(received, [self.stage])
-            self.waiting = [
-                swap(self.rest, self.places[-1]),
-                swap(self.stages[self.stage], self.places[self.stage - 1]),
-            ]
-            self.rest = None
-        elif self.stage == len(self.places) - 1:
-            self.gather(received, range(self.stage))
-            self.stage -= 1
-        elif self.stage > 0:
-            self.gather(received, range(self.stage + 1))
-            self.waiting.append(swap(self.stages[self.stage], self.places[self.stage - 1]))
-            self.stage -= 1
+def without_bit(index, bit):
+    return ((index >> (bit + 1)) << bit) | (index & ((1 << bit) - 1))
+
+
+class Homeward:
+    def __init__(self, grads, places):
+        bits = lax.axis_size("dp").bit_length() + lax.axis_size("expert").bit_length() - 2
+        self.held = grads.reshape((2,) * bits + (grads.shape[0] >> bits, grads.shape[1]))
+        self.ranks = list(reversed(range(bits)))
+        self.places = list(places)
+        self.start()
+
+    def start(self):
+        axis, bit = self.places[0]
+        owner_bits = lax.axis_size("expert").bit_length() - 1
+        depth = self.ranks.index(bit + (owner_bits if axis == "dp" else 0))
+        self.ranks.pop(depth)
+        upper = (lax.axis_index(axis) >> bit) & 1
+        away = lax.dynamic_index_in_dim(self.held, 1 - upper, depth, False)
+        self.held = lax.dynamic_index_in_dim(self.held, upper, depth, False)
+        self.received = swap(away, self.places.pop(0))
+
+    def join(self):
+        self.held = add_rounded(self.held, self.received)
+        if self.places:
+            self.start()
         else:
-            mine, received = self.stages[0][0].astype(F32), received[0].astype(F32)
-            self.mine = mine if self.split == 2 else mine + received
-            self.other = received
-
-
-def arrive(value, *trips):
-    value, *received = after(value, *[trip.waiting[0] for trip in trips])
-    for trip, array in zip(trips, received):
-        trip.waiting = trip.waiting[1:]
-        trip.step(array)
-    return value
+            self.received = None
+
+    def pin(self, value):
+        value, self.received = after(value, self.received)
+        self.join()
+        return value
+
+    def rows(self):
+        while self.received is not None:
+            self.join()
+        return self.held.astype(F32)
 
 
 def masks_of(places):
@@ -178,10 +170,12 @@
                 part * cos + half_swap(part) * sin
             ).astype(BF16)
 
+    first = width + LANES
     for start in range(0, width, key_width):
-        turn_into(q_ref, start, dot(h_ref[0], w_ref[:, start : start + key_width]))
-    turn_into(kv_ref, 0, dot(h_ref[0], w_ref[:, width : width + key_width]))
-    value = dot(h_ref[0], w_ref[:, width + key_width : width + 2 * key_width])
+        turn_into(q_ref, start, dot(h_ref[0], w_ref[:, first + start : first + start + key_width]))
+    first = first + width
+    turn_into(kv_ref, 0, dot(h_ref[0], w_ref[:, first : first + key_width]))
+    value = dot(h_ref[0], w_ref[:, first + key_width : first + 2 * key_width])
     kv_ref[0, :, key_width:] = value.astype(BF16)
 
 
@@ -195,7 +189,7 @@
         in_specs=[
             row_spec,
             pl.BlockSpec((1, width), lambda i: (0, 0)),
-            pl.BlockSpec(dense.shape, lambda i: (0, 0)),
+            pl.BlockSpec(dense.shape, lambda i: (0, 0), pipeline_mode=pl.Buffered(1)),
             pl.BlockSpec((rows, LANES), lambda i: (0, 0)),
             pl.BlockSpec((rows, LANES), lambda i: (0, 0)),
         ],
@@ -315,8 +309,10 @@
         dkv_ref[:, lanes] = (part * cos - half_swap(part) * sin).astype(BF16)
         lanes = slice(key_width + pair * LANES, key_width + (pair + 1) * LANES)
         dkv_ref[:, lanes] = pairs_ref[:, start + LANES : start + 2 * LANES]
-    dh = dot_cols(dq_ref[...], w_ref[:, :width])
-    dh = dh + dot_cols(dkv_ref[...], w_ref[:, width : width + 2 * key_width])
+    first = width + LANES
+    dh = dot_cols(dq_ref[...], w_ref[:, first : first + width])
+    first = first + width
+    dh = dh + dot_cols(dkv_ref[...], w_ref[:, first : first + 2 * key_width])
     x = x_ref[...].astype(F32)
     scale = lax.rsqrt(jnp.mean(x * x, axis=1, keepdims=True) + epsilon)
     dgain_ref[...] = jnp.sum(dh * x * scale, axis=0, keepdims=True)
@@ -336,7 +332,9 @@
         project_back_kernel,
         grid=(1,),
         in_specs=[
-            full, both, full, full, line, pl.BlockSpec(dense.shape, lambda i: (0, 0)), lane, lane,
+            full, both, full, full, line,
+            pl.BlockSpec(dense.shape, lambda i: (0, 0), pipeline_mode=pl.Buffered(1)),
+            lane, lane,
         ],
         out_specs=[full, both, line],
         out_shape=[
@@ -528,19 +526,22 @@
     )(places, q, kv, kv, grad, attended, lse, cos_t, sin_t)
 
 
-def expert_kernel(masks, stage_sizes, expert, aliased, me_ref, *refs):
+def expert_kernel(masks, sources, pair_bit, first, aliased, me_ref, *refs):
     count = len(masks)
-    pieces, refs = refs[:count], refs[count:]
+    arrays = 1 + max(array for per_expert in sources for array, _ in per_expert)
+    pieces, refs = refs[:arrays], refs[arrays:]
     h_ref, dy_ref, rank_ref, gate_ref = refs[:4]
     refs = refs[4 + (2 if aliased else 0) :]
     eg_ref, db_ref = refs[:2]
-    out_refs, refs = refs[2 : 2 + len(stage_sizes)], refs[2 + len(stage_sizes) :]
+    out_ref, refs = refs[2], refs[3:]
     w_in, w_down, g_in, g_down, rows_all, de_all, hidden_all, dau_all, in_sem, out_sem = refs
-    step = pl.program_id(0)
+    member, step = pl.program_id(0), pl.program_id(1)
+    expert = first + member
+    side = lax.rem(member, 2)
     blocks, tokens, width = h_ref.shape
     slots = eg_ref.shape[2]
     chunk = blocks * slots
-    inner = w_down.shape[0]
+    inner = w_down.shape[1]
     deep = width // count
     shallow = inner // count
     wide = width // inner
@@ -562,58 +563,60 @@
             )
         return pairs
 
-    def loads():
+    def loads(which):
+        made = []
+        into, down, sems = w_in.at[which % 2], w_down.at[which % 2], in_sem.at[which % 2]
+        for (array, index), mask in zip(sources[which], masks):
+            for source, target in windows(pieces[array].at[index], me ^ mask, into, down):
+                made.append(pltpu.make_async_copy(source, target, sems.at[len(made)]))
+        return made
+
+    def stores(which):
         made = []
         for piece, mask in enumerate(masks):
-            for source, target in windows(pieces[piece].at[expert], me ^ mask, w_in, w_down):
-                made.append(pltpu.make_async_copy(source, target, in_sem.at[len(made)]))
-        return made
-
-    def stores():
-        made = []
-        for piece, mask in enumerate(masks):
-            start = 0
-            for out_ref, size in zip(out_refs, stage_sizes):
-                if start <= piece < start + size:
-                    target = out_ref.at[piece - start]
-                start += size
+            target = out_ref.at[without_bit(me ^ mask, pair_bit), piece & 1, which]
             for there, here in windows(target, me ^ mask, g_in, g_down):
                 made.append(pltpu.make_async_copy(here, there, out_sem.at[len(made)]))
         return made
 
-    @pl.when(step == 0)
-    def _():
-        for copy in loads():
-            copy.start()
+    for which in range(len(sources)):
+        early = (member == 0) & (step == 0) if which == 0 else (member == which - 1) & (step == 1)
+
+        @pl.when(early)
+        def _(which=which):
+            for copy in loads(which):
+                copy.start()
 
     slot = lax.broadcasted_iota(jnp.int32, (slots, tokens), 0)
     grads = []
     weights = []
     for block in range(blocks):
         start = pl.multiple_of((step * blocks + block) * tokens, LANES)
-        hit = slot == rank_ref[expert : expert + 1, pl.ds(start, tokens)]
+        hit = slot == rank_ref[expert, :, pl.ds(start, tokens)]
         select = jnp.where(hit, 1.0, 0.0).astype(BF16)
         place = pl.ds(pl.multiple_of(step * chunk + block * slots, 16), slots)
         rows_all[place, :] = dot(select, h_ref[block]).astype(BF16)
         grads.append(dot(select, dy_ref[block]))
-        gate = gate_ref[expert : expert + 1, pl.ds(start, tokens)]
+        gate = gate_ref[expert, :, pl.ds(start, tokens)]
         weights.append(jnp.sum(jnp.where(hit, gate, 0.0), axis=1, keepdims=True))
 
-    @pl.when(step == 0)
-    def _():
-        for copy in loads():
-            copy.wait()
+    for which in range(len(sources)):
+
+        @pl.when((member == which) & (step == 0))
+        def _(which=which):
+            for copy in loads(which):
+                copy.wait()
 
     here = pl.ds(pl.multiple_of(step * chunk, 16), chunk)
     grad_rows = jnp.concatenate(grads, axis=0)
     weight = jnp.concatenate(weights, axis=0)
-    pre = dot(rows_all[here, :], w_in[...])
+    pre = dot(rows_all[here, :], w_in[side])
     gate_pre, up_pre = pre[:, :inner], pre[:, inner:]
     sigmoid = 1.0 / (1.0 + jnp.exp(-gate_pre))
     silu = gate_pre * sigmoid
     hidden = (silu * up_pre).astype(BF16)
     hidden_all[here, :] = hidden
-    out = dot(hidden, w_down[...]).astype(BF16).astype(F32)
+    out = dot(hidden, w_down[side]).astype(BF16).astype(F32)
     row_grad = jnp.sum(grad_rows * out, axis=1, keepdims=True)
     out = (weight * out).astype(BF16)
     lane = lax.broadcasted_iota(jnp.int32, (slots, LANES), 1)
@@ -625,84 +628,103 @@
         )
     de = (weight * grad_rows).astype(BF16)
     de_all[here, :] = de
-    grad_hidden = dot_cols(de, w_down[...])
+    grad_hidden = dot_cols(de, w_down[side])
     grad_up = (grad_hidden * silu).astype(BF16)
     grad_gate = (
         grad_hidden * up_pre * sigmoid * (1.0 + gate_pre * (1.0 - sigmoid))
     ).astype(BF16)
     dau_all[here, :inner] = grad_gate
     dau_all[here, inner:] = grad_up
-    back = dot_cols(dau_all[here, :], w_in[...]).astype(BF16)
+    back = dot_cols(dau_all[here, :], w_in[side]).astype(BF16)
     for block in range(blocks):
         db_ref[block, 0, :, :width] = back[block * slots : (block + 1) * slots]
 
-    @pl.when(step == pl.num_programs(0) - 1)
+    last = step == pl.num_programs(1) - 1
+    for which in range(1, len(sources)):
+
+        @pl.when(last & (member == which))
+        def _(which=which):
+            for copy in stores(which - 1):
+                copy.wait()
+
+    @pl.when(last)
     def _():
         for part in range(wide):
             lanes = slice(part * inner, (part + 1) * inner)
             g_in[lanes, :] = dot_rows(rows_all[:, lanes], dau_all[...]).astype(BF16)
         g_down[...] = dot_rows(hidden_all[...], de_all[...]).astype(BF16)
-        made = stores()
-        for copy in made:
-            copy.start()
-        for copy in made:
-            copy.wait()
-
-
-def run_expert(
-    expert, me, pieces, masks, h_all, dy_all, ranks, gates, slots, local, earlier
-):
+
+    for which in range(len(sources)):
+
+        @pl.when(last & (member == which))
+        def _(which=which):
+            for copy in stores(which):
+                copy.start()
+            if which == len(sources) - 1:
+                for copy in stores(which):
+                    copy.wait()
+
+
+def run_experts(first, me, pieces, masks, pair_bit, h_all, dy_all, ranks, gates, slots, local, earlier):
     block_count, tokens, width = h_all.shape
-    piece_rows, inner = pieces[0].shape[1:]
-    count = len(pieces)
-    stage_sizes = [1]
-    while 2 * sum(stage_sizes) < count:
-        stage_sizes.append(sum(stage_sizes))
-    stage_sizes += [count // 4, count // 4]
+    members = len(pieces)
+    arrays = []
+    sources = []
+    for per_expert in pieces:
+        found = []
+        for array, index in per_expert:
+            known = [place for place, other in enumerate(arrays) if other is array]
+            if not known:
+                known = [len(arrays)]
+                arrays.append(array)
+            found.append((known[0], index))
+        sources.append(found)
+    piece_rows, inner = arrays[0].shape[1:]
+    count = len(masks)
     steps = block_count // BLOCKS_PER_STEP
     rows = block_count * slots
-    block_spec = pl.BlockSpec((BLOCKS_PER_STEP, tokens, width), lambda i, s: (i, 0, 0))
+    block_spec = pl.BlockSpec((BLOCKS_PER_STEP, tokens, width), lambda g, i, s: (i, 0, 0))
     any_spec = pl.BlockSpec(memory_space=pl.ANY)
-    table = pl.BlockSpec(ranks.shape, lambda i, s: (0, 0))
+    table = pl.BlockSpec((ranks.shape[0], 1, ranks.shape[1]), lambda g, i, s: (0, 0, 0))
     widths = (width, width + LANES)
     copies = count * (2 + width // inner)
-    aliases = {}
-    extra = []
-    if earlier is not None:
-        extra = list(earlier)
-        aliases = {1 + count + 4: 0, 1 + count + 5: 1}
+    extra = [] if earlier is None else list(earlier)
+    start = 1 + len(arrays) + 4
+    aliases = {start + place: place for place in range(len(extra))}
     return pl.pallas_call(
-        functools.partial(expert_kernel, masks, stage_sizes, expert, earlier is not None),
+        functools.partial(expert_kernel, masks, sources, pair_bit, first, earlier is not None),
         grid_spec=pltpu.PrefetchScalarGridSpec(
             num_scalar_prefetch=1,
-            grid=(steps,),
-            in_specs=[any_spec] * count
+            grid=(members, steps),
+            in_specs=[any_spec] * len(arrays)
             + [block_spec, block_spec, table, table]
             + [any_spec] * len(extra),
             out_specs=[
-                pl.BlockSpec((BLOCKS_PER_STEP, 1, slots, w), lambda i, s: (i, expert, 0, 0))
+                pl.BlockSpec(
+                    (BLOCKS_PER_STEP, 1, slots, w), lambda g, i, s: (i, first + g, 0, 0)
+                )
                 for w in widths
             ]
-            + [any_spec] * len(stage_sizes),
+            + [any_spec],
             scratch_shapes=[
-                pltpu.VMEM((width, 2 * inner), BF16),
-                pltpu.VMEM((inner, width), BF16),
+                pltpu.VMEM((2, width, 2 * inner), BF16),
+                pltpu.VMEM((2, inner, width), BF16),
                 pltpu.VMEM((width, 2 * inner), BF16),
                 pltpu.VMEM((inner, width), BF16),
                 pltpu.VMEM((rows, width), BF16),
                 pltpu.VMEM((rows, width), BF16),
                 pltpu.VMEM((rows, inner), BF16),
                 pltpu.VMEM((rows, 2 * inner), BF16),
-                pltpu.SemaphoreType.DMA((copies,)),
+                pltpu.SemaphoreType.DMA((2, copies)),
                 pltpu.SemaphoreType.DMA((copies,)),
             ],
         ),
         out_shape=[jax.ShapeDtypeStruct((block_count, local, slots, w), BF16) for w in widths]
-        + [jax.ShapeDtypeStruct((size, piece_rows, inner), BF16) for size in stage_sizes],
+        + [jax.ShapeDtypeStruct((count // 2, 2, members, piece_rows, inner), BF16)],
         input_output_aliases=aliases,
-        cost_estimate=lasting(31),
-        compiler_params=params(60),
-    )(me, *pieces, h_all, dy_all, ranks, gates, *extra)
+        cost_estimate=lasting(31 * members),
+        compiler_params=params(60, 2),
+    )(me, *arrays, h_all, dy_all, ranks[:, None], gates[:, None], *extra)
 
 
 def combine_kernel(src_ref, place_ref, out_ref):
@@ -729,7 +751,7 @@
         out_specs=pl.BlockSpec((1, tokens, width), lambda i: (i, 0, 0)),
         out_shape=jax.ShapeDtypeStruct((size, tokens, width), BF16),
         cost_estimate=lasting(4.4),
-        compiler_params=params(32),
+        compiler_params=params(60),
     )(source, places)
 
 
@@ -801,13 +823,13 @@
 
     rows_owned = w_query.shape[0]
 
-    def dense_gather(parts):
+    def padded(parts):
         taken = sum(part.shape[1] for part in parts)
-        pad = jnp.zeros((rows_owned, -taken % LANES), BF16)
-        packed = jnp.concatenate(parts + [pad], axis=1)
-        return lax.all_gather(packed, AXES, axis=0, tiled=True)
-
-    dense_one = dense_gather([w_query, key_weight, value_weight, gain_attn[:, None]])
+        return parts + [jnp.zeros((rows_owned, -taken % LANES), BF16)]
+
+    packed = padded([w_output, w_router, gain_moe[:, None]])
+    packed += padded([w_query, key_weight, value_weight, gain_attn[:, None]])
+    dense = lax.all_gather(jnp.concatenate(packed, axis=1), AXES, axis=0, tiled=True)
 
     def packed_half(which):
         return pack_experts(
@@ -845,70 +867,61 @@
         dys.append(dy)
         dy_rows.append(jnp.concatenate([dy, code.astype(BF16)], axis=1))
 
+    cut = (local + 1) // 2
     rows_here = jnp.stack(dy_rows)[None]
-    direct = [
-        swap(other_packed if stage == 0 else mine_packed, place)
-        for stage, place in enumerate(dp_places)
-    ]
+    first_piece = swap(other_packed, dp_places[0])
+    last_piece = swap(mine_packed, dp_places[-1])
     dy_received = swap(rows_here, token_places[0][0])
-    dense_one, dy_received, *direct = after(dense_one, dy_received, *direct)
+    own_rows, dense, rows_here, first_piece, last_piece, dy_received = after(
+        mine_packed, dense, rows_here, first_piece, last_piece, dy_received
+    )
+    between = swap(own_rows, dp_places[1])
     rows_here = jnp.concatenate([rows_here, dy_received], axis=0)
-
-    weight_pieces = [mine_packed, direct[0]]
-    for stage, place in enumerate(dp_places[1:], 1):
-        received = [direct[stage]]
-        for piece in weight_pieces[1:]:
-            if len(received) > 1:
-                piece, received[-1] = after(piece, received[-1])
-            received.append(swap(piece, place))
-        weight_pieces = weight_pieces + received
-    levels = [index.bit_count() for index in range(len(weight_pieces))]
-
-    def weights_here(value, indices):
-        value, *pieces = after(value, *[weight_pieces[index] for index in indices])
-        for index, piece in zip(indices, pieces):
-            weight_pieces[index] = piece
-        return value
-
-    output_rows, dense_one = after(w_output, dense_one)
-    dense_two = dense_gather([output_rows, w_router, gain_moe[:, None]])
-    for place in token_places[0][1:-1]:
-        rows_here = jnp.concatenate([rows_here, swap(rows_here, place)], axis=0)
-
-    gain_one = dense_one[:, width + 2 * key_width].astype(F32)[None]
-    gain_two = dense_two[:, width + EXPERTS].astype(F32)[None]
+    dy_received = swap(rows_here, token_places[0][1])
+    if len(token_places[0]) > 3:
+        rows_here = jnp.concatenate([rows_here, dy_received], axis=0)
+        dy_received = swap(rows_here, token_places[0][2])
+    forward = swap(first_piece, dp_places[-1])
+
+    gain_one = dense[:, dense.shape[1] - LANES].astype(F32)[None]
+    gain_two = dense[:, width + EXPERTS].astype(F32)[None]
     x = layer_input[0]
-    normed, queries, keys_values = project(x, gain_one, dense_one, cos, sin)
+    normed, queries, keys_values = project(x, gain_one, dense, cos, sin)
     key_rows, attended, log_totals, middles, normed_two, gates = [], [], [], [], [], []
     row_halves = []
     for index in range(micro_count):
         halves = gather_rows(keys_values[index], key_places)
         key_rows.append(jnp.concatenate(halves, axis=0).reshape(-1, 2 * key_width))
+
+    rows, lse = attend(attend_places[0], queries[0], key_rows[0])
+    attended.append(rows)
+    log_totals.append(lse)
+    rows, lse = attend(attend_places[1], queries[1], key_rows[1])
+    attended.append(rows)
+    log_totals.append(lse)
+    stage_rows = []
     for index in range(micro_count):
-        if index == 1:
-            attend_places[index], rows_here = after(attend_places[index], rows_here)
-            rows_there = swap(rows_here, token_places[0][-1])
-        rows, lse = attend(attend_places[index], queries[index], key_rows[index])
-        attended.append(rows)
-        log_totals.append(lse)
-        if index == 1:
-            gain_two = weights_here(
-                gain_two,
-                [
-                    i for i, level in enumerate(levels)
-                    if level == 2 and i > len(levels) // 2
-                ][:1],
-            )
-        middle, normed_rows, gate = middle_rows(x[index], rows, dense_two, gain_two, codes[index])
+        middle, normed_rows, gate = middle_rows(
+            x[index], attended[index], dense, gain_two, codes[index]
+        )
         middles.append(middle)
         normed_two.append(normed_rows)
         gates.append(gate)
-        row_halves += gather_rows(normed_rows, token_places[index])
-    row_all = jnp.concatenate(row_halves, axis=0)
-    block_count = row_all.shape[0]
-    per_micro = block_count // micro_count
+        stage_rows.append([swap(normed_rows, place) for place in token_places[index][:-1]])
+    flat = [row for rows in stage_rows for row in rows]
+    between, forward, first_piece, dy_received, *flat = after(
+        between, forward, first_piece, dy_received, *flat
+    )
+    rows_here = jnp.concatenate([rows_here, dy_received], axis=0)
+    stage_rows = [flat[: len(flat) // 2], flat[len(flat) // 2 :]]
+    firsts = [first_piece[:cut], first_piece[cut:]]
+    onward = [swap(firsts[0], dp_places[1])]
+    along = swap(between, dp_places[-1])
+    rows_there = swap(rows_here, token_places[0][-1])
 
     dy_blocks = []
+    per_micro = 2 * rows_here.shape[0]
+    block_count = micro_count * per_micro
     for index in range(micro_count):
         order = [token_places[0].index(place) for place in token_places[index]]
         for piece in range(per_micro):
@@ -920,8 +933,28 @@
     code_all = jnp.roll(code_all.reshape(EXPERTS, block_count * tokens), -first_expert, axis=0)
     rank_table = code_all[:8].astype(jnp.int32)
 
-    router_t = jnp.roll(dense_two[:, width : width + EXPERTS].T, -first_expert, axis=0)
-    router_t = weights_here(router_t, [i for i, level in enumerate(levels) if level == 2])
+    for index in range(micro_count):
+        pieces = [normed_two[index], *stage_rows[index]]
+        pieces.append(swap(pieces[1], token_places[index][1]))
+        pieces = jnp.stack(pieces)
+        if index == 1:
+            pieces, along, onward[0], firsts[1], dy_all, rank_table = after(
+                pieces, along, onward[0], firsts[1], dy_all, rank_table
+            )
+            onward.append(swap(firsts[1], dp_places[1]))
+            across = [swap(part, dp_places[-1]) for part in onward]
+        row_halves += [pieces, swap(pieces, token_places[index][-1])]
+    row_all = jnp.concatenate(row_halves, axis=0)
+
+    def expert_pieces(expert):
+        return [
+            (parts[0], expert)
+            if len(parts) == 1
+            else (parts[expert >= cut], expert - cut * (expert >= cut))
+            for parts in weight_parts
+        ]
+
+    router_t = jnp.roll(dense[:, width : width + EXPERTS].T, -first_expert, axis=0)
     logits = dot_cols(router_t, row_all.reshape(block_count * tokens, width))
     chosen = code_all > -1.5
     peak = jnp.max(jnp.where(chosen, logits, masked_score), axis=0, keepdims=True)
@@ -929,18 +962,28 @@
     gate_table = (raised / jnp.sum(raised, axis=0, keepdims=True))[:8]
     me = jnp.stack([dp_index, first_expert]).astype(jnp.int32)
     held = None
-    trips = []
-    for expert in range(local):
-        if 2 <= expert <= 4:
-            me = arrive(me, *[trips[0], trips[0], trips[1]][expert - 2 : expert - 1])
-            if expert == 4:
-                me = arrive(me, trips[0])
-        outs = run_expert(
-            expert, me, weight_pieces, weight_masks, row_all, dy_all, rank_table,
-            gate_table, slots, local, held,
+    groups = [
+        [index for index in range(dp_count) if index >> pair_bit & 1 == side] for side in range(2)
+    ]
+    summed = []
+    me, *across = after(me, *across)
+    weight_parts = [[mine_packed], [first_piece], [between], onward, [last_piece], [forward], [along], across]
+    if len(dp_places) > 3:
+        more = [[mine_packed], [first_piece], [between], onward]
+        for place in dp_places[2:-1]:
+            more = more + [[swap(part, place) for part in parts] for parts in more]
+        weight_parts = more + [[swap(part, dp_places[-1]) for part in parts] for parts in more]
+
+    for first, end in ((0, cut), (cut, local)):
+        *held, grads = run_experts(
+            first, me, [expert_pieces(expert) for expert in range(first, end)], weight_masks,
+            pair_bit, row_all, dy_all, rank_table, gate_table, slots, local, held,
         )
-        held = outs[:2]
-        trips.append(Trip(list(outs[2:]), dp_places, split))
+        summed.append(
+            lax.psum_scatter(
+                grads, "dp", scatter_dimension=0, axis_index_groups=groups, tiled=True
+            )[0]
+        )
     eg_all, db_all = held
 
     slot_place = rank_table[:local]
@@ -968,9 +1011,7 @@
             )
         return found
 
-    slot_place = arrive(slot_place, trips[1])
     sums = first_trade(db_all, slot_place)
-    sums[1][1] = arrive(sums[1][1], trips[2], trips[1], trips[0])
     received = [
         swap(sums[index][1], token_places[index][-2]) for index in range(micro_count)
     ]
@@ -979,16 +1020,14 @@
     flat, shape = jax.tree.flatten((received, mixed))
     received, mixed = jax.tree.unflatten(shape, lax.optimization_barrier(tuple(flat)))
     row_grads = []
-    lows[0] = arrive(lows[0], trips[2])
     for index in range(micro_count):
         total = add_rounded(lows[index], received[index])
         row_grads.append(sum_home(total[:1], total[1:], token_places[index][:1])[0])
-    back_gain = arrive(gain_two, trips[3], trips[2], trips[1])
 
     router_grads, middle_grads, branch_grads, head_grads, gain_two_grads = [], [], [], [], []
     for index in range(micro_count):
         dz, dy1, branch, head_grad, gain_grad = middle_back(
-            row_grads[index], middles[index], dys[index], gates[index], back_gain, dense_two
+            row_grads[index], middles[index], dys[index], gates[index], gain_two, dense
         )
         router_grads.append(dz)
         middle_grads.append(dy1)
@@ -999,24 +1038,22 @@
     def tall(parts):
         return jnp.concatenate(parts, axis=0)
 
-    def to_owner(grads):
-        return lax.psum_scatter(grads, AXES, scatter_dimension=0, tiled=True).astype(F32)
-
-    gain_two_grads[0] = arrive(gain_two_grads[0], trips[3])
     early = weight_grads(
         [tall(attended), tall(normed_two)],
         [tall(branch_grads), tall(router_grads)],
         sum(gain_two_grads),
         width + LANES,
     )
-    output_grads = to_owner(early)
+    along_z = [("dp", bit) for bit in reversed(range(1, dp_bits))]
+    along_x = [("dp", 0)] if dp_bits else []
+    home_two = Homeward(early, [("expert", 0)] + along_x + row_places + along_z)
     head_grads[0], early = after(head_grads[0], early)
 
     query_grads, pair_grads = [], []
     for index in range(micro_count):
         if index == micro_count - 1:
             attend_places[index], query_grads[0] = after(attend_places[index], query_grads[0])
-            attend_places[index] = arrive(attend_places[index], trips[4], trips[3], trips[2])
+            attend_places[index] = home_two.pin(attend_places[index])
         dq, pairs = attend_back(
             attend_places[index], queries[index], key_rows[index], head_grads[index],
             attended[index], log_totals[index], cos_t, sin_t,
@@ -1027,30 +1064,40 @@
         query_grads.append(dq)
     normed_all = normed.reshape(micro_count * tokens, width)
 
-    query_grads[-1], *highs = after(query_grads[-1], *[pair[1] for pair in mixed])
-    last_gain = arrive(gain_one, trips[4])
-    mix_received = [
-        swap(highs[index], token_places[index][-2]) for index in range(micro_count)
-    ]
+    pair_grads[0], summed[0] = after(pair_grads[0], summed[0])
+    other = [swap(summed[0][1], dp_places[0])]
     key_grads, input_grads, gain_one_grads = [], [], []
     for index in range(micro_count):
         dx, dkv, gain_grad = project_back(
-            query_grads[index], pair_grads[index], x[index], middle_grads[index], last_gain,
-            dense_one, cos, sin,
+            query_grads[index], pair_grads[index], x[index], middle_grads[index], gain_one,
+            dense, cos, sin,
         )
         input_grads.append(dx)
         key_grads.append(dkv)
         gain_one_grads.append(gain_grad)
-    gain_one_grad = arrive(sum(gain_one_grads), trips[4], trips[3])
-    gain_one_grad, output_grads, *mix_received = after(gain_one_grad, output_grads, *mix_received)
+    gain_one_grad = home_two.pin(sum(gain_one_grads))
     late = weight_grads(
         [normed_all, normed_all],
         [tall(query_grads), tall(key_grads)],
         gain_one_grad,
         width + 2 * key_width + LANES,
     )
-    late_grads = to_owner(late)
-    mix_received[0], late = after(mix_received[0], late)
+    home_one = Homeward(late, [("expert", 0)] + row_places + along_x + along_z)
+    other.append(swap(summed[1][1], dp_places[0]))
+    home_one.received, home_two.received = after(home_one.received, home_two.received)
+    home_one.join()
+    home_two.join()
+    home_one.received, home_two.received = after(home_one.received, home_two.received)
+    home_one.join()
+    home_two.join()
+    highs = after(home_one.held, *[pair[1] for pair in mixed])[1:]
+    mix_received = [
+        swap(highs[index], token_places[index][-2]) for index in range(micro_count)
+    ]
+    home_one.received, *other = after(home_one.received, *other)
+    home_one.join()
+    home_one.received, *mix_received = after(home_one.received, *mix_received)
+    home_one.join()
     mixtures = []
     for index in range(micro_count):
         total = add_rounded(mixed[index][0], mix_received[index])
@@ -1061,17 +1108,16 @@
             for index in range(micro_count)
         ]
     )[None]
-    for trip in trips:
-        while trip.mine is None:
-            trip.step(trip.waiting.pop(0))
-
-    mine = jnp.stack([trip.mine for trip in trips])
+
+    mine = jnp.concatenate([part[0] for part in summed], axis=0).astype(F32)
+    other = jnp.concatenate(other, axis=0).astype(F32)
     if split == 2:
-        other = jnp.stack([trip.other for trip in trips])
         lower = half == 0
         mine = jnp.concatenate(
             [jnp.where(lower, mine, other), jnp.where(lower, other, mine)], axis=0
         )
+    else:
+        mine = mine + other
     deep = w_gate.shape[1]
     inner = w_gate.shape[2]
     grad_gate = mine[:, :deep]
@@ -1082,6 +1128,8 @@
         .transpose(0, 2, 1, 3)
         .reshape(w_down.shape)
     )
+    late_grads = home_one.rows()
+    output_grads = home_two.rows()
     return (
         layer_output,
         jnp.stack(input_grads)[None],

time: 1330 us -> 1210 us (0.910)
  waiting for transfers between devices: 657 us -> 558 us
    reduce_scatter x2, waiting for transfers between devices: 91.9 us -> 14.7 us  [shards(): lax.psum_scatter(grads, 'dp', scatter_dimension=0, axis_index_groups=grou...]
    all_gather x2 -> x1, waiting for transfers between devices: 37.8 us -> 3.2 us  [shards(): lax.all_gather(jnp.concatenate(packed, axis=1), AXES, axis=0, tiled=True)]
    unnamed x229 -> x182, local copies, waits for them, and re-layouts: 75.3 us -> 45.3 us
    pallas_call x5 -> x2, Pallas kernels: 158 us -> 135 us  [run_experts(): pl.pallas_call(functools.partial(expert_kernel, masks, sources, pair_bit,...]
    pallas_call x8, Pallas kernels: 30.6 us -> 52 us  [combine(): pl.pallas_call(combine_kernel, grid=(size,), in_specs=[pl.BlockSpec((1, l...]
    squeeze x1 -> x13, local copies, waits for them, and re-layouts: 0.1 us -> 18.8 us  [the longest x10 13.5 us: start(): away = lax.dynamic_index_in_dim(self.held, 1 - upper, depth, False)]
    ppermute x58 -> x52, waiting for transfers between devices: 528 us -> 540 us  [swap(): lax.ppermute(array, AXES, [(i, i ^ flip) for i in range(dp_count * owner_...]
    ppermute x58 -> x52, starting transfers between devices: 56.6 us -> 53.4 us  [swap(): lax.ppermute(array, AXES, [(i, i ^ flip) for i in range(dp_count * owner_...]
  transfers between devices with their start and end apart: 62 -> 55, of which waited for: 24 -> 25; matrix products, arithmetic and copies ran while one was open for 17% -> 16% of each run, Pallas kernels for 20% -> 21%
where the time goes in v2:
time: 1210 us; the launch traced here: 1200 us
  waiting for transfers between devices  558 us (46%)
  Pallas kernels  342 us (28%)
  local copies, waits for them, and re-layouts  114 us (9%)
  other arithmetic  111 us (9%)
  starting transfers between devices  53.5 us (4%)
  between operations  15.6 us (1%)
    ppermute x52, waiting for transfers between devices, swap(): lax.ppermute(array, AXES, [(i, i ^ flip) for i in range(dp_count * owner_...  540 us
    pallas_call x2, Pallas kernels, run_experts(): pl.pallas_call(functools.partial(expert_kernel, masks, sources, pair_bit,...  135 us
    ppermute x52, starting transfers between devices, swap(): lax.ppermute(array, AXES, [(i, i ^ flip) for i in range(dp_count * owner_...  53.4 us
    pallas_call x8, Pallas kernels, combine(): pl.pallas_call(combine_kernel, grid=(size,), in_specs=[pl.BlockSpec((1, l...  52 us
    pallas_call x2, Pallas kernels, attend_back(): pl.pallas_call(attend_back_kernel, grid_spec=pltpu.PrefetchScalarGridSpec...  47.2 us
    unnamed x182, local copies, waits for them, and re-layouts  45.3 us
    convert_element_type x18, other arithmetic, add_rounded(): return (left.astype(F32) + right.astype(F32)).astype(left.dtype)  44.2 us
    pallas_call x2, Pallas kernels, attend(): pl.pallas_call(attend_kernel, grid_spec=pltpu.PrefetchScalarGridSpec(num_...  37.5 us
  transfers between devices with their start and end apart: 55, of which 25 were waited for; matrix products, arithmetic and copies ran while one was open for 16% of the time, Pallas kernels for 21%

profile of v2, /device:TPU:0, one launch (start us, length us, event | category | flops | bytes accessed | tf_op | source)
XLA Modules:
  0.0 1198.3 jit_solution(3641584975340157767)
XLA Ops:
  38.0 42.5 %collective-permute-done.2 = bf16[1,2,256,1664]{3,2,1,0:T(8,128)(2,1)} collective-permute-done((bf16[1,2,256,1664]{3,2,1,0:T(8,128)(2,1)}, bf16[1,2,256,1664]{3,2,1,0:T(8,128)(2,1)}, u32[]{:S(2)}, u32[]{:S(2)}) %collective-permute-start.2) | collective-permute-done | bytes 1703968 | tf_op jit(solution)/shard_map/ppermute | solution.py:66
  80.5 68.8 %collective-permute-done.refs_1_ = bf16[5,576,512]{2,1,0:T(8,128)(2,1)} collective-permute-done((bf16[5,576,512]{2,1,0:T(8,128)(2,1)}, bf16[5,576,512]{2,1,0:T(8,128)(2,1)}, u32[]{:S(2)}, u32[]{:S(2)}) %collective-permute-start) | collective-permute-done | bytes 2949152 | tf_op jit(solution)/shard_map/ppermute | solution.py:66
  154.1 9.6 shard_map.238
  181.5 9.3 collective-permute-done.3
  195.9 18.9 %shard_map.239 = (bf16[256,1536]{1,0:T(8,128)(2,1)S(1)}, f32[4,8,256]{2,1,0:T(8,128)S(1)}) custom-call(s32[6]{0:T(128)S(1)} %concatenate.92.places_ref, bf16[256,1536]{1,0:T(8,128)(2,1)S(1)} %get-tuple-element.289.q_ref, bf16[1024,1024]{1,0:T(8,128)(2,1)S(1)} %bitcast.238, bf16[1024,1024]{1,0:T(8,128)(2,1)S(1)} %bitcast.239), custom_call_target="tpu_custom_call" | custom-call | flops 570000000 | tf_op jit(solution)/shard_map/pallas_call | solution.py:424
  228.2 18.7 %shard_map.241 = (bf16[256,1536]{1,0:T(8,128)(2,1)S(1)}, f32[4,8,256]{2,1,0:T(8,128)S(1)}) custom-call(s32[6]{0:T(128)S(1)} %concatenate.102.places_ref, bf16[256,1536]{1,0:T(8,128)(2,1)S(1)} %get-tuple-element.290.q_ref, bf16[1024,1024]{1,0:T(8,128)(2,1)S(1)} %bitcast.234, bf16[1024,1024]{1,0:T(8,128)(2,1)S(1)} %bitcast.235), custom_call_target="tpu_custom_call" | custom-call | flops 570000000 | tf_op jit(solution)/shard_map/pallas_call | solution.py:424
  254.5 73.7 %collective-permute-done.11 = bf16[256,1536]{1,0:T(8,128)(2,1)} collective-permute-done((bf16[256,1536]{1,0:T(8,128)(2,1)S(1)}, bf16[256,1536]{1,0:T(8,128)(2,1)}, u32[]{:S(2)}, u32[]{:S(2)}) %collective-permute-start.11) | collective-permute-done | bytes 786464 | tf_op jit(solution)/shard_map/ppermute | solution.py:66
  329.9 13.9 %collective-permute-done.12 = bf16[256,1536]{1,0:T(8,128)(2,1)} collective-permute-done((bf16[256,1536]{1,0:T(8,128)(2,1)S(1)}, bf16[256,1536]{1,0:T(8,128)(2,1)}, u32[]{:S(2)}, u32[]{:S(2)}) %collective-permute-start.12) | collective-permute-done | bytes 786464 | tf_op jit(solution)/shard_map/ppermute | solution.py:66
  345.3 6.6 pad_maximum_fusion
  369.4 51.2 %collective-permute-done.21 = bf16[256,1536]{1,0:T(8,128)(2,1)S(1)} collective-permute-done((bf16[256,1536]{1,0:T(8,128)(2,1)}, bf16[256,1536]{1,0:T(8,128)(2,1)S(1)}, u32[]{:S(2)}, u32[]{:S(2)}) %collective-permute-start.21) | collective-permute-done | bytes 786464 | tf_op jit(solution)/shard_map/ppermute | solution.py:66
  442.1 4.8 copy-done.30
  456.1 49.1 %collective-permute-done.19.refs_3_ = bf16[2,576,512]{2,1,0:T(8,128)(2,1)S(1)} collective-permute-done((bf16[2,576,512]{2,1,0:T(8,128)(2,1)}, bf16[2,576,512]{2,1,0:T(8,128)(2,1)S(1)}, u32[]{:S(2)}, u32[]{:S(2)}) %collective-permute-start.19) | collective-permute-done | bytes 1179680 | tf_op jit(solution)/shard_map/ppermute | solution.py:66
  510.4 22.0 %collective-permute-done.20.refs_7_ = bf16[2,576,512]{2,1,0:T(8,128)(2,1)S(1)} collective-permute-done((bf16[2,576,512]{2,1,0:T(8,128)(2,1)S(1)}, bf16[2,576,512]{2,1,0:T(8,128)(2,1)S(1)}, u32[]{:S(2)}, u32[]{:S(2)}) %collective-permute-start.20) | collective-permute-done | bytes 1179680 | tf_op jit(solution)/shard_map/ppermute | solution.py:66
  538.9 79.5 %shard_map.243 = (bf16[16,5,64,1536]{3,2,1,0:T(8,128)(2,1)}, bf16[16,5,64,1664]{3,2,1,0:T(8,128)(2,1)}, bf16[4,2,3,576,512]{4,3,2,1,0:T(8,128)(2,1)}) custom-call(s32[2]{0:T(128)} %pad_add_fusion.me_ref, bf16[5,576,512]{2,1,0:T(8,128)(2,1)} %pad_maximum_fusion.5.refs_0_, bf16[5,576,512]{2,1,0:T(8,128)(2,1)} %collective-permute-done.refs_1_, ...), custom_call_target="tpu_custom_call" | custom-call | flops 2790000128 | tf_op jit(solution)/shard_map/pallas_call | solution.py:694
  623.6 55.6 %shard_map.244 = (bf16[16,5,64,1536]{3,2,1,0:T(8,128)(2,1)}, bf16[16,5,64,1664]{3,2,1,0:T(8,128)(2,1)}, bf16[4,2,2,576,512]{4,3,2,1,0:T(8,128)(2,1)}) custom-call(s32[2]{0:T(128)} %pad_add_fusion.me_ref, bf16[5,576,512]{2,1,0:T(8,128)(2,1)} %pad_maximum_fusion.5.refs_0_, ...), custom_call_target="tpu_custom_call", output_to_operand_aliasing={{0}: (13, {}), {1}: (14, {})} | custom-call | flops 1860000000 | tf_op jit(solution)/shard_map/pallas_call | solution.py:694
  679.2 6.7 shard_map.246
  685.9 6.7 shard_map.248
  693.0 6.5 shard_map.245
  699.6 6.5 shard_map.247
  706.1 6.1 add_convert_fusion.3
  716.8 6.2 shard_map.250
  723.4 6.4 shard_map.252
  731.4 6.2 shard_map.249
  737.6 6.7 shard_map.251
  744.3 5.6 add_convert_fusion.10
  754.4 46.4 %collective-permute-done.25 = bf16[2,256,1664]{2,1,0:T(8,128)(2,1)} collective-permute-done((bf16[2,256,1664]{2,1,0:T(8,128)(2,1)}, bf16[2,256,1664]{2,1,0:T(8,128)(2,1)}, u32[]{:S(2)}, u32[]{:S(2)}) %collective-permute-start.25) | collective-permute-done | bytes 1703968 | tf_op jit(solution)/shard_map/ppermute | solution.py:66
  808.6 15.0 %collective-permute-done.30 = bf16[1,256,1664]{2,1,0:T(8,128)(2,1)S(1)} collective-permute-done((bf16[1,256,1664]{2,1,0:T(8,128)(2,1)S(1)}, bf16[1,256,1664]{2,1,0:T(8,128)(2,1)S(1)}, u32[]{:S(2)}, u32[]{:S(2)}) %collective-permute-start.30) | collective-permute-done | bytes 852000 | tf_op jit(solution)/shard_map/ppermute | solution.py:66
  824.6 6.6 shard_map.253
  831.2 13.0 %collective-permute-done.31 = bf16[1,256,1664]{2,1,0:T(8,128)(2,1)S(1)} collective-permute-done((bf16[1,256,1664]{2,1,0:T(8,128)(2,1)}, bf16[1,256,1664]{2,1,0:T(8,128)(2,1)S(1)}, u32[]{:S(2)}, u32[]{:S(2)}) %collective-permute-start.31) | collective-permute-done | bytes 852000 | tf_op jit(solution)/shard_map/ppermute | solution.py:66
  845.4 6.6 shard_map.254
  857.3 7.9 shard_map.255
  869.5 23.3 %shard_map.256 = (bf16[256,1536]{1,0:T(8,128)(2,1)}, bf16[1024,1024]{1,0:T(8,128)(2,1)}) custom-call(s32[6]{0:T(128)} %copy-done.27, bf16[256,1536]{1,0:T(8,128)(2,1)} %copy-done.5, bf16[1024,1024]{1,0:T(8,128)(2,1)} %bitcast.240, bf16[1024,1024]{1,0:T(8,128)(2,1)} %bitcast.241, bf16[256,1536]{1,0:T(8,128)(2,1)} %get-tuple-element.155.do_ref, ...), custom_call_target="tpu_custom_call" | custom-call | flops 705000000 | tf_op jit(solution)/shard_map/pallas_call | solution.py:502
  897.0 23.9 %shard_map.257 = (bf16[256,1536]{1,0:T(8,128)(2,1)}, bf16[1024,1024]{1,0:T(8,128)(2,1)}) custom-call(s32[6]{0:T(128)} %copy-done.28, bf16[256,1536]{1,0:T(8,128)(2,1)} %copy-done.4, bf16[1024,1024]{1,0:T(8,128)(2,1)} %bitcast.236, bf16[1024,1024]{1,0:T(8,128)(2,1)} %bitcast.237, bf16[256,1536]{1,0:T(8,128)(2,1)} %get-tuple-element.161.do_ref, ...), custom_call_target="tpu_custom_call" | custom-call | flops 705000000 | tf_op jit(solution)/shard_map/pallas_call | solution.py:502
  929.1 9.6 collective-permute-done.34
  942.2 7.3 collective-permute-done.36
  950.6 9.6 shard_map.259
  960.2 10.0 shard_map.258
  971.5 6.3 collective-permute-done.37
  979.9 10.3 shard_map.260
  997.7 15.5 %collective-permute-done.39 = bf16[2,2,48,1664]{3,2,1,0:T(8,128)(2,1)S(1)} collective-permute-done((bf16[2,2,48,1664]{3,2,1,0:T(8,128)(2,1)S(1)}, bf16[2,2,48,1664]{3,2,1,0:T(8,128)(2,1)S(1)}, u32[]{:S(2)}, u32[]{:S(2)}) %collective-permute-start.39) | collective-permute-done | bytes 639008 | tf_op jit(solution)/shard_map/ppermute | solution.py:66
  1014.0 4.9 fusion
  1023.7 14.7 %reduce-scatter.5.cloned.1.call-done = bf16[1,2,2,576,512]{4,3,2,1,0:T(8,128)(2,1)} async-done(((bf16[4,2,2,576,512]{4,3,2,1,0:T(8,128)(2,1)}), bf16[1,2,2,576,512]{4,3,2,1,0:T(8,128)(2,1)}) %reduce-scatter.5.cloned.1.call-update) | async-done | bytes 2359312 | tf_op jit(solution)/shard_map/reduce_scatter | solution.py:983
  1047.1 27.7 %collective-permute-done.41 = bf16[2,48,1664]{2,1,0:T(8,128)(2,1)S(1)} collective-permute-done((bf16[2,48,1664]{2,1,0:T(8,128)(2,1)S(1)}, bf16[2,48,1664]{2,1,0:T(8,128)(2,1)S(1)}, u32[]{:S(2)}, u32[]{:S(2)}) %collective-permute-start.41) | collective-permute-done | bytes 319520 | tf_op jit(solution)/shard_map/ppermute | solution.py:66
  1086.0 29.4 %collective-permute-done.43 = bf16[3,576,512]{2,1,0:T(8,128)(2,1)} collective-permute-done((bf16[3,576,512]{2,1,0:T(8,128)(2,1)}, bf16[3,576,512]{2,1,0:T(8,128)(2,1)}, u32[]{:S(2)}, u32[]{:S(2)}) %collective-permute-start.43) | collective-permute-done | bytes 1769504 | tf_op jit(solution)/shard_map/ppermute | solution.py:66
  1132.9 5.0 copy.155
  1138.0 7.7 reshape.215
  1145.7 15.7 %collective-permute-done.45 = bf16[2,48,2688]{2,1,0:T(8,128)(2,1)} collective-permute-done((bf16[2,48,2688]{2,1,0:T(8,128)(2,1)}, bf16[2,48,2688]{2,1,0:T(8,128)(2,1)}, u32[]{:S(2)}, u32[]{:S(2)}) %collective-permute-start.45) | collective-permute-done | bytes 516128 | tf_op jit(solution)/shard_map/ppermute | solution.py:66
  1171.9 15.2 %collective-permute-done.50 = bf16[48,2688]{1,0:T(8,128)(2,1)S(1)} collective-permute-done((bf16[48,2688]{1,0:T(8,128)(2,1)S(1)}, bf16[48,2688]{1,0:T(8,128)(2,1)S(1)}, u32[]{:S(2)}, u32[]{:S(2)}) %collective-permute-start.50) | collective-permute-done | bytes 258080 | tf_op jit(solution)/shard_map/ppermute | solution.py:66
  (408 shorter events, 263.3 us)
Async XLA Ops:
  7.2 145.3 %all-gather.2.cloned.1.call-start = ((), (), s32[]{:S(2)}) async-start(), calls=%async_computation.2 | async-start | bytes 13787136 | tf_op jit(solution)/shard_map/all_gather | solution.py:832
  11.4 948.8 %reduce-scatter.3.cloned.1.call-start = ((), (), s32[]{:S(2)}) async-start(), calls=%async_computation.3 | async-start | bytes 17694720 | tf_op jit(solution)/shard_map/reduce_scatter | solution.py:983
  20.2 129.1 %collective-permute-start = (bf16[5,576,512]{2,1,0:T(8,128)(2,1)}, bf16[5,576,512]{2,1,0:T(8,128)(2,1)}, u32[]{:S(2)}, u32[]{:S(2)}) collective-permute-start(bf16[5,576,512]{2,1,0:T(8,128)(2,1)} %pad_maximum_fusion.6), channel_id=1, source_target_pairs={{0,8},{1,9},{2,10},{3,11},{4,12},{5,13},{6,14},{7,15},{8,0},{9,1},... | collective-permute-start | bytes 8847368 | tf_op jit(solution)/shard_map/ppermute | solution.py:66
  27.2 122.1 %collective-permute-start.1 = (bf16[5,576,512]{2,1,0:T(8,128)(2,1)}, bf16[5,576,512]{2,1,0:T(8,128)(2,1)}, u32[]{:S(2)}, u32[]{:S(2)}) collective-permute-start(bf16[5,576,512]{2,1,0:T(8,128)(2,1)} %pad_maximum_fusion.5.refs_0_), channel_id=1, source_target_pairs={{0,4},{1,5},{2,6},{3,7},{4,0},{5,1},{6,2},{7,3},{8,12},{9,13},{10,... | collective-permute-start | bytes 8847368 | tf_op jit(solution)/shard_map/ppermute | solution.py:66
  35.7 44.7 %collective-permute-start.2 = (bf16[1,2,256,1664]{3,2,1,0:T(8,128)(2,1)}, bf16[1,2,256,1664]{3,2,1,0:T(8,128)(2,1)}, u32[]{:S(2)}, u32[]{:S(2)}) collective-permute-start(bf16[1,2,256,1664]{3,2,1,0:T(8,128)(2,1)} %maximum_bitcast_fusion.1), channel_id=1, source_target_pairs={{0,2},{1,3},{2,0},{3,1},{4,6},{5,7},{6,4},{7,5},{8,10},{9,11},{10,... | collective-permute-start | bytes 5111816 | tf_op jit(solution)/shard_map/ppermute | solution.py:66
  166.8 24.0 %collective-permute-start.3 = (bf16[256,1024]{1,0:T(8,128)(2,1)}, bf16[256,1024]{1,0:T(8,128)(2,1)}, u32[]{:S(2)}, u32[]{:S(2)}) collective-permute-start(bf16[256,1024]{1,0:T(8,128)(2,1)} %get-tuple-element.294), channel_id=1, source_target_pairs={{0,2},{1,3},{2,0},{3,1},{4,6},{5,7},{6,4},{7,5},{8,10},{9,11},{10,... | collective-permute-start | bytes 1572872 | tf_op jit(solution)/shard_map/ppermute | solution.py:66
  171.2 174.0 %collective-permute-start.9 = (bf16[2,2,256,1664]{3,2,1,0:T(8,128)(2,1)}, bf16[2,2,256,1664]{3,2,1,0:T(8,128)(2,1)}, u32[]{:S(2)}, u32[]{:S(2)}) collective-permute-start(bf16[2,2,256,1664]{3,2,1,0:T(8,128)(2,1)} %pad_maximum_fusion.2), channel_id=1, source_target_pairs={{0,8},{1,9},{2,10},{3,11},{4,12},{5,13},{6,14},{7,15},{8,0},{9,1},... | collective-permute-start | bytes 10223624 | tf_op jit(solution)/shard_map/ppermute | solution.py:66
  173.8 171.5 %collective-permute-start.7 = (bf16[5,576,512]{2,1,0:T(8,128)(2,1)}, bf16[5,576,512]{2,1,0:T(8,128)(2,1)}, u32[]{:S(2)}, u32[]{:S(2)}) collective-permute-start(bf16[5,576,512]{2,1,0:T(8,128)(2,1)} %pad_maximum_fusion.5.refs_0_), channel_id=1, source_target_pairs={{0,16},{1,17},{2,18},{3,19},{4,20},{5,21},{6,22},{7,23},{8,24},{9,... | collective-permute-start | bytes 8847368 | tf_op jit(solution)/shard_map/ppermute | solution.py:66
  176.3 169.0 %collective-permute-start.8 = (bf16[5,576,512]{2,1,0:T(8,128)(2,1)}, bf16[5,576,512]{2,1,0:T(8,128)(2,1)}, u32[]{:S(2)}, u32[]{:S(2)}) collective-permute-start(bf16[5,576,512]{2,1,0:T(8,128)(2,1)} %collective-permute-done.refs_1_), channel_id=1, source_target_pairs={{0,4},{1,5},{2,6},{3,7},{4,0},{5,1},{6,2},{7,3},{8,12},{9,13},{10,... | collective-permute-start | bytes 8847368 | tf_op jit(solution)/shard_map/ppermute | solution.py:66
  181.4 42.9 %collective-permute-start.6 = (bf16[2,256,1024]{2,1,0:T(8,128)(2,1)S(1)}, bf16[2,256,1024]{2,1,0:T(8,128)(2,1)S(1)}, u32[]{:S(2)}, u32[]{:S(2)}) collective-permute-start(bf16[2,256,1024]{2,1,0:T(8,128)(2,1)S(1)} %pad_maximum_fusion.16), channel_id=1, source_target_pairs={{0,1},{1,0},{2,3},{3,2},{4,5},{5,4},{6,7},{7,6},{8,9},{9,8},{10,11... | collective-permute-start | bytes 3145736 | tf_op jit(solution)/shard_map/ppermute | solution.py:66
  222.6 31.0 %collective-permute-start.10 = (bf16[256,1536]{1,0:T(8,128)(2,1)S(1)}, bf16[256,1536]{1,0:T(8,128)(2,1)}, u32[]{:S(2)}, u32[]{:S(2)}) collective-permute-start(bf16[256,1536]{1,0:T(8,128)(2,1)S(1)} %get-tuple-element.115), channel_id=1, source_target_pairs={{0,2},{1,3},{2,0},{3,1},{4,6},{5,7},{6,4},{7,5},{8,10},{9,11},{10,... | collective-permute-start | bytes 2359304 | tf_op jit(solution)/shard_map/ppermute | solution.py:66
  224.3 104.0 %collective-permute-start.11 = (bf16[256,1536]{1,0:T(8,128)(2,1)S(1)}, bf16[256,1536]{1,0:T(8,128)(2,1)}, u32[]{:S(2)}, u32[]{:S(2)}) collective-permute-start(bf16[256,1536]{1,0:T(8,128)(2,1)S(1)} %get-tuple-element.115), channel_id=1, source_target_pairs={{0,8},{1,9},{2,10},{3,11},{4,12},{5,13},{6,14},{7,15},{8,0},{9,1},... | collective-permute-start | bytes 2359304 | tf_op jit(solution)/shard_map/ppermute | solution.py:66
  253.5 90.3 %collective-permute-start.12 = (bf16[256,1536]{1,0:T(8,128)(2,1)S(1)}, bf16[256,1536]{1,0:T(8,128)(2,1)}, u32[]{:S(2)}, u32[]{:S(2)}) collective-permute-start(bf16[256,1536]{1,0:T(8,128)(2,1)S(1)} %get-tuple-element.110), channel_id=1, source_target_pairs={{0,8},{1,9},{2,10},{3,11},{4,12},{5,13},{6,14},{7,15},{8,0},{9,1},... | collective-permute-start | bytes 2359304 | tf_op jit(solution)/shard_map/ppermute | solution.py:66
  351.9 75.0 %collective-permute-start.17 = (bf16[4,2,256,1664]{3,2,1,0:T(8,128)(2,1)}, bf16[4,2,256,1664]{3,2,1,0:T(8,128)(2,1)}, u32[]{:S(2)}, u32[]{:S(2)}) collective-permute-start(bf16[4,2,256,1664]{3,2,1,0:T(8,128)(2,1)} %pad_maximum_fusion), channel_id=1, source_target_pairs={{0,1},{1,0},{2,3},{3,2},{4,5},{5,4},{6,7},{7,6},{8,9},{9,8},{10,11... | collective-permute-start | bytes 20447240 | tf_op jit(solution)/shard_map/ppermute | solution.py:66
  359.7 63.9 %collective-permute-start.14 = (bf16[256,1536]{1,0:T(8,128)(2,1)}, bf16[256,1536]{1,0:T(8,128)(2,1)S(1)}, u32[]{:S(2)}, u32[]{:S(2)}) collective-permute-start(bf16[256,1536]{1,0:T(8,128)(2,1)} %collective-permute-done.12), channel_id=1, source_target_pairs={{0,2},{1,3},{2,0},{3,1},{4,6},{5,7},{6,4},{7,5},{8,10},{9,11},{10,... | collective-permute-start | bytes 2359304 | tf_op jit(solution)/shard_map/ppermute | solution.py:66
  361.3 88.6 %collective-permute-start.15 = (bf16[5,576,512]{2,1,0:T(8,128)(2,1)}, bf16[5,576,512]{2,1,0:T(8,128)(2,1)}, u32[]{:S(2)}, u32[]{:S(2)}) collective-permute-start(bf16[5,576,512]{2,1,0:T(8,128)(2,1)} %collective-permute-done.7.refs_2_), channel_id=1, source_target_pairs={{0,4},{1,5},{2,6},{3,7},{4,0},{5,1},{6,2},{7,3},{8,12},{9,13},{10,... | collective-permute-start | bytes 8847368 | tf_op jit(solution)/shard_map/ppermute | solution.py:66
  362.8 87.1 %collective-permute-start.16 = (bf16[3,576,512]{2,1,0:T(8,128)(2,1)}, bf16[3,576,512]{2,1,0:T(8,128)(2,1)}, u32[]{:S(2)}, u32[]{:S(2)}) collective-permute-start(bf16[3,576,512]{2,1,0:T(8,128)(2,1)} %slice.295), channel_id=1, source_target_pairs={{0,16},{1,17},{2,18},{3,19},{4,20},{5,21},{6,22},{7,23},{8,24},{9,... | collective-permute-start | bytes 5308424 | tf_op jit(solution)/shard_map/ppermute | solution.py:66
  365.4 55.1 %collective-permute-start.21 = (bf16[256,1536]{1,0:T(8,128)(2,1)}, bf16[256,1536]{1,0:T(8,128)(2,1)S(1)}, u32[]{:S(2)}, u32[]{:S(2)}) collective-permute-start(bf16[256,1536]{1,0:T(8,128)(2,1)} %collective-permute-done.10), channel_id=1, source_target_pairs={{0,8},{1,9},{2,10},{3,11},{4,12},{5,13},{6,14},{7,15},{8,0},{9,1},... | collective-permute-start | bytes 2359304 | tf_op jit(solution)/shard_map/ppermute | solution.py:66
  423.6 83.5 %collective-permute-start.22 = (bf16[4,256,1536]{2,1,0:T(8,128)(2,1)}, bf16[4,256,1536]{2,1,0:T(8,128)(2,1)}, u32[]{:S(2)}, u32[]{:S(2)}) collective-permute-start(bf16[4,256,1536]{2,1,0:T(8,128)(2,1)} %pad_maximum_fusion.4), channel_id=1, source_target_pairs={{0,1},{1,0},{2,3},{3,2},{4,5},{5,4},{6,7},{7,6},{8,9},{9,8},{10,11... | collective-permute-start | bytes 9437192 | tf_op jit(solution)/shard_map/ppermute | solution.py:66
  449.9 82.5 %collective-permute-start.23 = (bf16[4,256,1536]{2,1,0:T(8,128)(2,1)}, bf16[4,256,1536]{2,1,0:T(8,128)(2,1)S(1)}, u32[]{:S(2)}, u32[]{:S(2)}) collective-permute-start(bf16[4,256,1536]{2,1,0:T(8,128)(2,1)} %pad_maximum_fusion.3), channel_id=1, source_target_pairs={{0,1},{1,0},{2,3},{3,2},{4,5},{5,4},{6,7},{7,6},{8,9},{9,8},{10,11... | collective-permute-start | bytes 9437192 | tf_op jit(solution)/shard_map/ppermute | solution.py:66
  451.0 54.3 %collective-permute-start.19 = (bf16[2,576,512]{2,1,0:T(8,128)(2,1)}, bf16[2,576,512]{2,1,0:T(8,128)(2,1)S(1)}, u32[]{:S(2)}, u32[]{:S(2)}) collective-permute-start(bf16[2,576,512]{2,1,0:T(8,128)(2,1)} %slice.296), channel_id=1, source_target_pairs={{0,16},{1,17},{2,18},{3,19},{4,20},{5,21},{6,22},{7,23},{8,24},{9,... | collective-permute-start | bytes 3538952 | tf_op jit(solution)/shard_map/ppermute | solution.py:66
  454.4 56.0 %collective-permute-start.18 = (bf16[3,576,512]{2,1,0:T(8,128)(2,1)}, bf16[3,576,512]{2,1,0:T(8,128)(2,1)S(1)}, u32[]{:S(2)}, u32[]{:S(2)}) collective-permute-start(bf16[3,576,512]{2,1,0:T(8,128)(2,1)} %collective-permute-done.16.refs_3_), channel_id=1, source_target_pairs={{0,4},{1,5},{2,6},{3,7},{4,0},{5,1},{6,2},{7,3},{8,12},{9,13},{10,... | collective-permute-start | bytes 5308424 | tf_op jit(solution)/shard_map/ppermute | solution.py:66
  505.3 27.0 %collective-permute-start.20 = (bf16[2,576,512]{2,1,0:T(8,128)(2,1)S(1)}, bf16[2,576,512]{2,1,0:T(8,128)(2,1)S(1)}, u32[]{:S(2)}, u32[]{:S(2)}) collective-permute-start(bf16[2,576,512]{2,1,0:T(8,128)(2,1)S(1)} %collective-permute-done.19.refs_3_), channel_id=1, source_target_pairs={{0,4},{1,5},{2,6},{3,7},{4,0},{5,1},{6,2},{7,3},{8,12},{9,13},{10,... | collective-permute-start | bytes 3538952 | tf_op jit(solution)/shard_map/ppermute | solution.py:66
  618.4 420.1 %reduce-scatter.5.cloned.1.call-start = ((), (), s32[]{:S(2)}) async-start(), calls=%async_computation.4 | async-start | bytes 11796480 | tf_op jit(solution)/shard_map/reduce_scatter | solution.py:983
  685.9 20.2 %collective-permute-start.24 = (bf16[4,256,1664]{2,1,0:T(8,128)(2,1)}, bf16[4,256,1664]{2,1,0:T(8,128)(2,1)}, u32[]{:S(2)}, u32[]{:S(2)}) collective-permute-start(bf16[4,256,1664]{2,1,0:T(8,128)(2,1)} %shard_map.246), channel_id=1, source_target_pairs={{0,1},{1,0},{2,3},{3,2},{4,5},{5,4},{6,7},{7,6},{8,9},{9,8},{10,11... | collective-permute-start | bytes 10223624 | tf_op jit(solution)/shard_map/ppermute | solution.py:66
  692.6 19.6 %collective-permute-start.26 = (bf16[4,256,1664]{2,1,0:T(8,128)(2,1)}, bf16[4,256,1664]{2,1,0:T(8,128)(2,1)}, u32[]{:S(2)}, u32[]{:S(2)}) collective-permute-start(bf16[4,256,1664]{2,1,0:T(8,128)(2,1)} %shard_map.248), channel_id=1, source_target_pairs={{0,1},{1,0},{2,3},{3,2},{4,5},{5,4},{6,7},{7,6},{8,9},{9,8},{10,11... | collective-permute-start | bytes 10223624 | tf_op jit(solution)/shard_map/ppermute | solution.py:66
  723.0 21.3 %collective-permute-start.28 = (bf16[4,256,1536]{2,1,0:T(8,128)(2,1)}, bf16[4,256,1536]{2,1,0:T(8,128)(2,1)}, u32[]{:S(2)}, u32[]{:S(2)}) collective-permute-start(bf16[4,256,1536]{2,1,0:T(8,128)(2,1)} %shard_map.250), channel_id=1, source_target_pairs={{0,1},{1,0},{2,3},{3,2},{4,5},{5,4},{6,7},{7,6},{8,9},{9,8},{10,11... | collective-permute-start | bytes 9437192 | tf_op jit(solution)/shard_map/ppermute | solution.py:66
  729.8 20.1 %collective-permute-start.29 = (bf16[4,256,1536]{2,1,0:T(8,128)(2,1)}, bf16[4,256,1536]{2,1,0:T(8,128)(2,1)}, u32[]{:S(2)}, u32[]{:S(2)}) collective-permute-start(bf16[4,256,1536]{2,1,0:T(8,128)(2,1)} %shard_map.252), channel_id=1, source_target_pairs={{0,1},{1,0},{2,3},{3,2},{4,5},{5,4},{6,7},{7,6},{8,9},{9,8},{10,11... | collective-permute-start | bytes 9437192 | tf_op jit(solution)/shard_map/ppermute | solution.py:66
  730.0 70.9 %collective-permute-start.25 = (bf16[2,256,1664]{2,1,0:T(8,128)(2,1)}, bf16[2,256,1664]{2,1,0:T(8,128)(2,1)}, u32[]{:S(2)}, u32[]{:S(2)}) collective-permute-start(bf16[2,256,1664]{2,1,0:T(8,128)(2,1)} %get-tuple-element.270), channel_id=1, source_target_pairs={{0,8},{1,9},{2,10},{3,11},{4,12},{5,13},{6,14},{7,15},{8,0},{9,1},... | collective-permute-start | bytes 5111816 | tf_op jit(solution)/shard_map/ppermute | solution.py:66
  730.5 70.4 %collective-permute-start.27 = (bf16[2,256,1664]{2,1,0:T(8,128)(2,1)}, bf16[2,256,1664]{2,1,0:T(8,128)(2,1)}, u32[]{:S(2)}, u32[]{:S(2)}) collective-permute-start(bf16[2,256,1664]{2,1,0:T(8,128)(2,1)} %get-tuple-element.268), channel_id=1, source_target_pairs={{0,2},{1,3},{2,0},{3,1},{4,6},{5,7},{6,4},{7,5},{8,10},{9,11},{10,... | collective-permute-start | bytes 5111816 | tf_op jit(solution)/shard_map/ppermute | solution.py:66
  803.0 20.5 %collective-permute-start.30 = (bf16[1,256,1664]{2,1,0:T(8,128)(2,1)S(1)}, bf16[1,256,1664]{2,1,0:T(8,128)(2,1)S(1)}, u32[]{:S(2)}, u32[]{:S(2)}) collective-permute-start(bf16[1,256,1664]{2,1,0:T(8,128)(2,1)S(1)} %slice.396), channel_id=1, source_target_pairs={{0,2},{1,3},{2,0},{3,1},{4,6},{5,7},{6,4},{7,5},{8,10},{9,11},{10,... | collective-permute-start | bytes 2555912 | tf_op jit(solution)/shard_map/ppermute | solution.py:66
  806.1 38.2 %collective-permute-start.31 = (bf16[1,256,1664]{2,1,0:T(8,128)(2,1)}, bf16[1,256,1664]{2,1,0:T(8,128)(2,1)S(1)}, u32[]{:S(2)}, u32[]{:S(2)}) collective-permute-start(bf16[1,256,1664]{2,1,0:T(8,128)(2,1)} %slice.398), channel_id=1, source_target_pairs={{0,8},{1,9},{2,10},{3,11},{4,12},{5,13},{6,14},{7,15},{8,0},{9,1},... | collective-permute-start | bytes 2555912 | tf_op jit(solution)/shard_map/ppermute | solution.py:66
  868.5 27.0 %collective-permute-start.32 = (bf16[2,2,2,2,48,1664]{5,4,3,2,1,0:T(8,128)(2,1)}, bf16[2,2,2,2,48,1664]{5,4,3,2,1,0:T(8,128)(2,1)S(1)}, u32[]{:S(2)}, u32[]{:S(2)}) collective-permute-start(bf16[2,2,2,2,48,1664]{5,4,3,2,1,0:T(8,128)(2,1)} %dynamic-slice_bitcast_fusion.1), channel_id=1, source_target_pairs={{0,1},{1,0},{2,3},{3,2},{4,5},{5,4},{6,7},{7,6},{8,9},{9,8},{10,11... | collective-permute-start | bytes 7667720 | tf_op jit(solution)/shard_map/ppermute | solution.py:66
  895.1 27.4 %collective-permute-start.33 = (bf16[2,256,1024]{2,1,0:T(8,128)(2,1)}, bf16[2,256,1024]{2,1,0:T(8,128)(2,1)}, u32[]{:S(2)}, u32[]{:S(2)}) collective-permute-start(bf16[2,256,1024]{2,1,0:T(8,128)(2,1)} %bitcast.75), channel_id=1, source_target_pairs={{0,1},{1,0},{2,3},{3,2},{4,5},{5,4},{6,7},{7,6},{8,9},{9,8},{10,11... | collective-permute-start | bytes 3145736 | tf_op jit(solution)/shard_map/ppermute | solution.py:66
  926.7 51.1 %collective-permute-start.37 = (bf16[2,2,2,48,1664]{4,3,2,1,0:T(8,128)(2,1)}, bf16[2,2,2,48,1664]{4,3,2,1,0:T(8,128)(2,1)}, u32[]{:S(2)}, u32[]{:S(2)}) collective-permute-start(bf16[2,2,2,48,1664]{4,3,2,1,0:T(8,128)(2,1)} %dynamic-slice_bitcast_fusion.3), channel_id=1, source_target_pairs={{0,4},{1,5},{2,6},{3,7},{4,0},{5,1},{6,2},{7,3},{8,12},{9,13},{10,... | collective-permute-start | bytes 3833864 | tf_op jit(solution)/shard_map/ppermute | solution.py:66
  928.4 21.1 %collective-permute-start.36 = (bf16[1,256,1024]{2,1,0:T(8,128)(2,1)S(1)}, bf16[1,256,1024]{2,1,0:T(8,128)(2,1)S(1)}, u32[]{:S(2)}, u32[]{:S(2)}) collective-permute-start(bf16[1,256,1024]{2,1,0:T(8,128)(2,1)S(1)} %fusion.9), channel_id=1, source_target_pairs={{0,2},{1,3},{2,0},{3,1},{4,6},{5,7},{6,4},{7,5},{8,10},{9,11},{10,... | collective-permute-start | bytes 1572872 | tf_op jit(solution)/shard_map/ppermute | solution.py:66
  994.6 19.4 %collective-permute-start.38 = (bf16[2,2,2,2,48,2688]{5,4,3,2,1,0:T(8,128)(2,1)}, bf16[2,2,2,2,48,2688]{5,4,3,2,1,0:T(8,128)(2,1)}, u32[]{:S(2)}, u32[]{:S(2)}) collective-permute-start(bf16[2,2,2,2,48,2688]{5,4,3,2,1,0:T(8,128)(2,1)} %dynamic-slice_bitcast_fusion), channel_id=1, source_target_pairs={{0,1},{1,0},{2,3},{3,2},{4,5},{5,4},{6,7},{7,6},{8,9},{9,8},{10,11... | collective-permute-start | bytes 12386312 | tf_op jit(solution)/shard_map/ppermute | solution.py:66
  1022.4 52.4 %collective-permute-start.40 = (bf16[2,2,2,48,2688]{4,3,2,1,0:T(8,128)(2,1)}, bf16[2,2,2,48,2688]{4,3,2,1,0:T(8,128)(2,1)}, u32[]{:S(2)}, u32[]{:S(2)}) collective-permute-start(bf16[2,2,2,48,2688]{4,3,2,1,0:T(8,128)(2,1)} %dynamic-slice_bitcast_fusion.2), channel_id=1, source_target_pairs={{0,2},{1,3},{2,0},{3,1},{4,6},{5,7},{6,4},{7,5},{8,10},{9,11},{10,... | collective-permute-start | bytes 6193160 | tf_op jit(solution)/shard_map/ppermute | solution.py:66
  1041.5 44.6 %collective-permute-start.44 = (bf16[2,576,512]{2,1,0:T(8,128)(2,1)}, bf16[2,576,512]{2,1,0:T(8,128)(2,1)}, u32[]{:S(2)}, u32[]{:S(2)}) collective-permute-start(bf16[2,576,512]{2,1,0:T(8,128)(2,1)} %get-tuple-element.280), channel_id=1, source_target_pairs={{0,8},{1,9},{2,10},{3,11},{4,12},{5,13},{6,14},{7,15},{8,0},{9,1},... | collective-permute-start | bytes 3538952 | tf_op jit(solution)/shard_map/ppermute | solution.py:66
  1042.8 32.1 %collective-permute-start.41 = (bf16[2,48,1664]{2,1,0:T(8,128)(2,1)S(1)}, bf16[2,48,1664]{2,1,0:T(8,128)(2,1)S(1)}, u32[]{:S(2)}, u32[]{:S(2)}) collective-permute-start(bf16[2,48,1664]{2,1,0:T(8,128)(2,1)S(1)} %dynamic-slice_bitcast_fusion.8), channel_id=1, source_target_pairs={{0,16},{1,17},{2,18},{3,19},{4,20},{5,21},{6,22},{7,23},{8,24},{9,... | collective-permute-start | bytes 958472 | tf_op jit(solution)/shard_map/ppermute | solution.py:66
  1046.8 68.6 %collective-permute-start.43 = (bf16[3,576,512]{2,1,0:T(8,128)(2,1)}, bf16[3,576,512]{2,1,0:T(8,128)(2,1)}, u32[]{:S(2)}, u32[]{:S(2)}) collective-permute-start(bf16[3,576,512]{2,1,0:T(8,128)(2,1)} %get-tuple-element.278), channel_id=1, source_target_pairs={{0,8},{1,9},{2,10},{3,11},{4,12},{5,13},{6,14},{7,15},{8,0},{9,1},... | collective-permute-start | bytes 5308424 | tf_op jit(solution)/shard_map/ppermute | solution.py:66
  1078.1 37.3 %collective-permute-start.42 = (bf16[2,2,48,2688]{3,2,1,0:T(8,128)(2,1)}, bf16[2,2,48,2688]{3,2,1,0:T(8,128)(2,1)}, u32[]{:S(2)}, u32[]{:S(2)}) collective-permute-start(bf16[2,2,48,2688]{3,2,1,0:T(8,128)(2,1)} %dynamic-slice_bitcast_fusion.4), channel_id=1, source_target_pairs={{0,4},{1,5},{2,6},{3,7},{4,0},{5,1},{6,2},{7,3},{8,12},{9,13},{10,... | collective-permute-start | bytes 3096584 | tf_op jit(solution)/shard_map/ppermute | solution.py:66
  1083.5 35.8 %collective-permute-start.51 = (bf16[48,1664]{1,0:T(8,128)(2,1)S(1)}, bf16[48,1664]{1,0:T(8,128)(2,1)S(1)}, u32[]{:S(2)}, u32[]{:S(2)}) collective-permute-start(bf16[48,1664]{1,0:T(8,128)(2,1)S(1)} %dynamic-slice_bitcast_fusion.10), channel_id=1, source_target_pairs={{0,8},{1,9},{2,10},{3,11},{4,12},{5,13},{6,14},{7,15},{8,0},{9,1},... | collective-permute-start | bytes 479240 | tf_op jit(solution)/shard_map/ppermute | solution.py:66
  1117.9 45.4 %collective-permute-start.46 = (bf16[2,256,1536]{2,1,0:T(8,128)(2,1)}, bf16[2,256,1536]{2,1,0:T(8,128)(2,1)}, u32[]{:S(2)}, u32[]{:S(2)}) collective-permute-start(bf16[2,256,1536]{2,1,0:T(8,128)(2,1)} %get-tuple-element.185), channel_id=1, source_target_pairs={{0,8},{1,9},{2,10},{3,11},{4,12},{5,13},{6,14},{7,15},{8,0},{9,1},... | collective-permute-start | bytes 4718600 | tf_op jit(solution)/shard_map/ppermute | solution.py:66
  1117.9 45.4 %collective-permute-start.47 = (bf16[2,256,1536]{2,1,0:T(8,128)(2,1)}, bf16[2,256,1536]{2,1,0:T(8,128)(2,1)}, u32[]{:S(2)}, u32[]{:S(2)}) collective-permute-start(bf16[2,256,1536]{2,1,0:T(8,128)(2,1)} %get-tuple-element.186), channel_id=1, source_target_pairs={{0,2},{1,3},{2,0},{3,1},{4,6},{5,7},{6,4},{7,5},{8,10},{9,11},{10,... | collective-permute-start | bytes 4718600 | tf_op jit(solution)/shard_map/ppermute | solution.py:66
  1123.3 38.0 %collective-permute-start.45 = (bf16[2,48,2688]{2,1,0:T(8,128)(2,1)}, bf16[2,48,2688]{2,1,0:T(8,128)(2,1)}, u32[]{:S(2)}, u32[]{:S(2)}) collective-permute-start(bf16[2,48,2688]{2,1,0:T(8,128)(2,1)} %dynamic-slice_bitcast_fusion.7), channel_id=1, source_target_pairs={{0,16},{1,17},{2,18},{3,19},{4,20},{5,21},{6,22},{7,23},{8,24},{9,... | collective-permute-start | bytes 1548296 | tf_op jit(solution)/shard_map/ppermute | solution.py:66
  1165.1 24.2 %collective-permute-start.49 = (bf16[1,256,1536]{2,1,0:T(8,128)(2,1)S(1)}, bf16[1,256,1536]{2,1,0:T(8,128)(2,1)S(1)}, u32[]{:S(2)}, u32[]{:S(2)}) collective-permute-start(bf16[1,256,1536]{2,1,0:T(8,128)(2,1)S(1)} %slice.407), channel_id=1, source_target_pairs={{0,8},{1,9},{2,10},{3,11},{4,12},{5,13},{6,14},{7,15},{8,0},{9,1},... | collective-permute-start | bytes 2359304 | tf_op jit(solution)/shard_map/ppermute | solution.py:66
  1167.2 19.9 %collective-permute-start.50 = (bf16[48,2688]{1,0:T(8,128)(2,1)S(1)}, bf16[48,2688]{1,0:T(8,128)(2,1)S(1)}, u32[]{:S(2)}, u32[]{:S(2)}) collective-permute-start(bf16[48,2688]{1,0:T(8,128)(2,1)S(1)} %dynamic-slice_bitcast_fusion.9), channel_id=1, source_target_pairs={{0,8},{1,9},{2,10},{3,11},{4,12},{5,13},{6,14},{7,15},{8,0},{9,1},... | collective-permute-start | bytes 774152 | tf_op jit(solution)/shard_map/ppermute | solution.py:66
  (86 other events, 2202.1 us)
Sparse Core Ops, SparseCore 0:
  11.5 140.9 all-gather.1
  618.5 246.1 reduce-scatter.2
  867.8 170.5 reduce-scatter.4

commit v3 on v2

--- a/solution.py
+++ b/solution.py
@@ -1038,22 +1038,10 @@
     def tall(parts):
         return jnp.concatenate(parts, axis=0)
 
-    early = weight_grads(
-        [tall(attended), tall(normed_two)],
-        [tall(branch_grads), tall(router_grads)],
-        sum(gain_two_grads),
-        width + LANES,
-    )
-    along_z = [("dp", bit) for bit in reversed(range(1, dp_bits))]
-    along_x = [("dp", 0)] if dp_bits else []
-    home_two = Homeward(early, [("expert", 0)] + along_x + row_places + along_z)
-    head_grads[0], early = after(head_grads[0], early)
-
     query_grads, pair_grads = [], []
     for index in range(micro_count):
         if index == micro_count - 1:
             attend_places[index], query_grads[0] = after(attend_places[index], query_grads[0])
-            attend_places[index] = home_two.pin(attend_places[index])
         dq, pairs = attend_back(
             attend_places[index], queries[index], key_rows[index], head_grads[index],
             attended[index], log_totals[index], cos_t, sin_t,
@@ -1062,9 +1050,20 @@
         middle_point = owner_count // 2
         pair_grads.append(sum_home(pairs[:middle_point], pairs[middle_point:], key_places)[0])
         query_grads.append(dq)
+    branch_grads[0], query_grads[-1] = after(branch_grads[0], query_grads[-1])
+    early = weight_grads(
+        [tall(attended), tall(normed_two)],
+        [tall(branch_grads), tall(router_grads)],
+        sum(gain_two_grads),
+        width + LANES,
+    )
+    along_z = [("dp", bit) for bit in reversed(range(1, dp_bits))]
+    along_x = [("dp", 0)] if dp_bits else []
+    home_two = Homeward(early, [("expert", 0)] + along_x + row_places + along_z)
+
     normed_all = normed.reshape(micro_count * tokens, width)
 
-    pair_grads[0], summed[0] = after(pair_grads[0], summed[0])
+    pair_grads[0], summed[0], early = after(pair_grads[0], summed[0], early)
     other = [swap(summed[0][1], dp_places[0])]
     key_grads, input_grads, gain_one_grads = [], [], []
     for index in range(micro_count):
@@ -1084,20 +1083,22 @@
     )
     home_one = Homeward(late, [("expert", 0)] + row_places + along_x + along_z)
     other.append(swap(summed[1][1], dp_places[0]))
-    home_one.received, home_two.received = after(home_one.received, home_two.received)
     home_one.join()
-    home_two.join()
-    home_one.received, home_two.received = after(home_one.received, home_two.received)
     home_one.join()
-    home_two.join()
     highs = after(home_one.held, *[pair[1] for pair in mixed])[1:]
     mix_received = [
         swap(highs[index], token_places[index][-2]) for index in range(micro_count)
     ]
-    home_one.received, *other = after(home_one.received, *other)
+    home_one.received, home_two.received, other[0], *mix_received = after(
+        home_one.received, home_two.received, other[0], *mix_received
+    )
     home_one.join()
-    home_one.received, *mix_received = after(home_one.received, *mix_received)
+    home_two.join()
+    home_one.received, home_two.received, other[1] = after(
+        home_one.received, home_two.received, other[1]
+    )
     home_one.join()
+    home_two.join()
     mixtures = []
     for index in range(micro_count):
         total = add_rounded(mixed[index][0], mix_received[index])

time: 1210 us -> 1190 us (0.983)
    reduce_scatter x2, waiting for transfers between devices: 14.7 us -> 1.38 us  [shards(): lax.psum_scatter(grads, 'dp', scatter_dimension=0, axis_index_groups=grou...]
    unnamed x182 -> x202, local copies, waits for them, and re-layouts: 45.3 us -> 46.3 us
  transfers between devices with their start and end apart: 55 -> 55, of which waited for: 25 -> 25; matrix products, arithmetic and copies ran while one was open for 16% -> 15% of each run, Pallas kernels for 21% -> 22%
where the time goes in v3:
time: 1190 us; the launch traced here: 1180 us
  waiting for transfers between devices  547 us (46%)
  Pallas kernels  343 us (29%)
  local copies, waits for them, and re-layouts  113 us (9%)
  other arithmetic  106 us (9%)
  starting transfers between devices  47.3 us (4%)
  between operations  15.4 us (1%)
    ppermute x52, waiting for transfers between devices, swap(): lax.ppermute(array, AXES, [(i, i ^ flip) for i in range(dp_count * owner_...  542 us
    pallas_call x2, Pallas kernels, run_experts(): pl.pallas_call(functools.partial(expert_kernel, masks, sources, pair_bit,...  135 us
    pallas_call x8, Pallas kernels, combine(): pl.pallas_call(combine_kernel, grid=(size,), in_specs=[pl.BlockSpec((1, l...  52.2 us
    pallas_call x2, Pallas kernels, attend_back(): pl.pallas_call(attend_back_kernel, grid_spec=pltpu.PrefetchScalarGridSpec...  47.3 us
    ppermute x52, starting transfers between devices, swap(): lax.ppermute(array, AXES, [(i, i ^ flip) for i in range(dp_count * owner_...  47.1 us
    unnamed x202, local copies, waits for them, and re-layouts  46.3 us
    convert_element_type x18, other arithmetic, add_rounded(): return (left.astype(F32) + right.astype(F32)).astype(left.dtype)  40.5 us
    pallas_call x2, Pallas kernels, attend(): pl.pallas_call(attend_kernel, grid_spec=pltpu.PrefetchScalarGridSpec(num_...  37.8 us
  transfers between devices with their start and end apart: 55, of which 25 were waited for; matrix products, arithmetic and copies ran while one was open for 15% of the time, Pallas kernels for 22%

profile of v3, /device:TPU:0, one launch (start us, length us, event | category | flops | bytes accessed | tf_op | source)
XLA Modules:
  0.0 1178.8 jit_solution(3020386842706090263)
XLA Ops:
  40.6 39.5 %collective-permute-done.2 = bf16[1,2,256,1664]{3,2,1,0:T(8,128)(2,1)} collective-permute-done((bf16[1,2,256,1664]{3,2,1,0:T(8,128)(2,1)S(1)}, bf16[1,2,256,1664]{3,2,1,0:T(8,128)(2,1)}, u32[]{:S(2)}, u32[]{:S(2)}) %collective-permute-start.2) | collective-permute-done | bytes 1703968 | tf_op jit(solution)/shard_map/ppermute | solution.py:66
  80.2 69.1 %collective-permute-done.refs_1_ = bf16[5,576,512]{2,1,0:T(8,128)(2,1)} collective-permute-done((bf16[5,576,512]{2,1,0:T(8,128)(2,1)}, bf16[5,576,512]{2,1,0:T(8,128)(2,1)}, u32[]{:S(2)}, u32[]{:S(2)}) %collective-permute-start) | collective-permute-done | bytes 2949152 | tf_op jit(solution)/shard_map/ppermute | solution.py:66
  154.1 9.6 shard_map.238
  181.8 9.2 collective-permute-done.3
  196.2 19.1 %shard_map.239 = (bf16[256,1536]{1,0:T(8,128)(2,1)S(1)}, f32[4,8,256]{2,1,0:T(8,128)S(1)}) custom-call(s32[6]{0:T(128)S(1)} %concatenate.92.places_ref, bf16[256,1536]{1,0:T(8,128)(2,1)S(1)} %get-tuple-element.281.q_ref, bf16[1024,1024]{1,0:T(8,128)(2,1)S(1)} %bitcast.233, bf16[1024,1024]{1,0:T(8,128)(2,1)S(1)} %bitcast.234), custom_call_target="tpu_custom_call" | custom-call | flops 570000000 | tf_op jit(solution)/shard_map/pallas_call | solution.py:424
  229.5 18.7 %shard_map.241 = (bf16[256,1536]{1,0:T(8,128)(2,1)S(1)}, f32[4,8,256]{2,1,0:T(8,128)S(1)}) custom-call(s32[6]{0:T(128)S(1)} %concatenate.102.places_ref, bf16[256,1536]{1,0:T(8,128)(2,1)S(1)} %get-tuple-element.282.q_ref, bf16[1024,1024]{1,0:T(8,128)(2,1)S(1)} %bitcast.237, bf16[1024,1024]{1,0:T(8,128)(2,1)S(1)} %bitcast.238), custom_call_target="tpu_custom_call" | custom-call | flops 570000000 | tf_op jit(solution)/shard_map/pallas_call | solution.py:424
  255.9 72.0 %collective-permute-done.11 = bf16[256,1536]{1,0:T(8,128)(2,1)} collective-permute-done((bf16[256,1536]{1,0:T(8,128)(2,1)S(1)}, bf16[256,1536]{1,0:T(8,128)(2,1)}, u32[]{:S(2)}, u32[]{:S(2)}) %collective-permute-start.11) | collective-permute-done | bytes 786464 | tf_op jit(solution)/shard_map/ppermute | solution.py:66
  329.6 13.8 %collective-permute-done.12 = bf16[256,1536]{1,0:T(8,128)(2,1)S(1)} collective-permute-done((bf16[256,1536]{1,0:T(8,128)(2,1)S(1)}, bf16[256,1536]{1,0:T(8,128)(2,1)S(1)}, u32[]{:S(2)}, u32[]{:S(2)}) %collective-permute-start.12) | collective-permute-done | bytes 786464 | tf_op jit(solution)/shard_map/ppermute | solution.py:66
  344.9 6.1 pad_maximum_fusion
  368.5 51.2 %collective-permute-done.21 = bf16[256,1536]{1,0:T(8,128)(2,1)S(1)} collective-permute-done((bf16[256,1536]{1,0:T(8,128)(2,1)}, bf16[256,1536]{1,0:T(8,128)(2,1)S(1)}, u32[]{:S(2)}, u32[]{:S(2)}) %collective-permute-start.21) | collective-permute-done | bytes 786464 | tf_op jit(solution)/shard_map/ppermute | solution.py:66
  439.2 4.8 copy-done.28
  453.6 48.4 %collective-permute-done.19.refs_3_ = bf16[2,576,512]{2,1,0:T(8,128)(2,1)S(1)} collective-permute-done((bf16[2,576,512]{2,1,0:T(8,128)(2,1)}, bf16[2,576,512]{2,1,0:T(8,128)(2,1)S(1)}, u32[]{:S(2)}, u32[]{:S(2)}) %collective-permute-start.19) | collective-permute-done | bytes 1179680 | tf_op jit(solution)/shard_map/ppermute | solution.py:66
  507.1 21.9 %collective-permute-done.20.refs_7_ = bf16[2,576,512]{2,1,0:T(8,128)(2,1)S(1)} collective-permute-done((bf16[2,576,512]{2,1,0:T(8,128)(2,1)S(1)}, bf16[2,576,512]{2,1,0:T(8,128)(2,1)S(1)}, u32[]{:S(2)}, u32[]{:S(2)}) %collective-permute-start.20) | collective-permute-done | bytes 1179680 | tf_op jit(solution)/shard_map/ppermute | solution.py:66
  530.1 6.5 select_reduce_fusion
  538.5 79.5 %shard_map.243 = (bf16[16,5,64,1536]{3,2,1,0:T(8,128)(2,1)}, bf16[16,5,64,1664]{3,2,1,0:T(8,128)(2,1)}, bf16[4,2,3,576,512]{4,3,2,1,0:T(8,128)(2,1)}) custom-call(s32[2]{0:T(128)} %pad_add_fusion.me_ref, bf16[5,576,512]{2,1,0:T(8,128)(2,1)} %pad_maximum_fusion.5.refs_0_, bf16[5,576,512]{2,1,0:T(8,128)(2,1)} %collective-permute-done.refs_1_, ...), custom_call_target="tpu_custom_call" | custom-call | flops 2790000128 | tf_op jit(solution)/shard_map/pallas_call | solution.py:694
  623.3 55.7 %shard_map.244 = (bf16[16,5,64,1536]{3,2,1,0:T(8,128)(2,1)}, bf16[16,5,64,1664]{3,2,1,0:T(8,128)(2,1)}, bf16[4,2,2,576,512]{4,3,2,1,0:T(8,128)(2,1)}) custom-call(s32[2]{0:T(128)} %pad_add_fusion.me_ref, bf16[5,576,512]{2,1,0:T(8,128)(2,1)} %pad_maximum_fusion.5.refs_0_, ...), custom_call_target="tpu_custom_call", output_to_operand_aliasing={{0}: (13, {}), {1}: (14, {})} | custom-call | flops 1860000000 | tf_op jit(solution)/shard_map/pallas_call | solution.py:694
  679.0 6.8 shard_map.246
  685.8 6.6 shard_map.248
  692.9 6.5 shard_map.245
  699.4 6.7 shard_map.247
  706.1 6.1 add_convert_fusion.3
  716.7 6.3 shard_map.250
  723.3 6.5 shard_map.252
  733.3 6.4 shard_map.249
  739.7 6.5 shard_map.251
  746.2 5.6 add_convert_fusion.10
  751.7 4.9 add_convert_fusion.8
  756.6 44.2 %collective-permute-done.25 = bf16[2,256,1664]{2,1,0:T(8,128)(2,1)} collective-permute-done((bf16[2,256,1664]{2,1,0:T(8,128)(2,1)}, bf16[2,256,1664]{2,1,0:T(8,128)(2,1)}, u32[]{:S(2)}, u32[]{:S(2)}) %collective-permute-start.25) | collective-permute-done | bytes 1703968 | tf_op jit(solution)/shard_map/ppermute | solution.py:66
  806.3 17.4 %collective-permute-done.30 = bf16[1,256,1664]{2,1,0:T(8,128)(2,1)S(1)} collective-permute-done((bf16[1,256,1664]{2,1,0:T(8,128)(2,1)S(1)}, bf16[1,256,1664]{2,1,0:T(8,128)(2,1)S(1)}, u32[]{:S(2)}, u32[]{:S(2)}) %collective-permute-start.30) | collective-permute-done | bytes 852000 | tf_op jit(solution)/shard_map/ppermute | solution.py:66
  824.9 6.6 shard_map.253
  831.4 23.4 %shard_map.254 = (bf16[256,1536]{1,0:T(8,128)(2,1)}, bf16[1024,1024]{1,0:T(8,128)(2,1)}) custom-call(s32[6]{0:T(128)} %copy-done.25, bf16[256,1536]{1,0:T(8,128)(2,1)} %copy-done.5, bf16[1024,1024]{1,0:T(8,128)(2,1)} %bitcast.235, bf16[1024,1024]{1,0:T(8,128)(2,1)} %bitcast.236, bf16[256,1536]{1,0:T(8,128)(2,1)} %get-tuple-element.141.do_ref, ...), custom_call_target="tpu_custom_call" | custom-call | flops 705000000 | tf_op jit(solution)/shard_map/pallas_call | solution.py:502
  856.0 6.6 shard_map.255
  862.6 23.9 %shard_map.256 = (bf16[256,1536]{1,0:T(8,128)(2,1)}, bf16[1024,1024]{1,0:T(8,128)(2,1)}) custom-call(s32[6]{0:T(128)} %copy-done.26, bf16[256,1536]{1,0:T(8,128)(2,1)} %copy-done.4, bf16[1024,1024]{1,0:T(8,128)(2,1)} %bitcast.239, bf16[1024,1024]{1,0:T(8,128)(2,1)} %bitcast.240, bf16[256,1536]{1,0:T(8,128)(2,1)} %get-tuple-element.151.do_ref, ...), custom_call_target="tpu_custom_call" | custom-call | flops 705000000 | tf_op jit(solution)/shard_map/pallas_call | solution.py:502
  889.1 7.9 shard_map.257
  901.3 5.1 collective-permute-done.34
  910.2 11.2 collective-permute-done.35
  922.5 10.1 shard_map.259
  934.8 9.9 shard_map.258
  948.5 10.8 shard_map.260
  959.3 4.7 dynamic-slice_bitcast_fusion
  964.1 7.4 collective-permute-done.37
  982.9 43.8 %collective-permute-done.38 = bf16[2,2,2,48,2688]{4,3,2,1,0:T(8,128)(2,1)} collective-permute-done((bf16[2,2,2,48,2688]{4,3,2,1,0:T(8,128)(2,1)}, bf16[2,2,2,48,2688]{4,3,2,1,0:T(8,128)(2,1)}, u32[]{:S(2)}, u32[]{:S(2)}) %collective-permute-start.38) | collective-permute-done | bytes 2064416 | tf_op jit(solution)/shard_map/ppermute | solution.py:66
  1041.5 23.5 %collective-permute-done.40 = bf16[2,2,2,48,1664]{4,3,2,1,0:T(8,128)(2,1)} collective-permute-done((bf16[2,2,2,48,1664]{4,3,2,1,0:T(8,128)(2,1)}, bf16[2,2,2,48,1664]{4,3,2,1,0:T(8,128)(2,1)}, u32[]{:S(2)}, u32[]{:S(2)}) %collective-permute-start.40) | collective-permute-done | bytes 1277984 | tf_op jit(solution)/shard_map/ppermute | solution.py:66
  1066.3 19.1 %collective-permute-done.39 = bf16[2,2,48,2688]{3,2,1,0:T(8,128)(2,1)} collective-permute-done((bf16[2,2,48,2688]{3,2,1,0:T(8,128)(2,1)}, bf16[2,2,48,2688]{3,2,1,0:T(8,128)(2,1)}, u32[]{:S(2)}, u32[]{:S(2)}) %collective-permute-start.39) | collective-permute-done | bytes 1032224 | tf_op jit(solution)/shard_map/ppermute | solution.py:66
  1097.6 21.7 %collective-permute-done.48 = bf16[2,576,512]{2,1,0:T(8,128)(2,1)S(1)} collective-permute-done((bf16[2,576,512]{2,1,0:T(8,128)(2,1)S(1)}, bf16[2,576,512]{2,1,0:T(8,128)(2,1)S(1)}, u32[]{:S(2)}, u32[]{:S(2)}) %collective-permute-start.48) | collective-permute-done | bytes 1179680 | tf_op jit(solution)/shard_map/ppermute | solution.py:66
  1119.3 13.7 %collective-permute-done.46 = bf16[2,48,2688]{2,1,0:T(8,128)(2,1)S(1)} collective-permute-done((bf16[2,48,2688]{2,1,0:T(8,128)(2,1)S(1)}, bf16[2,48,2688]{2,1,0:T(8,128)(2,1)S(1)}, u32[]{:S(2)}, u32[]{:S(2)}) %collective-permute-start.46) | collective-permute-done | bytes 516128 | tf_op jit(solution)/shard_map/ppermute | solution.py:66
  1145.5 5.0 copy.155
  1150.5 7.8 reshape.215
  (428 shorter events, 245.8 us)
Async XLA Ops:
  7.2 145.3 %all-gather.2.cloned.1.call-start = ((), (), s32[]{:S(2)}) async-start(), calls=%async_computation.2 | async-start | bytes 13787136 | tf_op jit(solution)/shard_map/all_gather | solution.py:832
  11.4 923.3 %reduce-scatter.3.cloned.1.call-start = ((), (), s32[]{:S(2)}) async-start(), calls=%async_computation.3 | async-start | bytes 17694720 | tf_op jit(solution)/shard_map/reduce_scatter | solution.py:983
  20.2 129.1 %collective-permute-start = (bf16[5,576,512]{2,1,0:T(8,128)(2,1)}, bf16[5,576,512]{2,1,0:T(8,128)(2,1)}, u32[]{:S(2)}, u32[]{:S(2)}) collective-permute-start(bf16[5,576,512]{2,1,0:T(8,128)(2,1)} %pad_maximum_fusion.6), channel_id=1, source_target_pairs={{0,8},{1,9},{2,10},{3,11},{4,12},{5,13},{6,14},{7,15},{8,0},{9,1},... | collective-permute-start | bytes 8847368 | tf_op jit(solution)/shard_map/ppermute | solution.py:66
  27.2 122.1 %collective-permute-start.1 = (bf16[5,576,512]{2,1,0:T(8,128)(2,1)}, bf16[5,576,512]{2,1,0:T(8,128)(2,1)}, u32[]{:S(2)}, u32[]{:S(2)}) collective-permute-start(bf16[5,576,512]{2,1,0:T(8,128)(2,1)} %pad_maximum_fusion.5.refs_0_), channel_id=1, source_target_pairs={{0,4},{1,5},{2,6},{3,7},{4,0},{5,1},{6,2},{7,3},{8,12},{9,13},{10,... | collective-permute-start | bytes 8847368 | tf_op jit(solution)/shard_map/ppermute | solution.py:66
  35.6 44.6 %collective-permute-start.2 = (bf16[1,2,256,1664]{3,2,1,0:T(8,128)(2,1)S(1)}, bf16[1,2,256,1664]{3,2,1,0:T(8,128)(2,1)}, u32[]{:S(2)}, u32[]{:S(2)}) collective-permute-start(bf16[1,2,256,1664]{3,2,1,0:T(8,128)(2,1)S(1)} %maximum_bitcast_fusion.1), channel_id=1, source_target_pairs={{0,2},{1,3},{2,0},{3,1},{4,6},{5,7},{6,4},{7,5},{8,10},{9,11},{10,... | collective-permute-start | bytes 5111816 | tf_op jit(solution)/shard_map/ppermute | solution.py:66
  167.0 24.0 %collective-permute-start.3 = (bf16[256,1024]{1,0:T(8,128)(2,1)}, bf16[256,1024]{1,0:T(8,128)(2,1)}, u32[]{:S(2)}, u32[]{:S(2)}) collective-permute-start(bf16[256,1024]{1,0:T(8,128)(2,1)} %get-tuple-element.288), channel_id=1, source_target_pairs={{0,2},{1,3},{2,0},{3,1},{4,6},{5,7},{6,4},{7,5},{8,10},{9,11},{10,... | collective-permute-start | bytes 1572872 | tf_op jit(solution)/shard_map/ppermute | solution.py:66
  170.9 174.0 %collective-permute-start.9 = (bf16[2,2,256,1664]{3,2,1,0:T(8,128)(2,1)}, bf16[2,2,256,1664]{3,2,1,0:T(8,128)(2,1)}, u32[]{:S(2)}, u32[]{:S(2)}) collective-permute-start(bf16[2,2,256,1664]{3,2,1,0:T(8,128)(2,1)} %pad_maximum_fusion.2), channel_id=1, source_target_pairs={{0,8},{1,9},{2,10},{3,11},{4,12},{5,13},{6,14},{7,15},{8,0},{9,1},... | collective-permute-start | bytes 10223624 | tf_op jit(solution)/shard_map/ppermute | solution.py:66
  173.4 171.5 %collective-permute-start.7 = (bf16[5,576,512]{2,1,0:T(8,128)(2,1)}, bf16[5,576,512]{2,1,0:T(8,128)(2,1)}, u32[]{:S(2)}, u32[]{:S(2)}) collective-permute-start(bf16[5,576,512]{2,1,0:T(8,128)(2,1)} %pad_maximum_fusion.5.refs_0_), channel_id=1, source_target_pairs={{0,16},{1,17},{2,18},{3,19},{4,20},{5,21},{6,22},{7,23},{8,24},{9,... | collective-permute-start | bytes 8847368 | tf_op jit(solution)/shard_map/ppermute | solution.py:66
  175.9 169.0 %collective-permute-start.8 = (bf16[5,576,512]{2,1,0:T(8,128)(2,1)}, bf16[5,576,512]{2,1,0:T(8,128)(2,1)}, u32[]{:S(2)}, u32[]{:S(2)}) collective-permute-start(bf16[5,576,512]{2,1,0:T(8,128)(2,1)} %collective-permute-done.refs_1_), channel_id=1, source_target_pairs={{0,4},{1,5},{2,6},{3,7},{4,0},{5,1},{6,2},{7,3},{8,12},{9,13},{10,... | collective-permute-start | bytes 8847368 | tf_op jit(solution)/shard_map/ppermute | solution.py:66
  181.7 43.8 %collective-permute-start.6 = (bf16[2,256,1024]{2,1,0:T(8,128)(2,1)S(1)}, bf16[2,256,1024]{2,1,0:T(8,128)(2,1)S(1)}, u32[]{:S(2)}, u32[]{:S(2)}) collective-permute-start(bf16[2,256,1024]{2,1,0:T(8,128)(2,1)S(1)} %pad_maximum_fusion.16), channel_id=1, source_target_pairs={{0,1},{1,0},{2,3},{3,2},{4,5},{5,4},{6,7},{7,6},{8,9},{9,8},{10,11... | collective-permute-start | bytes 3145736 | tf_op jit(solution)/shard_map/ppermute | solution.py:66
  223.8 31.1 %collective-permute-start.10 = (bf16[256,1536]{1,0:T(8,128)(2,1)S(1)}, bf16[256,1536]{1,0:T(8,128)(2,1)}, u32[]{:S(2)}, u32[]{:S(2)}) collective-permute-start(bf16[256,1536]{1,0:T(8,128)(2,1)S(1)} %get-tuple-element.112), channel_id=1, source_target_pairs={{0,2},{1,3},{2,0},{3,1},{4,6},{5,7},{6,4},{7,5},{8,10},{9,11},{10,... | collective-permute-start | bytes 2359304 | tf_op jit(solution)/shard_map/ppermute | solution.py:66
  225.5 102.4 %collective-permute-start.11 = (bf16[256,1536]{1,0:T(8,128)(2,1)S(1)}, bf16[256,1536]{1,0:T(8,128)(2,1)}, u32[]{:S(2)}, u32[]{:S(2)}) collective-permute-start(bf16[256,1536]{1,0:T(8,128)(2,1)S(1)} %get-tuple-element.112), channel_id=1, source_target_pairs={{0,8},{1,9},{2,10},{3,11},{4,12},{5,13},{6,14},{7,15},{8,0},{9,1},... | collective-permute-start | bytes 2359304 | tf_op jit(solution)/shard_map/ppermute | solution.py:66
  254.9 88.5 %collective-permute-start.12 = (bf16[256,1536]{1,0:T(8,128)(2,1)S(1)}, bf16[256,1536]{1,0:T(8,128)(2,1)S(1)}, u32[]{:S(2)}, u32[]{:S(2)}) collective-permute-start(bf16[256,1536]{1,0:T(8,128)(2,1)S(1)} %get-tuple-element.107), channel_id=1, source_target_pairs={{0,8},{1,9},{2,10},{3,11},{4,12},{5,13},{6,14},{7,15},{8,0},{9,1},... | collective-permute-start | bytes 2359304 | tf_op jit(solution)/shard_map/ppermute | solution.py:66
  327.9 17.0 %collective-permute-start.13 = (bf16[256,1536]{1,0:T(8,128)(2,1)S(1)}, bf16[256,1536]{1,0:T(8,128)(2,1)S(1)}, u32[]{:S(2)}, u32[]{:S(2)}) collective-permute-start(bf16[256,1536]{1,0:T(8,128)(2,1)S(1)} %get-tuple-element.107), channel_id=1, source_target_pairs={{0,2},{1,3},{2,0},{3,1},{4,6},{5,7},{6,4},{7,5},{8,10},{9,11},{10,... | collective-permute-start | bytes 2359304 | tf_op jit(solution)/shard_map/ppermute | solution.py:66
  351.0 74.0 %collective-permute-start.17 = (bf16[4,2,256,1664]{3,2,1,0:T(8,128)(2,1)}, bf16[4,2,256,1664]{3,2,1,0:T(8,128)(2,1)}, u32[]{:S(2)}, u32[]{:S(2)}) collective-permute-start(bf16[4,2,256,1664]{3,2,1,0:T(8,128)(2,1)} %pad_maximum_fusion), channel_id=1, source_target_pairs={{0,1},{1,0},{2,3},{3,2},{4,5},{5,4},{6,7},{7,6},{8,9},{9,8},{10,11... | collective-permute-start | bytes 20447240 | tf_op jit(solution)/shard_map/ppermute | solution.py:66
  358.8 64.2 %collective-permute-start.14 = (bf16[256,1536]{1,0:T(8,128)(2,1)S(1)}, bf16[256,1536]{1,0:T(8,128)(2,1)S(1)}, u32[]{:S(2)}, u32[]{:S(2)}) collective-permute-start(bf16[256,1536]{1,0:T(8,128)(2,1)S(1)} %collective-permute-done.12), channel_id=1, source_target_pairs={{0,2},{1,3},{2,0},{3,1},{4,6},{5,7},{6,4},{7,5},{8,10},{9,11},{10,... | collective-permute-start | bytes 2359304 | tf_op jit(solution)/shard_map/ppermute | solution.py:66
  360.4 86.1 %collective-permute-start.15 = (bf16[5,576,512]{2,1,0:T(8,128)(2,1)}, bf16[5,576,512]{2,1,0:T(8,128)(2,1)}, u32[]{:S(2)}, u32[]{:S(2)}) collective-permute-start(bf16[5,576,512]{2,1,0:T(8,128)(2,1)} %collective-permute-done.7.refs_2_), channel_id=1, source_target_pairs={{0,4},{1,5},{2,6},{3,7},{4,0},{5,1},{6,2},{7,3},{8,12},{9,13},{10,... | collective-permute-start | bytes 8847368 | tf_op jit(solution)/shard_map/ppermute | solution.py:66
  361.9 84.6 %collective-permute-start.16 = (bf16[3,576,512]{2,1,0:T(8,128)(2,1)}, bf16[3,576,512]{2,1,0:T(8,128)(2,1)}, u32[]{:S(2)}, u32[]{:S(2)}) collective-permute-start(bf16[3,576,512]{2,1,0:T(8,128)(2,1)} %slice.295), channel_id=1, source_target_pairs={{0,16},{1,17},{2,18},{3,19},{4,20},{5,21},{6,22},{7,23},{8,24},{9,... | collective-permute-start | bytes 5308424 | tf_op jit(solution)/shard_map/ppermute | solution.py:66
  364.5 55.1 %collective-permute-start.21 = (bf16[256,1536]{1,0:T(8,128)(2,1)}, bf16[256,1536]{1,0:T(8,128)(2,1)S(1)}, u32[]{:S(2)}, u32[]{:S(2)}) collective-permute-start(bf16[256,1536]{1,0:T(8,128)(2,1)} %collective-permute-done.10), channel_id=1, source_target_pairs={{0,8},{1,9},{2,10},{3,11},{4,12},{5,13},{6,14},{7,15},{8,0},{9,1},... | collective-permute-start | bytes 2359304 | tf_op jit(solution)/shard_map/ppermute | solution.py:66
  423.0 80.8 %collective-permute-start.22 = (bf16[4,256,1536]{2,1,0:T(8,128)(2,1)}, bf16[4,256,1536]{2,1,0:T(8,128)(2,1)}, u32[]{:S(2)}, u32[]{:S(2)}) collective-permute-start(bf16[4,256,1536]{2,1,0:T(8,128)(2,1)} %pad_maximum_fusion.4), channel_id=1, source_target_pairs={{0,1},{1,0},{2,3},{3,2},{4,5},{5,4},{6,7},{7,6},{8,9},{9,8},{10,11... | collective-permute-start | bytes 9437192 | tf_op jit(solution)/shard_map/ppermute | solution.py:66
  446.6 82.5 %collective-permute-start.23 = (bf16[4,256,1536]{2,1,0:T(8,128)(2,1)}, bf16[4,256,1536]{2,1,0:T(8,128)(2,1)S(1)}, u32[]{:S(2)}, u32[]{:S(2)}) collective-permute-start(bf16[4,256,1536]{2,1,0:T(8,128)(2,1)} %pad_maximum_fusion.3), channel_id=1, source_target_pairs={{0,1},{1,0},{2,3},{3,2},{4,5},{5,4},{6,7},{7,6},{8,9},{9,8},{10,11... | collective-permute-start | bytes 9437192 | tf_op jit(solution)/shard_map/ppermute | solution.py:66
  447.7 54.3 %collective-permute-start.19 = (bf16[2,576,512]{2,1,0:T(8,128)(2,1)}, bf16[2,576,512]{2,1,0:T(8,128)(2,1)S(1)}, u32[]{:S(2)}, u32[]{:S(2)}) collective-permute-start(bf16[2,576,512]{2,1,0:T(8,128)(2,1)} %slice.296), channel_id=1, source_target_pairs={{0,16},{1,17},{2,18},{3,19},{4,20},{5,21},{6,22},{7,23},{8,24},{9,... | collective-permute-start | bytes 3538952 | tf_op jit(solution)/shard_map/ppermute | solution.py:66
  451.8 55.3 %collective-permute-start.18 = (bf16[3,576,512]{2,1,0:T(8,128)(2,1)}, bf16[3,576,512]{2,1,0:T(8,128)(2,1)S(1)}, u32[]{:S(2)}, u32[]{:S(2)}) collective-permute-start(bf16[3,576,512]{2,1,0:T(8,128)(2,1)} %collective-permute-done.16.refs_3_), channel_id=1, source_target_pairs={{0,4},{1,5},{2,6},{3,7},{4,0},{5,1},{6,2},{7,3},{8,12},{9,13},{10,... | collective-permute-start | bytes 5308424 | tf_op jit(solution)/shard_map/ppermute | solution.py:66
  502.0 27.1 %collective-permute-start.20 = (bf16[2,576,512]{2,1,0:T(8,128)(2,1)S(1)}, bf16[2,576,512]{2,1,0:T(8,128)(2,1)S(1)}, u32[]{:S(2)}, u32[]{:S(2)}) collective-permute-start(bf16[2,576,512]{2,1,0:T(8,128)(2,1)S(1)} %collective-permute-done.19.refs_3_), channel_id=1, source_target_pairs={{0,4},{1,5},{2,6},{3,7},{4,0},{5,1},{6,2},{7,3},{8,12},{9,13},{10,... | collective-permute-start | bytes 3538952 | tf_op jit(solution)/shard_map/ppermute | solution.py:66
  618.1 419.0 %reduce-scatter.5.cloned.1.call-start = ((), (), s32[]{:S(2)}) async-start(), calls=%async_computation.4 | async-start | bytes 11796480 | tf_op jit(solution)/shard_map/reduce_scatter | solution.py:983
  685.8 20.3 %collective-permute-start.24 = (bf16[4,256,1664]{2,1,0:T(8,128)(2,1)}, bf16[4,256,1664]{2,1,0:T(8,128)(2,1)}, u32[]{:S(2)}, u32[]{:S(2)}) collective-permute-start(bf16[4,256,1664]{2,1,0:T(8,128)(2,1)} %shard_map.246), channel_id=1, source_target_pairs={{0,1},{1,0},{2,3},{3,2},{4,5},{5,4},{6,7},{7,6},{8,9},{9,8},{10,11... | collective-permute-start | bytes 10223624 | tf_op jit(solution)/shard_map/ppermute | solution.py:66
  692.4 19.7 %collective-permute-start.26 = (bf16[4,256,1664]{2,1,0:T(8,128)(2,1)}, bf16[4,256,1664]{2,1,0:T(8,128)(2,1)}, u32[]{:S(2)}, u32[]{:S(2)}) collective-permute-start(bf16[4,256,1664]{2,1,0:T(8,128)(2,1)} %shard_map.248), channel_id=1, source_target_pairs={{0,1},{1,0},{2,3},{3,2},{4,5},{5,4},{6,7},{7,6},{8,9},{9,8},{10,11... | collective-permute-start | bytes 10223624 | tf_op jit(solution)/shard_map/ppermute | solution.py:66
  723.1 23.1 %collective-permute-start.28 = (bf16[4,256,1536]{2,1,0:T(8,128)(2,1)}, bf16[4,256,1536]{2,1,0:T(8,128)(2,1)}, u32[]{:S(2)}, u32[]{:S(2)}) collective-permute-start(bf16[4,256,1536]{2,1,0:T(8,128)(2,1)} %shard_map.250), channel_id=1, source_target_pairs={{0,1},{1,0},{2,3},{3,2},{4,5},{5,4},{6,7},{7,6},{8,9},{9,8},{10,11... | collective-permute-start | bytes 9437192 | tf_op jit(solution)/shard_map/ppermute | solution.py:66
  729.8 21.9 %collective-permute-start.29 = (bf16[4,256,1536]{2,1,0:T(8,128)(2,1)}, bf16[4,256,1536]{2,1,0:T(8,128)(2,1)}, u32[]{:S(2)}, u32[]{:S(2)}) collective-permute-start(bf16[4,256,1536]{2,1,0:T(8,128)(2,1)} %shard_map.252), channel_id=1, source_target_pairs={{0,1},{1,0},{2,3},{3,2},{4,5},{5,4},{6,7},{7,6},{8,9},{9,8},{10,11... | collective-permute-start | bytes 9437192 | tf_op jit(solution)/shard_map/ppermute | solution.py:66
  730.0 70.9 %collective-permute-start.25 = (bf16[2,256,1664]{2,1,0:T(8,128)(2,1)}, bf16[2,256,1664]{2,1,0:T(8,128)(2,1)}, u32[]{:S(2)}, u32[]{:S(2)}) collective-permute-start(bf16[2,256,1664]{2,1,0:T(8,128)(2,1)} %get-tuple-element.262), channel_id=1, source_target_pairs={{0,8},{1,9},{2,10},{3,11},{4,12},{5,13},{6,14},{7,15},{8,0},{9,1},... | collective-permute-start | bytes 5111816 | tf_op jit(solution)/shard_map/ppermute | solution.py:66
  730.3 70.6 %collective-permute-start.27 = (bf16[2,256,1664]{2,1,0:T(8,128)(2,1)}, bf16[2,256,1664]{2,1,0:T(8,128)(2,1)}, u32[]{:S(2)}, u32[]{:S(2)}) collective-permute-start(bf16[2,256,1664]{2,1,0:T(8,128)(2,1)} %get-tuple-element.260), channel_id=1, source_target_pairs={{0,2},{1,3},{2,0},{3,1},{4,6},{5,7},{6,4},{7,5},{8,10},{9,11},{10,... | collective-permute-start | bytes 5111816 | tf_op jit(solution)/shard_map/ppermute | solution.py:66
  803.0 20.8 %collective-permute-start.30 = (bf16[1,256,1664]{2,1,0:T(8,128)(2,1)S(1)}, bf16[1,256,1664]{2,1,0:T(8,128)(2,1)S(1)}, u32[]{:S(2)}, u32[]{:S(2)}) collective-permute-start(bf16[1,256,1664]{2,1,0:T(8,128)(2,1)S(1)} %slice.396), channel_id=1, source_target_pairs={{0,2},{1,3},{2,0},{3,1},{4,6},{5,7},{6,4},{7,5},{8,10},{9,11},{10,... | collective-permute-start | bytes 2555912 | tf_op jit(solution)/shard_map/ppermute | solution.py:66
  805.0 49.9 %collective-permute-start.31 = (bf16[1,256,1664]{2,1,0:T(8,128)(2,1)S(1)}, bf16[1,256,1664]{2,1,0:T(8,128)(2,1)S(1)}, u32[]{:S(2)}, u32[]{:S(2)}) collective-permute-start(bf16[1,256,1664]{2,1,0:T(8,128)(2,1)S(1)} %slice.398), channel_id=1, source_target_pairs={{0,8},{1,9},{2,10},{3,11},{4,12},{5,13},{6,14},{7,15},{8,0},{9,1},... | collective-permute-start | bytes 2555912 | tf_op jit(solution)/shard_map/ppermute | solution.py:66
  900.5 45.5 %collective-permute-start.36 = (bf16[2,2,2,2,48,1664]{5,4,3,2,1,0:T(8,128)(2,1)}, bf16[2,2,2,2,48,1664]{5,4,3,2,1,0:T(8,128)(2,1)S(1)}, u32[]{:S(2)}, u32[]{:S(2)}) collective-permute-start(bf16[2,2,2,2,48,1664]{5,4,3,2,1,0:T(8,128)(2,1)} %dynamic-slice_bitcast_fusion.1), channel_id=1, source_target_pairs={{0,1},{1,0},{2,3},{3,2},{4,5},{5,4},{6,7},{7,6},{8,9},{9,8},{10,11... | collective-permute-start | bytes 7667720 | tf_op jit(solution)/shard_map/ppermute | solution.py:66
  908.5 24.1 %collective-permute-start.33 = (bf16[1,256,1024]{2,1,0:T(8,128)(2,1)S(1)}, bf16[1,256,1024]{2,1,0:T(8,128)(2,1)}, u32[]{:S(2)}, u32[]{:S(2)}) collective-permute-start(bf16[1,256,1024]{2,1,0:T(8,128)(2,1)S(1)} %fusion.11), channel_id=1, source_target_pairs={{0,2},{1,3},{2,0},{3,1},{4,6},{5,7},{6,4},{7,5},{8,10},{9,11},{10,... | collective-permute-start | bytes 1572872 | tf_op jit(solution)/shard_map/ppermute | solution.py:66
  979.4 47.2 %collective-permute-start.38 = (bf16[2,2,2,48,2688]{4,3,2,1,0:T(8,128)(2,1)}, bf16[2,2,2,48,2688]{4,3,2,1,0:T(8,128)(2,1)}, u32[]{:S(2)}, u32[]{:S(2)}) collective-permute-start(bf16[2,2,2,48,2688]{4,3,2,1,0:T(8,128)(2,1)} %dynamic-slice_bitcast_fusion.2), channel_id=1, source_target_pairs={{0,2},{1,3},{2,0},{3,1},{4,6},{5,7},{6,4},{7,5},{8,10},{9,11},{10,... | collective-permute-start | bytes 6193160 | tf_op jit(solution)/shard_map/ppermute | solution.py:66
  982.9 83.5 %collective-permute-start.41 = (bf16[3,576,512]{2,1,0:T(8,128)(2,1)}, bf16[3,576,512]{2,1,0:T(8,128)(2,1)}, u32[]{:S(2)}, u32[]{:S(2)}) collective-permute-start(bf16[3,576,512]{2,1,0:T(8,128)(2,1)} %get-tuple-element.270), channel_id=1, source_target_pairs={{0,8},{1,9},{2,10},{3,11},{4,12},{5,13},{6,14},{7,15},{8,0},{9,1},... | collective-permute-start | bytes 5308424 | tf_op jit(solution)/shard_map/ppermute | solution.py:66
  1030.8 54.5 %collective-permute-start.42 = (bf16[2,256,1536]{2,1,0:T(8,128)(2,1)}, bf16[2,256,1536]{2,1,0:T(8,128)(2,1)}, u32[]{:S(2)}, u32[]{:S(2)}) collective-permute-start(bf16[2,256,1536]{2,1,0:T(8,128)(2,1)} %get-tuple-element.176), channel_id=1, source_target_pairs={{0,8},{1,9},{2,10},{3,11},{4,12},{5,13},{6,14},{7,15},{8,0},{9,1},... | collective-permute-start | bytes 4718600 | tf_op jit(solution)/shard_map/ppermute | solution.py:66
  1030.8 54.5 %collective-permute-start.43 = (bf16[2,256,1536]{2,1,0:T(8,128)(2,1)}, bf16[2,256,1536]{2,1,0:T(8,128)(2,1)}, u32[]{:S(2)}, u32[]{:S(2)}) collective-permute-start(bf16[2,256,1536]{2,1,0:T(8,128)(2,1)} %get-tuple-element.177), channel_id=1, source_target_pairs={{0,2},{1,3},{2,0},{3,1},{4,6},{5,7},{6,4},{7,5},{8,10},{9,11},{10,... | collective-permute-start | bytes 4718600 | tf_op jit(solution)/shard_map/ppermute | solution.py:66
  1033.7 31.3 %collective-permute-start.40 = (bf16[2,2,2,48,1664]{4,3,2,1,0:T(8,128)(2,1)}, bf16[2,2,2,48,1664]{4,3,2,1,0:T(8,128)(2,1)}, u32[]{:S(2)}, u32[]{:S(2)}) collective-permute-start(bf16[2,2,2,48,1664]{4,3,2,1,0:T(8,128)(2,1)} %dynamic-slice_bitcast_fusion.3), channel_id=1, source_target_pairs={{0,4},{1,5},{2,6},{3,7},{4,0},{5,1},{6,2},{7,3},{8,12},{9,13},{10,... | collective-permute-start | bytes 3833864 | tf_op jit(solution)/shard_map/ppermute | solution.py:66
  1033.7 51.7 %collective-permute-start.39 = (bf16[2,2,48,2688]{3,2,1,0:T(8,128)(2,1)}, bf16[2,2,48,2688]{3,2,1,0:T(8,128)(2,1)}, u32[]{:S(2)}, u32[]{:S(2)}) collective-permute-start(bf16[2,2,48,2688]{3,2,1,0:T(8,128)(2,1)} %get-tuple-element.274), channel_id=1, source_target_pairs={{0,4},{1,5},{2,6},{3,7},{4,0},{5,1},{6,2},{7,3},{8,12},{9,13},{10,... | collective-permute-start | bytes 3096584 | tf_op jit(solution)/shard_map/ppermute | solution.py:66
  1065.0 54.3 %collective-permute-start.48 = (bf16[2,576,512]{2,1,0:T(8,128)(2,1)S(1)}, bf16[2,576,512]{2,1,0:T(8,128)(2,1)S(1)}, u32[]{:S(2)}, u32[]{:S(2)}) collective-permute-start(bf16[2,576,512]{2,1,0:T(8,128)(2,1)S(1)} %get-tuple-element.272), channel_id=1, source_target_pairs={{0,8},{1,9},{2,10},{3,11},{4,12},{5,13},{6,14},{7,15},{8,0},{9,1},... | collective-permute-start | bytes 3538952 | tf_op jit(solution)/shard_map/ppermute | solution.py:66
  1088.2 70.1 %collective-permute-start.45 = (bf16[1,256,1536]{2,1,0:T(8,128)(2,1)}, bf16[1,256,1536]{2,1,0:T(8,128)(2,1)}, u32[]{:S(2)}, u32[]{:S(2)}) collective-permute-start(bf16[1,256,1536]{2,1,0:T(8,128)(2,1)} %slice.406), channel_id=1, source_target_pairs={{0,8},{1,9},{2,10},{3,11},{4,12},{5,13},{6,14},{7,15},{8,0},{9,1},... | collective-permute-start | bytes 2359304 | tf_op jit(solution)/shard_map/ppermute | solution.py:66
  1092.6 40.4 %collective-permute-start.47 = (bf16[2,2,48,1664]{3,2,1,0:T(8,128)(2,1)S(1)}, bf16[2,2,48,1664]{3,2,1,0:T(8,128)(2,1)S(1)}, u32[]{:S(2)}, u32[]{:S(2)}) collective-permute-start(bf16[2,2,48,1664]{3,2,1,0:T(8,128)(2,1)S(1)} %dynamic-slice_bitcast_fusion.6), channel_id=1, source_target_pairs={{0,2},{1,3},{2,0},{3,1},{4,6},{5,7},{6,4},{7,5},{8,10},{9,11},{10,... | collective-permute-start | bytes 1916936 | tf_op jit(solution)/shard_map/ppermute | solution.py:66
  1094.1 38.9 %collective-permute-start.46 = (bf16[2,48,2688]{2,1,0:T(8,128)(2,1)S(1)}, bf16[2,48,2688]{2,1,0:T(8,128)(2,1)S(1)}, u32[]{:S(2)}, u32[]{:S(2)}) collective-permute-start(bf16[2,48,2688]{2,1,0:T(8,128)(2,1)S(1)} %dynamic-slice_bitcast_fusion.7), channel_id=1, source_target_pairs={{0,16},{1,17},{2,18},{3,19},{4,20},{5,21},{6,22},{7,23},{8,24},{9,... | collective-permute-start | bytes 1548296 | tf_op jit(solution)/shard_map/ppermute | solution.py:66
  1097.0 62.9 %collective-permute-start.44 = (bf16[1,256,1536]{2,1,0:T(8,128)(2,1)}, bf16[1,256,1536]{2,1,0:T(8,128)(2,1)}, u32[]{:S(2)}, u32[]{:S(2)}) collective-permute-start(bf16[1,256,1536]{2,1,0:T(8,128)(2,1)} %slice.404), channel_id=1, source_target_pairs={{0,2},{1,3},{2,0},{3,1},{4,6},{5,7},{6,4},{7,5},{8,10},{9,11},{10,... | collective-permute-start | bytes 2359304 | tf_op jit(solution)/shard_map/ppermute | solution.py:66
  1133.9 29.2 %collective-permute-start.49 = (bf16[48,2688]{1,0:T(8,128)(2,1)}, bf16[48,2688]{1,0:T(8,128)(2,1)}, u32[]{:S(2)}, u32[]{:S(2)}) collective-permute-start(bf16[48,2688]{1,0:T(8,128)(2,1)} %dynamic-slice_bitcast_fusion.9), channel_id=1, source_target_pairs={{0,8},{1,9},{2,10},{3,11},{4,12},{5,13},{6,14},{7,15},{8,0},{9,1},... | collective-permute-start | bytes 774152 | tf_op jit(solution)/shard_map/ppermute | solution.py:66
  1135.8 28.3 %collective-permute-start.50 = (bf16[2,48,1664]{2,1,0:T(8,128)(2,1)}, bf16[2,48,1664]{2,1,0:T(8,128)(2,1)S(1)}, u32[]{:S(2)}, u32[]{:S(2)}) collective-permute-start(bf16[2,48,1664]{2,1,0:T(8,128)(2,1)} %dynamic-slice_bitcast_fusion.8), channel_id=1, source_target_pairs={{0,16},{1,17},{2,18},{3,19},{4,20},{5,21},{6,22},{7,23},{8,24},{9,... | collective-permute-start | bytes 958472 | tf_op jit(solution)/shard_map/ppermute | solution.py:66
  (96 other events, 2408.9 us)
Sparse Core Ops, SparseCore 0:
  11.5 140.9 all-gather.1
  618.2 246.1 reduce-scatter.2
  867.6 169.4 reduce-scatter.4

commit v4 on v3

--- a/solution.py
+++ b/solution.py
@@ -756,12 +756,10 @@
 
 
 def pack_experts(gate, up, down):
-    count, shallow, width = down.shape
+    width = down.shape[2]
     inner = gate.shape[2]
-    turned = down.reshape(count, shallow, width // inner, inner).transpose(0, 2, 1, 3)
-    return jnp.concatenate(
-        [gate, up, turned.reshape(count, shallow * width // inner, inner)], axis=1
-    )
+    columns = [down[:, :, start : start + inner] for start in range(0, width, inner)]
+    return jnp.concatenate([gate, up] + columns, axis=1)
 
 
 def slot_codes(picks, valid, capacity):
@@ -1123,11 +1121,13 @@
     inner = w_gate.shape[2]
     grad_gate = mine[:, :deep]
     grad_up = mine[:, deep : 2 * deep]
-    grad_down = (
-        mine[:, 2 * deep :]
-        .reshape(owned, width // inner, w_down.shape[1], inner)
-        .transpose(0, 2, 1, 3)
-        .reshape(w_down.shape)
+    shallow = w_down.shape[1]
+    grad_down = jnp.concatenate(
+        [
+            mine[:, start : start + shallow]
+            for start in range(2 * deep, mine.shape[1], shallow)
+        ],
+        axis=2,
     )
     late_grads = home_one.rows()
     output_grads = home_two.rows()

time: 1190 us -> 1170 us (0.983)
  local copies, waits for them, and re-layouts: 113 us -> 98.2 us
    reshape x4 -> x0, local copies, waits for them, and re-layouts: 14.1 us -> none  [the longest x2 12.7 us: shards(): grad_down = mine[:, 2 * deep:].reshape(owned, width // inner, w_down.shap...]
    unnamed x202 -> x194, local copies, waits for them, and re-layouts: 46.3 us -> 52.4 us
  transfers between devices with their start and end apart: 55 -> 55, of which waited for: 25 -> 26; matrix products, arithmetic and copies ran while one was open for 15% -> 14% of each run, Pallas kernels for 22% -> 22%
where the time goes in v4:
time: 1170 us
  waiting for transfers between devices  555 us (47%)
  Pallas kernels  344 us (29%)
  other arithmetic  98.5 us (8%)
  local copies, waits for them, and re-layouts  98.2 us (8%)
  starting transfers between devices  46.8 us (4%)
  between operations  15.3 us (1%)
    ppermute x52, waiting for transfers between devices, swap(): lax.ppermute(array, AXES, [(i, i ^ flip) for i in range(dp_count * owner_...  550 us
    pallas_call x2, Pallas kernels, run_experts(): pl.pallas_call(functools.partial(expert_kernel, masks, sources, pair_bit,...  135 us
    unnamed x194, local copies, waits for them, and re-layouts  52.4 us
    pallas_call x8, Pallas kernels, combine(): pl.pallas_call(combine_kernel, grid=(size,), in_specs=[pl.BlockSpec((1, l...  52.2 us
    pallas_call x2, Pallas kernels, attend_back(): pl.pallas_call(attend_back_kernel, grid_spec=pltpu.PrefetchScalarGridSpec...  47.3 us
    ppermute x52, starting transfers between devices, swap(): lax.ppermute(array, AXES, [(i, i ^ flip) for i in range(dp_count * owner_...  46.7 us
    convert_element_type x18, other arithmetic, add_rounded(): return (left.astype(F32) + right.astype(F32)).astype(left.dtype)  40.4 us
    pallas_call x2, Pallas kernels, attend(): pl.pallas_call(attend_kernel, grid_spec=pltpu.PrefetchScalarGridSpec(num_...  37.8 us
  transfers between devices with their start and end apart: 55, of which 26 were waited for; matrix products, arithmetic and copies ran while one was open for 14% of the time, Pallas kernels for 22%

profile of v4, /device:TPU:0, one launch (start us, length us, event | category | flops | bytes accessed | tf_op | source)
XLA Modules:
  0.0 1165.0 jit_solution(440493921404338035)
XLA Ops:
  35.3 39.5 %collective-permute-done.2 = bf16[1,2,256,1664]{3,2,1,0:T(8,128)(2,1)} collective-permute-done((bf16[1,2,256,1664]{3,2,1,0:T(8,128)(2,1)S(1)}, bf16[1,2,256,1664]{3,2,1,0:T(8,128)(2,1)}, u32[]{:S(2)}, u32[]{:S(2)}) %collective-permute-start.2) | collective-permute-done | bytes 1703968 | tf_op jit(solution)/shard_map/ppermute | solution.py:66
  74.7 72.6 %collective-permute-done.refs_1_ = bf16[5,576,512]{2,1,0:T(8,128)(2,1)} collective-permute-done((bf16[5,576,512]{2,1,0:T(8,128)(2,1)}, bf16[5,576,512]{2,1,0:T(8,128)(2,1)}, u32[]{:S(2)}, u32[]{:S(2)}) %collective-permute-start) | collective-permute-done | bytes 2949152 | tf_op jit(solution)/shard_map/ppermute | solution.py:66
  153.2 9.9 shard_map.238
  181.1 9.2 collective-permute-done.3
  195.6 18.7 %shard_map.239 = (bf16[256,1536]{1,0:T(8,128)(2,1)S(1)}, f32[4,8,256]{2,1,0:T(8,128)S(1)}) custom-call(s32[6]{0:T(128)S(1)} %concatenate.95.places_ref, bf16[256,1536]{1,0:T(8,128)(2,1)S(1)} %get-tuple-element.284.q_ref, bf16[1024,1024]{1,0:T(8,128)(2,1)S(1)} %bitcast.225, bf16[1024,1024]{1,0:T(8,128)(2,1)S(1)} %bitcast.226), custom_call_target="tpu_custom_call" | custom-call | flops 570000000 | tf_op jit(solution)/shard_map/pallas_call | solution.py:424
  216.2 4.7 shard_map.240
  228.5 19.2 %shard_map.241 = (bf16[256,1536]{1,0:T(8,128)(2,1)S(1)}, f32[4,8,256]{2,1,0:T(8,128)S(1)}) custom-call(s32[6]{0:T(128)S(1)} %concatenate.105.places_ref, bf16[256,1536]{1,0:T(8,128)(2,1)S(1)} %get-tuple-element.285.q_ref, bf16[1024,1024]{1,0:T(8,128)(2,1)S(1)} %bitcast.229, bf16[1024,1024]{1,0:T(8,128)(2,1)S(1)} %bitcast.230), custom_call_target="tpu_custom_call" | custom-call | flops 570000000 | tf_op jit(solution)/shard_map/pallas_call | solution.py:424
  249.7 4.7 shard_map.242
  255.4 71.9 %collective-permute-done.11 = bf16[256,1536]{1,0:T(8,128)(2,1)} collective-permute-done((bf16[256,1536]{1,0:T(8,128)(2,1)S(1)}, bf16[256,1536]{1,0:T(8,128)(2,1)}, u32[]{:S(2)}, u32[]{:S(2)}) %collective-permute-start.11) | collective-permute-done | bytes 786464 | tf_op jit(solution)/shard_map/ppermute | solution.py:66
  328.9 13.8 %collective-permute-done.12 = bf16[256,1536]{1,0:T(8,128)(2,1)S(1)} collective-permute-done((bf16[256,1536]{1,0:T(8,128)(2,1)S(1)}, bf16[256,1536]{1,0:T(8,128)(2,1)S(1)}, u32[]{:S(2)}, u32[]{:S(2)}) %collective-permute-start.12) | collective-permute-done | bytes 786464 | tf_op jit(solution)/shard_map/ppermute | solution.py:66
  344.3 6.1 pad_maximum_fusion
  368.0 51.1 %collective-permute-done.21 = bf16[256,1536]{1,0:T(8,128)(2,1)S(1)} collective-permute-done((bf16[256,1536]{1,0:T(8,128)(2,1)}, bf16[256,1536]{1,0:T(8,128)(2,1)S(1)}, u32[]{:S(2)}, u32[]{:S(2)}) %collective-permute-start.21) | collective-permute-done | bytes 786464 | tf_op jit(solution)/shard_map/ppermute | solution.py:66
  438.6 4.8 copy-done.28
  452.9 48.4 %collective-permute-done.19.refs_3_ = bf16[2,576,512]{2,1,0:T(8,128)(2,1)S(1)} collective-permute-done((bf16[2,576,512]{2,1,0:T(8,128)(2,1)}, bf16[2,576,512]{2,1,0:T(8,128)(2,1)S(1)}, u32[]{:S(2)}, u32[]{:S(2)}) %collective-permute-start.19) | collective-permute-done | bytes 1179680 | tf_op jit(solution)/shard_map/ppermute | solution.py:66
  506.4 21.9 %collective-permute-done.20.refs_7_ = bf16[2,576,512]{2,1,0:T(8,128)(2,1)S(1)} collective-permute-done((bf16[2,576,512]{2,1,0:T(8,128)(2,1)S(1)}, bf16[2,576,512]{2,1,0:T(8,128)(2,1)S(1)}, u32[]{:S(2)}, u32[]{:S(2)}) %collective-permute-start.20) | collective-permute-done | bytes 1179680 | tf_op jit(solution)/shard_map/ppermute | solution.py:66
  529.4 6.5 select_reduce_fusion
  537.8 79.6 %shard_map.243 = (bf16[16,5,64,1536]{3,2,1,0:T(8,128)(2,1)}, bf16[16,5,64,1664]{3,2,1,0:T(8,128)(2,1)}, bf16[4,2,3,576,512]{4,3,2,1,0:T(8,128)(2,1)}) custom-call(s32[2]{0:T(128)} %pad_add_fusion.me_ref, bf16[5,576,512]{2,1,0:T(8,128)(2,1)} %dynamic-slice_dynamic-update-slice_fusion.7.refs_0_, bf16[5,576,512]{2,1,0:T(8,128)(2,1)} %collective-permute-done.refs_1_, ...), custom_call_target="tpu_custom_call" | custom-call | flops 2790000128 | tf_op jit(solution)/shard_map/pallas_call | solution.py:694
  622.6 55.7 %shard_map.244 = (bf16[16,5,64,1536]{3,2,1,0:T(8,128)(2,1)}, bf16[16,5,64,1664]{3,2,1,0:T(8,128)(2,1)}, bf16[4,2,2,576,512]{4,3,2,1,0:T(8,128)(2,1)}) custom-call(s32[2]{0:T(128)} %pad_add_fusion.me_ref, bf16[5,576,512]{2,1,0:T(8,128)(2,1)} %dynamic-slice_dynamic-update-slice_fusion.7.refs_0_, ...), custom_call_target="tpu_custom_call", output_to_operand_aliasing={{0}: (13, {}), {1}: (14, {})} | custom-call | flops 1860000000 | tf_op jit(solution)/shard_map/pallas_call | solution.py:694
  678.3 6.8 shard_map.246
  685.1 6.7 shard_map.248
  692.2 6.5 shard_map.245
  698.7 6.7 shard_map.247
  705.4 6.0 add_convert_fusion.3
  716.0 6.3 shard_map.250
  722.6 6.4 shard_map.252
  732.6 6.4 shard_map.249
  739.0 6.4 shard_map.251
  745.5 5.5 add_convert_fusion.10
  751.0 4.9 add_convert_fusion.8
  756.0 44.2 %collective-permute-done.25 = bf16[2,256,1664]{2,1,0:T(8,128)(2,1)} collective-permute-done((bf16[2,256,1664]{2,1,0:T(8,128)(2,1)}, bf16[2,256,1664]{2,1,0:T(8,128)(2,1)}, u32[]{:S(2)}, u32[]{:S(2)}) %collective-permute-start.25) | collective-permute-done | bytes 1703968 | tf_op jit(solution)/shard_map/ppermute | solution.py:66
  805.6 17.4 %collective-permute-done.30 = bf16[1,256,1664]{2,1,0:T(8,128)(2,1)S(1)} collective-permute-done((bf16[1,256,1664]{2,1,0:T(8,128)(2,1)S(1)}, bf16[1,256,1664]{2,1,0:T(8,128)(2,1)S(1)}, u32[]{:S(2)}, u32[]{:S(2)}) %collective-permute-start.30) | collective-permute-done | bytes 852000 | tf_op jit(solution)/shard_map/ppermute | solution.py:66
  824.2 6.6 shard_map.253
  830.8 23.4 %shard_map.254 = (bf16[256,1536]{1,0:T(8,128)(2,1)}, bf16[1024,1024]{1,0:T(8,128)(2,1)}) custom-call(s32[6]{0:T(128)} %copy-done.25, bf16[256,1536]{1,0:T(8,128)(2,1)} %copy-done.5, bf16[1024,1024]{1,0:T(8,128)(2,1)} %bitcast.227, bf16[1024,1024]{1,0:T(8,128)(2,1)} %bitcast.228, bf16[256,1536]{1,0:T(8,128)(2,1)} %get-tuple-element.141.do_ref, ...), custom_call_target="tpu_custom_call" | custom-call | flops 705000000 | tf_op jit(solution)/shard_map/pallas_call | solution.py:502
  855.3 6.6 shard_map.255
  862.0 23.8 %shard_map.256 = (bf16[256,1536]{1,0:T(8,128)(2,1)}, bf16[1024,1024]{1,0:T(8,128)(2,1)}) custom-call(s32[6]{0:T(128)} %copy-done.26, bf16[256,1536]{1,0:T(8,128)(2,1)} %copy-done.4, bf16[1024,1024]{1,0:T(8,128)(2,1)} %bitcast.231, bf16[1024,1024]{1,0:T(8,128)(2,1)} %bitcast.232, bf16[256,1536]{1,0:T(8,128)(2,1)} %get-tuple-element.151.do_ref, ...), custom_call_target="tpu_custom_call" | custom-call | flops 705000000 | tf_op jit(solution)/shard_map/pallas_call | solution.py:502
  888.4 7.9 shard_map.257
  900.6 5.1 collective-permute-done.34
  909.6 11.2 collective-permute-done.35
  921.8 10.1 shard_map.259
  934.0 10.0 shard_map.258
  947.8 10.8 shard_map.260
  958.6 4.7 dynamic-slice_bitcast_fusion
  963.3 7.4 collective-permute-done.37
  982.1 43.8 %collective-permute-done.38 = bf16[2,2,2,48,2688]{4,3,2,1,0:T(8,128)(2,1)} collective-permute-done((bf16[2,2,2,48,2688]{4,3,2,1,0:T(8,128)(2,1)}, bf16[2,2,2,48,2688]{4,3,2,1,0:T(8,128)(2,1)}, u32[]{:S(2)}, u32[]{:S(2)}) %collective-permute-start.38) | collective-permute-done | bytes 2064416 | tf_op jit(solution)/shard_map/ppermute | solution.py:66
  1040.9 23.4 %collective-permute-done.40 = bf16[2,2,2,48,1664]{4,3,2,1,0:T(8,128)(2,1)} collective-permute-done((bf16[2,2,2,48,1664]{4,3,2,1,0:T(8,128)(2,1)}, bf16[2,2,2,48,1664]{4,3,2,1,0:T(8,128)(2,1)}, u32[]{:S(2)}, u32[]{:S(2)}) %collective-permute-start.40) | collective-permute-done | bytes 1277984 | tf_op jit(solution)/shard_map/ppermute | solution.py:66
  1065.6 19.0 %collective-permute-done.39 = bf16[2,2,48,2688]{3,2,1,0:T(8,128)(2,1)} collective-permute-done((bf16[2,2,48,2688]{3,2,1,0:T(8,128)(2,1)}, bf16[2,2,48,2688]{3,2,1,0:T(8,128)(2,1)}, u32[]{:S(2)}, u32[]{:S(2)}) %collective-permute-start.39) | collective-permute-done | bytes 1032224 | tf_op jit(solution)/shard_map/ppermute | solution.py:66
  1095.2 23.5 %collective-permute-done.48 = bf16[2,576,512]{2,1,0:T(8,128)(2,1)S(1)} collective-permute-done((bf16[2,576,512]{2,1,0:T(8,128)(2,1)S(1)}, bf16[2,576,512]{2,1,0:T(8,128)(2,1)S(1)}, u32[]{:S(2)}, u32[]{:S(2)}) %collective-permute-start.48) | collective-permute-done | bytes 1179680 | tf_op jit(solution)/shard_map/ppermute | solution.py:66
  1118.6 13.7 %collective-permute-done.46 = bf16[2,48,2688]{2,1,0:T(8,128)(2,1)S(1)} collective-permute-done((bf16[2,48,2688]{2,1,0:T(8,128)(2,1)S(1)}, bf16[2,48,2688]{2,1,0:T(8,128)(2,1)S(1)}, u32[]{:S(2)}, u32[]{:S(2)}) %collective-permute-start.46) | collective-permute-done | bytes 516128 | tf_op jit(solution)/shard_map/ppermute | solution.py:66
  (414 shorter events, 230.4 us)
Async XLA Ops:
  7.2 144.4 %all-gather.2.cloned.1.call-start = ((), (), s32[]{:S(2)}) async-start(), calls=%async_computation.2 | async-start | bytes 13787136 | tf_op jit(solution)/shard_map/all_gather | solution.py:830
  11.5 922.5 %reduce-scatter.3.cloned.1.call-start = ((), (), s32[]{:S(2)}) async-start(), calls=%async_computation.3 | async-start | bytes 17694720 | tf_op jit(solution)/shard_map/reduce_scatter | solution.py:981
  19.3 128.0 %collective-permute-start = (bf16[5,576,512]{2,1,0:T(8,128)(2,1)}, bf16[5,576,512]{2,1,0:T(8,128)(2,1)}, u32[]{:S(2)}, u32[]{:S(2)}) collective-permute-start(bf16[5,576,512]{2,1,0:T(8,128)(2,1)} %get-tuple-element.276), channel_id=1, source_target_pairs={{0,8},{1,9},{2,10},{3,11},{4,12},{5,13},{6,14},{7,15},{8,0},{9,1},... | collective-permute-start | bytes 8847368 | tf_op jit(solution)/shard_map/ppermute | solution.py:66
  23.1 124.3 %collective-permute-start.1 = (bf16[5,576,512]{2,1,0:T(8,128)(2,1)}, bf16[5,576,512]{2,1,0:T(8,128)(2,1)}, u32[]{:S(2)}, u32[]{:S(2)}) collective-permute-start(bf16[5,576,512]{2,1,0:T(8,128)(2,1)} %dynamic-slice_dynamic-update-slice_fusion.7.refs_0_), channel_id=1, source_target_pairs={{0,4},{1,5},{2,6},{3,7},{4,0},{5,1},{6,2},{7,3},{8,12},{9,13},{10,... | collective-permute-start | bytes 8847368 | tf_op jit(solution)/shard_map/ppermute | solution.py:66
  30.2 44.5 %collective-permute-start.2 = (bf16[1,2,256,1664]{3,2,1,0:T(8,128)(2,1)S(1)}, bf16[1,2,256,1664]{3,2,1,0:T(8,128)(2,1)}, u32[]{:S(2)}, u32[]{:S(2)}) collective-permute-start(bf16[1,2,256,1664]{3,2,1,0:T(8,128)(2,1)S(1)} %maximum_bitcast_fusion.1), channel_id=1, source_target_pairs={{0,2},{1,3},{2,0},{3,1},{4,6},{5,7},{6,4},{7,5},{8,10},{9,11},{10,... | collective-permute-start | bytes 5111816 | tf_op jit(solution)/shard_map/ppermute | solution.py:66
  166.4 24.0 %collective-permute-start.3 = (bf16[256,1024]{1,0:T(8,128)(2,1)}, bf16[256,1024]{1,0:T(8,128)(2,1)}, u32[]{:S(2)}, u32[]{:S(2)}) collective-permute-start(bf16[256,1024]{1,0:T(8,128)(2,1)} %get-tuple-element.291), channel_id=1, source_target_pairs={{0,2},{1,3},{2,0},{3,1},{4,6},{5,7},{6,4},{7,5},{8,10},{9,11},{10,... | collective-permute-start | bytes 1572872 | tf_op jit(solution)/shard_map/ppermute | solution.py:66
  170.3 174.0 %collective-permute-start.9 = (bf16[2,2,256,1664]{3,2,1,0:T(8,128)(2,1)}, bf16[2,2,256,1664]{3,2,1,0:T(8,128)(2,1)}, u32[]{:S(2)}, u32[]{:S(2)}) collective-permute-start(bf16[2,2,256,1664]{3,2,1,0:T(8,128)(2,1)} %pad_maximum_fusion.2), channel_id=1, source_target_pairs={{0,8},{1,9},{2,10},{3,11},{4,12},{5,13},{6,14},{7,15},{8,0},{9,1},... | collective-permute-start | bytes 10223624 | tf_op jit(solution)/shard_map/ppermute | solution.py:66
  172.8 171.5 %collective-permute-start.7 = (bf16[5,576,512]{2,1,0:T(8,128)(2,1)}, bf16[5,576,512]{2,1,0:T(8,128)(2,1)}, u32[]{:S(2)}, u32[]{:S(2)}) collective-permute-start(bf16[5,576,512]{2,1,0:T(8,128)(2,1)} %dynamic-slice_dynamic-update-slice_fusion.7.refs_0_), channel_id=1, source_target_pairs={{0,16},{1,17},{2,18},{3,19},{4,20},{5,21},{6,22},{7,23},{8,24},{9,... | collective-permute-start | bytes 8847368 | tf_op jit(solution)/shard_map/ppermute | solution.py:66
  175.4 168.9 %collective-permute-start.8 = (bf16[5,576,512]{2,1,0:T(8,128)(2,1)}, bf16[5,576,512]{2,1,0:T(8,128)(2,1)}, u32[]{:S(2)}, u32[]{:S(2)}) collective-permute-start(bf16[5,576,512]{2,1,0:T(8,128)(2,1)} %collective-permute-done.refs_1_), channel_id=1, source_target_pairs={{0,4},{1,5},{2,6},{3,7},{4,0},{5,1},{6,2},{7,3},{8,12},{9,13},{10,... | collective-permute-start | bytes 8847368 | tf_op jit(solution)/shard_map/ppermute | solution.py:66
  181.1 43.3 %collective-permute-start.6 = (bf16[2,256,1024]{2,1,0:T(8,128)(2,1)S(1)}, bf16[2,256,1024]{2,1,0:T(8,128)(2,1)S(1)}, u32[]{:S(2)}, u32[]{:S(2)}) collective-permute-start(bf16[2,256,1024]{2,1,0:T(8,128)(2,1)S(1)} %pad_maximum_fusion.14), channel_id=1, source_target_pairs={{0,1},{1,0},{2,3},{3,2},{4,5},{5,4},{6,7},{7,6},{8,9},{9,8},{10,11... | collective-permute-start | bytes 3145736 | tf_op jit(solution)/shard_map/ppermute | solution.py:66
  222.7 31.7 %collective-permute-start.10 = (bf16[256,1536]{1,0:T(8,128)(2,1)S(1)}, bf16[256,1536]{1,0:T(8,128)(2,1)}, u32[]{:S(2)}, u32[]{:S(2)}) collective-permute-start(bf16[256,1536]{1,0:T(8,128)(2,1)S(1)} %get-tuple-element.112), channel_id=1, source_target_pairs={{0,2},{1,3},{2,0},{3,1},{4,6},{5,7},{6,4},{7,5},{8,10},{9,11},{10,... | collective-permute-start | bytes 2359304 | tf_op jit(solution)/shard_map/ppermute | solution.py:66
  224.4 102.9 %collective-permute-start.11 = (bf16[256,1536]{1,0:T(8,128)(2,1)S(1)}, bf16[256,1536]{1,0:T(8,128)(2,1)}, u32[]{:S(2)}, u32[]{:S(2)}) collective-permute-start(bf16[256,1536]{1,0:T(8,128)(2,1)S(1)} %get-tuple-element.112), channel_id=1, source_target_pairs={{0,8},{1,9},{2,10},{3,11},{4,12},{5,13},{6,14},{7,15},{8,0},{9,1},... | collective-permute-start | bytes 2359304 | tf_op jit(solution)/shard_map/ppermute | solution.py:66
  254.4 88.3 %collective-permute-start.12 = (bf16[256,1536]{1,0:T(8,128)(2,1)S(1)}, bf16[256,1536]{1,0:T(8,128)(2,1)S(1)}, u32[]{:S(2)}, u32[]{:S(2)}) collective-permute-start(bf16[256,1536]{1,0:T(8,128)(2,1)S(1)} %get-tuple-element.107), channel_id=1, source_target_pairs={{0,8},{1,9},{2,10},{3,11},{4,12},{5,13},{6,14},{7,15},{8,0},{9,1},... | collective-permute-start | bytes 2359304 | tf_op jit(solution)/shard_map/ppermute | solution.py:66
  327.3 17.0 %collective-permute-start.13 = (bf16[256,1536]{1,0:T(8,128)(2,1)S(1)}, bf16[256,1536]{1,0:T(8,128)(2,1)S(1)}, u32[]{:S(2)}, u32[]{:S(2)}) collective-permute-start(bf16[256,1536]{1,0:T(8,128)(2,1)S(1)} %get-tuple-element.107), channel_id=1, source_target_pairs={{0,2},{1,3},{2,0},{3,1},{4,6},{5,7},{6,4},{7,5},{8,10},{9,11},{10,... | collective-permute-start | bytes 2359304 | tf_op jit(solution)/shard_map/ppermute | solution.py:66
  350.4 74.0 %collective-permute-start.17 = (bf16[4,2,256,1664]{3,2,1,0:T(8,128)(2,1)}, bf16[4,2,256,1664]{3,2,1,0:T(8,128)(2,1)}, u32[]{:S(2)}, u32[]{:S(2)}) collective-permute-start(bf16[4,2,256,1664]{3,2,1,0:T(8,128)(2,1)} %pad_maximum_fusion), channel_id=1, source_target_pairs={{0,1},{1,0},{2,3},{3,2},{4,5},{5,4},{6,7},{7,6},{8,9},{9,8},{10,11... | collective-permute-start | bytes 20447240 | tf_op jit(solution)/shard_map/ppermute | solution.py:66
  358.2 64.2 %collective-permute-start.14 = (bf16[256,1536]{1,0:T(8,128)(2,1)S(1)}, bf16[256,1536]{1,0:T(8,128)(2,1)S(1)}, u32[]{:S(2)}, u32[]{:S(2)}) collective-permute-start(bf16[256,1536]{1,0:T(8,128)(2,1)S(1)} %collective-permute-done.12), channel_id=1, source_target_pairs={{0,2},{1,3},{2,0},{3,1},{4,6},{5,7},{6,4},{7,5},{8,10},{9,11},{10,... | collective-permute-start | bytes 2359304 | tf_op jit(solution)/shard_map/ppermute | solution.py:66
  359.8 86.1 %collective-permute-start.15 = (bf16[5,576,512]{2,1,0:T(8,128)(2,1)}, bf16[5,576,512]{2,1,0:T(8,128)(2,1)}, u32[]{:S(2)}, u32[]{:S(2)}) collective-permute-start(bf16[5,576,512]{2,1,0:T(8,128)(2,1)} %collective-permute-done.7.refs_2_), channel_id=1, source_target_pairs={{0,4},{1,5},{2,6},{3,7},{4,0},{5,1},{6,2},{7,3},{8,12},{9,13},{10,... | collective-permute-start | bytes 8847368 | tf_op jit(solution)/shard_map/ppermute | solution.py:66
  361.3 84.6 %collective-permute-start.16 = (bf16[3,576,512]{2,1,0:T(8,128)(2,1)}, bf16[3,576,512]{2,1,0:T(8,128)(2,1)}, u32[]{:S(2)}, u32[]{:S(2)}) collective-permute-start(bf16[3,576,512]{2,1,0:T(8,128)(2,1)} %slice.325), channel_id=1, source_target_pairs={{0,16},{1,17},{2,18},{3,19},{4,20},{5,21},{6,22},{7,23},{8,24},{9,... | collective-permute-start | bytes 5308424 | tf_op jit(solution)/shard_map/ppermute | solution.py:66
  363.9 55.1 %collective-permute-start.21 = (bf16[256,1536]{1,0:T(8,128)(2,1)}, bf16[256,1536]{1,0:T(8,128)(2,1)S(1)}, u32[]{:S(2)}, u32[]{:S(2)}) collective-permute-start(bf16[256,1536]{1,0:T(8,128)(2,1)} %collective-permute-done.10), channel_id=1, source_target_pairs={{0,8},{1,9},{2,10},{3,11},{4,12},{5,13},{6,14},{7,15},{8,0},{9,1},... | collective-permute-start | bytes 2359304 | tf_op jit(solution)/shard_map/ppermute | solution.py:66
  422.4 80.8 %collective-permute-start.22 = (bf16[4,256,1536]{2,1,0:T(8,128)(2,1)}, bf16[4,256,1536]{2,1,0:T(8,128)(2,1)}, u32[]{:S(2)}, u32[]{:S(2)}) collective-permute-start(bf16[4,256,1536]{2,1,0:T(8,128)(2,1)} %pad_maximum_fusion.4), channel_id=1, source_target_pairs={{0,1},{1,0},{2,3},{3,2},{4,5},{5,4},{6,7},{7,6},{8,9},{9,8},{10,11... | collective-permute-start | bytes 9437192 | tf_op jit(solution)/shard_map/ppermute | solution.py:66
  445.9 82.5 %collective-permute-start.23 = (bf16[4,256,1536]{2,1,0:T(8,128)(2,1)}, bf16[4,256,1536]{2,1,0:T(8,128)(2,1)S(1)}, u32[]{:S(2)}, u32[]{:S(2)}) collective-permute-start(bf16[4,256,1536]{2,1,0:T(8,128)(2,1)} %pad_maximum_fusion.3), channel_id=1, source_target_pairs={{0,1},{1,0},{2,3},{3,2},{4,5},{5,4},{6,7},{7,6},{8,9},{9,8},{10,11... | collective-permute-start | bytes 9437192 | tf_op jit(solution)/shard_map/ppermute | solution.py:66
  447.0 54.3 %collective-permute-start.19 = (bf16[2,576,512]{2,1,0:T(8,128)(2,1)}, bf16[2,576,512]{2,1,0:T(8,128)(2,1)S(1)}, u32[]{:S(2)}, u32[]{:S(2)}) collective-permute-start(bf16[2,576,512]{2,1,0:T(8,128)(2,1)} %slice.326), channel_id=1, source_target_pairs={{0,16},{1,17},{2,18},{3,19},{4,20},{5,21},{6,22},{7,23},{8,24},{9,... | collective-permute-start | bytes 3538952 | tf_op jit(solution)/shard_map/ppermute | solution.py:66
  451.1 55.3 %collective-permute-start.18 = (bf16[3,576,512]{2,1,0:T(8,128)(2,1)}, bf16[3,576,512]{2,1,0:T(8,128)(2,1)S(1)}, u32[]{:S(2)}, u32[]{:S(2)}) collective-permute-start(bf16[3,576,512]{2,1,0:T(8,128)(2,1)} %collective-permute-done.16.refs_3_), channel_id=1, source_target_pairs={{0,4},{1,5},{2,6},{3,7},{4,0},{5,1},{6,2},{7,3},{8,12},{9,13},{10,... | collective-permute-start | bytes 5308424 | tf_op jit(solution)/shard_map/ppermute | solution.py:66
  501.3 27.1 %collective-permute-start.20 = (bf16[2,576,512]{2,1,0:T(8,128)(2,1)S(1)}, bf16[2,576,512]{2,1,0:T(8,128)(2,1)S(1)}, u32[]{:S(2)}, u32[]{:S(2)}) collective-permute-start(bf16[2,576,512]{2,1,0:T(8,128)(2,1)S(1)} %collective-permute-done.19.refs_3_), channel_id=1, source_target_pairs={{0,4},{1,5},{2,6},{3,7},{4,0},{5,1},{6,2},{7,3},{8,12},{9,13},{10,... | collective-permute-start | bytes 3538952 | tf_op jit(solution)/shard_map/ppermute | solution.py:66
  617.4 419.0 %reduce-scatter.5.cloned.1.call-start = ((), (), s32[]{:S(2)}) async-start(), calls=%async_computation.4 | async-start | bytes 11796480 | tf_op jit(solution)/shard_map/reduce_scatter | solution.py:981
  685.1 20.3 %collective-permute-start.24 = (bf16[4,256,1664]{2,1,0:T(8,128)(2,1)}, bf16[4,256,1664]{2,1,0:T(8,128)(2,1)}, u32[]{:S(2)}, u32[]{:S(2)}) collective-permute-start(bf16[4,256,1664]{2,1,0:T(8,128)(2,1)} %shard_map.246), channel_id=1, source_target_pairs={{0,1},{1,0},{2,3},{3,2},{4,5},{5,4},{6,7},{7,6},{8,9},{9,8},{10,11... | collective-permute-start | bytes 10223624 | tf_op jit(solution)/shard_map/ppermute | solution.py:66
  691.8 19.7 %collective-permute-start.26 = (bf16[4,256,1664]{2,1,0:T(8,128)(2,1)}, bf16[4,256,1664]{2,1,0:T(8,128)(2,1)}, u32[]{:S(2)}, u32[]{:S(2)}) collective-permute-start(bf16[4,256,1664]{2,1,0:T(8,128)(2,1)} %shard_map.248), channel_id=1, source_target_pairs={{0,1},{1,0},{2,3},{3,2},{4,5},{5,4},{6,7},{7,6},{8,9},{9,8},{10,11... | collective-permute-start | bytes 10223624 | tf_op jit(solution)/shard_map/ppermute | solution.py:66
  722.3 23.2 %collective-permute-start.28 = (bf16[4,256,1536]{2,1,0:T(8,128)(2,1)}, bf16[4,256,1536]{2,1,0:T(8,128)(2,1)}, u32[]{:S(2)}, u32[]{:S(2)}) collective-permute-start(bf16[4,256,1536]{2,1,0:T(8,128)(2,1)} %shard_map.250), channel_id=1, source_target_pairs={{0,1},{1,0},{2,3},{3,2},{4,5},{5,4},{6,7},{7,6},{8,9},{9,8},{10,11... | collective-permute-start | bytes 9437192 | tf_op jit(solution)/shard_map/ppermute | solution.py:66
  729.1 21.9 %collective-permute-start.29 = (bf16[4,256,1536]{2,1,0:T(8,128)(2,1)}, bf16[4,256,1536]{2,1,0:T(8,128)(2,1)}, u32[]{:S(2)}, u32[]{:S(2)}) collective-permute-start(bf16[4,256,1536]{2,1,0:T(8,128)(2,1)} %shard_map.252), channel_id=1, source_target_pairs={{0,1},{1,0},{2,3},{3,2},{4,5},{5,4},{6,7},{7,6},{8,9},{9,8},{10,11... | collective-permute-start | bytes 9437192 | tf_op jit(solution)/shard_map/ppermute | solution.py:66
  729.2 71.0 %collective-permute-start.25 = (bf16[2,256,1664]{2,1,0:T(8,128)(2,1)}, bf16[2,256,1664]{2,1,0:T(8,128)(2,1)}, u32[]{:S(2)}, u32[]{:S(2)}) collective-permute-start(bf16[2,256,1664]{2,1,0:T(8,128)(2,1)} %get-tuple-element.263), channel_id=1, source_target_pairs={{0,8},{1,9},{2,10},{3,11},{4,12},{5,13},{6,14},{7,15},{8,0},{9,1},... | collective-permute-start | bytes 5111816 | tf_op jit(solution)/shard_map/ppermute | solution.py:66
  729.5 70.7 %collective-permute-start.27 = (bf16[2,256,1664]{2,1,0:T(8,128)(2,1)}, bf16[2,256,1664]{2,1,0:T(8,128)(2,1)}, u32[]{:S(2)}, u32[]{:S(2)}) collective-permute-start(bf16[2,256,1664]{2,1,0:T(8,128)(2,1)} %get-tuple-element.261), channel_id=1, source_target_pairs={{0,2},{1,3},{2,0},{3,1},{4,6},{5,7},{6,4},{7,5},{8,10},{9,11},{10,... | collective-permute-start | bytes 5111816 | tf_op jit(solution)/shard_map/ppermute | solution.py:66
  802.3 20.8 %collective-permute-start.30 = (bf16[1,256,1664]{2,1,0:T(8,128)(2,1)S(1)}, bf16[1,256,1664]{2,1,0:T(8,128)(2,1)S(1)}, u32[]{:S(2)}, u32[]{:S(2)}) collective-permute-start(bf16[1,256,1664]{2,1,0:T(8,128)(2,1)S(1)} %slice.428), channel_id=1, source_target_pairs={{0,2},{1,3},{2,0},{3,1},{4,6},{5,7},{6,4},{7,5},{8,10},{9,11},{10,... | collective-permute-start | bytes 2555912 | tf_op jit(solution)/shard_map/ppermute | solution.py:66
  804.3 49.9 %collective-permute-start.31 = (bf16[1,256,1664]{2,1,0:T(8,128)(2,1)S(1)}, bf16[1,256,1664]{2,1,0:T(8,128)(2,1)S(1)}, u32[]{:S(2)}, u32[]{:S(2)}) collective-permute-start(bf16[1,256,1664]{2,1,0:T(8,128)(2,1)S(1)} %slice.430), channel_id=1, source_target_pairs={{0,8},{1,9},{2,10},{3,11},{4,12},{5,13},{6,14},{7,15},{8,0},{9,1},... | collective-permute-start | bytes 2555912 | tf_op jit(solution)/shard_map/ppermute | solution.py:66
  899.8 45.5 %collective-permute-start.36 = (bf16[2,2,2,2,48,1664]{5,4,3,2,1,0:T(8,128)(2,1)}, bf16[2,2,2,2,48,1664]{5,4,3,2,1,0:T(8,128)(2,1)S(1)}, u32[]{:S(2)}, u32[]{:S(2)}) collective-permute-start(bf16[2,2,2,2,48,1664]{5,4,3,2,1,0:T(8,128)(2,1)} %dynamic-slice_bitcast_fusion.1), channel_id=1, source_target_pairs={{0,1},{1,0},{2,3},{3,2},{4,5},{5,4},{6,7},{7,6},{8,9},{9,8},{10,11... | collective-permute-start | bytes 7667720 | tf_op jit(solution)/shard_map/ppermute | solution.py:66
  907.8 24.1 %collective-permute-start.33 = (bf16[1,256,1024]{2,1,0:T(8,128)(2,1)S(1)}, bf16[1,256,1024]{2,1,0:T(8,128)(2,1)}, u32[]{:S(2)}, u32[]{:S(2)}) collective-permute-start(bf16[1,256,1024]{2,1,0:T(8,128)(2,1)S(1)} %fusion.14), channel_id=1, source_target_pairs={{0,2},{1,3},{2,0},{3,1},{4,6},{5,7},{6,4},{7,5},{8,10},{9,11},{10,... | collective-permute-start | bytes 1572872 | tf_op jit(solution)/shard_map/ppermute | solution.py:66
  978.7 47.2 %collective-permute-start.38 = (bf16[2,2,2,48,2688]{4,3,2,1,0:T(8,128)(2,1)}, bf16[2,2,2,48,2688]{4,3,2,1,0:T(8,128)(2,1)}, u32[]{:S(2)}, u32[]{:S(2)}) collective-permute-start(bf16[2,2,2,48,2688]{4,3,2,1,0:T(8,128)(2,1)} %dynamic-slice_bitcast_fusion.2), channel_id=1, source_target_pairs={{0,2},{1,3},{2,0},{3,1},{4,6},{5,7},{6,4},{7,5},{8,10},{9,11},{10,... | collective-permute-start | bytes 6193160 | tf_op jit(solution)/shard_map/ppermute | solution.py:66
  982.1 83.5 %collective-permute-start.41 = (bf16[3,576,512]{2,1,0:T(8,128)(2,1)}, bf16[3,576,512]{2,1,0:T(8,128)(2,1)}, u32[]{:S(2)}, u32[]{:S(2)}) collective-permute-start(bf16[3,576,512]{2,1,0:T(8,128)(2,1)} %get-tuple-element.271), channel_id=1, source_target_pairs={{0,8},{1,9},{2,10},{3,11},{4,12},{5,13},{6,14},{7,15},{8,0},{9,1},... | collective-permute-start | bytes 5308424 | tf_op jit(solution)/shard_map/ppermute | solution.py:66
  1030.1 54.5 %collective-permute-start.42 = (bf16[2,256,1536]{2,1,0:T(8,128)(2,1)}, bf16[2,256,1536]{2,1,0:T(8,128)(2,1)}, u32[]{:S(2)}, u32[]{:S(2)}) collective-permute-start(bf16[2,256,1536]{2,1,0:T(8,128)(2,1)} %get-tuple-element.176), channel_id=1, source_target_pairs={{0,8},{1,9},{2,10},{3,11},{4,12},{5,13},{6,14},{7,15},{8,0},{9,1},... | collective-permute-start | bytes 4718600 | tf_op jit(solution)/shard_map/ppermute | solution.py:66
  1030.1 54.5 %collective-permute-start.43 = (bf16[2,256,1536]{2,1,0:T(8,128)(2,1)}, bf16[2,256,1536]{2,1,0:T(8,128)(2,1)}, u32[]{:S(2)}, u32[]{:S(2)}) collective-permute-start(bf16[2,256,1536]{2,1,0:T(8,128)(2,1)} %get-tuple-element.177), channel_id=1, source_target_pairs={{0,2},{1,3},{2,0},{3,1},{4,6},{5,7},{6,4},{7,5},{8,10},{9,11},{10,... | collective-permute-start | bytes 4718600 | tf_op jit(solution)/shard_map/ppermute | solution.py:66
  1032.9 31.3 %collective-permute-start.40 = (bf16[2,2,2,48,1664]{4,3,2,1,0:T(8,128)(2,1)}, bf16[2,2,2,48,1664]{4,3,2,1,0:T(8,128)(2,1)}, u32[]{:S(2)}, u32[]{:S(2)}) collective-permute-start(bf16[2,2,2,48,1664]{4,3,2,1,0:T(8,128)(2,1)} %dynamic-slice_bitcast_fusion.3), channel_id=1, source_target_pairs={{0,4},{1,5},{2,6},{3,7},{4,0},{5,1},{6,2},{7,3},{8,12},{9,13},{10,... | collective-permute-start | bytes 3833864 | tf_op jit(solution)/shard_map/ppermute | solution.py:66
  1032.9 51.7 %collective-permute-start.39 = (bf16[2,2,48,2688]{3,2,1,0:T(8,128)(2,1)}, bf16[2,2,48,2688]{3,2,1,0:T(8,128)(2,1)}, u32[]{:S(2)}, u32[]{:S(2)}) collective-permute-start(bf16[2,2,48,2688]{3,2,1,0:T(8,128)(2,1)} %get-tuple-element.275), channel_id=1, source_target_pairs={{0,4},{1,5},{2,6},{3,7},{4,0},{5,1},{6,2},{7,3},{8,12},{9,13},{10,... | collective-permute-start | bytes 3096584 | tf_op jit(solution)/shard_map/ppermute | solution.py:66
  1064.3 54.4 %collective-permute-start.48 = (bf16[2,576,512]{2,1,0:T(8,128)(2,1)S(1)}, bf16[2,576,512]{2,1,0:T(8,128)(2,1)S(1)}, u32[]{:S(2)}, u32[]{:S(2)}) collective-permute-start(bf16[2,576,512]{2,1,0:T(8,128)(2,1)S(1)} %get-tuple-element.273), channel_id=1, source_target_pairs={{0,8},{1,9},{2,10},{3,11},{4,12},{5,13},{6,14},{7,15},{8,0},{9,1},... | collective-permute-start | bytes 3538952 | tf_op jit(solution)/shard_map/ppermute | solution.py:66
  1086.5 58.9 %collective-permute-start.45 = (bf16[1,256,1536]{2,1,0:T(8,128)(2,1)S(1)}, bf16[1,256,1536]{2,1,0:T(8,128)(2,1)S(1)}, u32[]{:S(2)}, u32[]{:S(2)}) collective-permute-start(bf16[1,256,1536]{2,1,0:T(8,128)(2,1)S(1)} %slice.438), channel_id=1, source_target_pairs={{0,8},{1,9},{2,10},{3,11},{4,12},{5,13},{6,14},{7,15},{8,0},{9,1},... | collective-permute-start | bytes 2359304 | tf_op jit(solution)/shard_map/ppermute | solution.py:66
  1091.0 41.3 %collective-permute-start.47 = (bf16[2,2,48,1664]{3,2,1,0:T(8,128)(2,1)S(1)}, bf16[2,2,48,1664]{3,2,1,0:T(8,128)(2,1)S(1)}, u32[]{:S(2)}, u32[]{:S(2)}) collective-permute-start(bf16[2,2,48,1664]{3,2,1,0:T(8,128)(2,1)S(1)} %dynamic-slice_bitcast_fusion.6), channel_id=1, source_target_pairs={{0,2},{1,3},{2,0},{3,1},{4,6},{5,7},{6,4},{7,5},{8,10},{9,11},{10,... | collective-permute-start | bytes 1916936 | tf_op jit(solution)/shard_map/ppermute | solution.py:66
  1092.5 39.8 %collective-permute-start.46 = (bf16[2,48,2688]{2,1,0:T(8,128)(2,1)S(1)}, bf16[2,48,2688]{2,1,0:T(8,128)(2,1)S(1)}, u32[]{:S(2)}, u32[]{:S(2)}) collective-permute-start(bf16[2,48,2688]{2,1,0:T(8,128)(2,1)S(1)} %dynamic-slice_bitcast_fusion.7), channel_id=1, source_target_pairs={{0,16},{1,17},{2,18},{3,19},{4,20},{5,21},{6,22},{7,23},{8,24},{9,... | collective-permute-start | bytes 1548296 | tf_op jit(solution)/shard_map/ppermute | solution.py:66
  1094.5 51.3 %collective-permute-start.44 = (bf16[1,256,1536]{2,1,0:T(8,128)(2,1)S(1)}, bf16[1,256,1536]{2,1,0:T(8,128)(2,1)S(1)}, u32[]{:S(2)}, u32[]{:S(2)}) collective-permute-start(bf16[1,256,1536]{2,1,0:T(8,128)(2,1)S(1)} %slice.436), channel_id=1, source_target_pairs={{0,2},{1,3},{2,0},{3,1},{4,6},{5,7},{6,4},{7,5},{8,10},{9,11},{10,... | collective-permute-start | bytes 2359304 | tf_op jit(solution)/shard_map/ppermute | solution.py:66
  1132.5 16.0 %collective-permute-start.49 = (bf16[48,2688]{1,0:T(8,128)(2,1)S(1)}, bf16[48,2688]{1,0:T(8,128)(2,1)S(1)}, u32[]{:S(2)}, u32[]{:S(2)}) collective-permute-start(bf16[48,2688]{1,0:T(8,128)(2,1)S(1)} %dynamic-slice_bitcast_fusion.9), channel_id=1, source_target_pairs={{0,8},{1,9},{2,10},{3,11},{4,12},{5,13},{6,14},{7,15},{8,0},{9,1},... | collective-permute-start | bytes 774152 | tf_op jit(solution)/shard_map/ppermute | solution.py:66
  1133.6 17.1 %collective-permute-start.50 = (bf16[2,48,1664]{2,1,0:T(8,128)(2,1)S(1)}, bf16[2,48,1664]{2,1,0:T(8,128)(2,1)S(1)}, u32[]{:S(2)}, u32[]{:S(2)}) collective-permute-start(bf16[2,48,1664]{2,1,0:T(8,128)(2,1)S(1)} %dynamic-slice_bitcast_fusion.8), channel_id=1, source_target_pairs={{0,16},{1,17},{2,18},{3,19},{4,20},{5,21},{6,22},{7,23},{8,24},{9,... | collective-permute-start | bytes 958472 | tf_op jit(solution)/shard_map/ppermute | solution.py:66
  (90 other events, 2377.6 us)
Sparse Core Ops, SparseCore 0:
  11.7 139.8 all-gather.1
  617.6 246.1 reduce-scatter.2
  866.9 169.4 reduce-scatter.4
